TPU v7x, 512 devices: a whole 4x8x8 slice. The times are simulated.
512 devices in a mesh: enc: 32 (over y, x), section: 8 (over z_lo, core), llmdp: 2 (over z_hi).
Axes of the slice: x: 4, y: 8, z: 8 (z_hi: 2, z_lo: 4; z = z_hi * 4 + z_lo), core: 2. Of those that a mesh axis runs over, the one named last changes fastest.
Arguments:
- patches: bfloat16 [8192, 3200], P('enc', ('section', 'llmdp')), may hold values from -6 to 6
- gain: float32 [3200], replicated, may hold values from 0.25 to 1.75
- shift: float32 [3200], replicated, may hold values from -3 to 3
- proj_weight: bfloat16 [3200, 8192], P('enc', ('section', 'llmdp')), may hold values from -0.109375 to 0.109375
- llm_rank: int32 [8192, 1], P('enc'), may hold values from 0 to 31; in each aligned block of 256 rows (0 to 255, 256 to 511, ...) at most 24 rows name the same one
- embed_grad: bfloat16 [24576, 8192], P('enc', ('section', 'llmdp')), may hold values from -0.59765625 to 0.59765625
Outputs:
- embeds_recv: bfloat16 [24576, 8192], P('enc', ('section', 'llmdp'))
- hidden_state_gradient: bfloat16 [8192, 3200], P('enc', ('section', 'llmdp'))
- grad_weight: float32 [3200, 8192], P('enc', ('section', 'llmdp'))
- gain_gradient: float32 [3200], P(('section', 'llmdp'))
- grad_shift: float32 [3200], P(('section', 'llmdp'))
Inputs may be any that keep to these rules, and one draw needn't show every extreme that they name: `llm_rank`: among the 256 rows of one device, at most 24 name the same owner, a bound that some block reaches.
All inputs are finite; a program needn't handle non-finite values.
Results may differ from a plain program's by a relative error of at most 0.018.
Values may be sent and summed in bfloat16 or wider, within the bound.
No kernel may reach another device: no remote copies, remote signals or barrier semaphores. Data moves between devices by JAX's collectives and lax.ppermute only.
A program may use at most 64 MiB of HBM per device.

v0:
```python
import jax
import jax.numpy as jnp
from jax import lax
from jax.sharding import Mesh
from jax.sharding import PartitionSpec as P

ENC = ("enc_0", "enc_1")


EPSILON = 1e-05


def whole_of(x, axes, dim):
    for axis in reversed(axes):
        x = lax.all_gather(x, axis, axis=dim, tiled=True)
    return x


def summed_rows(terms, axes):
    running = terms.astype(jnp.bfloat16)
    for axis in axes:
        running = lax.psum_scatter(running, axis, scatter_dimension=0, tiled=True)
    return running.astype(jnp.float32)


def copy_for_each(x, axis):
    peers = lax.axis_size(axis)
    return lax.all_to_all(jnp.broadcast_to(x[None], (peers, *x.shape)), axis, 0, 0, tiled=True)


def taken_together(x, axis):
    everything = copy_for_each(x, axis)
    return jnp.sum(everything, axis=0)


def packed_total(arrays, axis):
    ends = [0]
    for a in arrays:
        ends.append(ends[-1] + a.size)
    running = taken_together(jnp.concatenate([a.ravel() for a in arrays]), axis)
    return tuple((running[b:e].reshape(a.shape) for a, b, e in zip(arrays, ends, ends[1:])))


def body(patches, gain, shift, proj_weight, llm_rank, embed_grad):
    row_count = patches.shape[0]
    owned_width = patches.shape[1]
    width = gain.shape[0]
    out_cols = proj_weight.shape[1]
    column_start = lax.axis_index(("section", "llmdp")) * owned_width
    gain_own = lax.dynamic_slice_in_dim(gain, column_start, owned_width, 0)
    complete_rows = lax.all_gather(patches, ("section", "llmdp"), axis=1, tiled=True).astype(
        jnp.float32
    )
    row_average = jnp.mean(complete_rows, 1, keepdims=True)
    variance = jnp.mean(complete_rows * complete_rows, 1, keepdims=True) - row_average * row_average
    inverse_deviation = lax.rsqrt(variance + EPSILON)
    standardized_full = (complete_rows - row_average) * inverse_deviation
    normed_hidden = (standardized_full * gain + shift).astype(jnp.bfloat16)
    standardized_owned = lax.dynamic_slice_in_dim(standardized_full, column_start, owned_width, 1)
    weight_full = whole_of(proj_weight, ENC, 0)
    embed_acc = jnp.dot(normed_hidden, weight_full, preferred_element_type=jnp.float32)
    embed = embed_acc.astype(jnp.bfloat16)
    senders = lax.axis_size(ENC)
    most_slots = embed_grad.shape[0] // senders
    target = llm_rank[:, 0]
    owners = jnp.arange(senders, dtype=jnp.int32)
    hits = (target[:, None] == owners[None, :]).astype(jnp.int32)
    rank = jnp.sum((jnp.cumsum(hits, 0) - hits) * hits, 1)
    slot = target * most_slots + rank
    outgoing = jnp.zeros((senders * most_slots, out_cols), jnp.bfloat16).at[slot].set(embed)
    arrived = lax.all_to_all(
        outgoing.reshape(senders, most_slots, out_cols),
        ENC,
        split_axis=0,
        concat_axis=0,
        tiled=True,
    )
    embeds_recv = arrived.reshape(senders * most_slots, out_cols)
    returned = lax.all_to_all(
        embed_grad.reshape(senders, most_slots, out_cols),
        ENC,
        split_axis=0,
        concat_axis=0,
        tiled=True,
    )
    d_embed = returned.reshape(senders * most_slots, out_cols)[slot]
    partial_grad = lax.dot_general(
        d_embed, weight_full, (((1,), (1,)), ((), ())), preferred_element_type=jnp.float32
    )
    grad_weight = summed_rows(
        lax.dot_general(
            normed_hidden, d_embed, (((0,), (0,)), ((), ())), preferred_element_type=jnp.float32
        ),
        ENC,
    )
    group_count = width // owned_width
    pieces = partial_grad.astype(jnp.bfloat16).reshape(row_count, group_count, owned_width)
    columns = lax.all_to_all(pieces, ("section", "llmdp"), split_axis=1, concat_axis=1, tiled=True)
    owned_normalized_gradient = jnp.sum(columns.astype(jnp.float32), 1)
    owned_centered_gradient = owned_normalized_gradient * gain_own
    mean_sum, cross_sum = packed_total(
        (
            jnp.sum(owned_centered_gradient, 1),
            jnp.sum(owned_centered_gradient * standardized_owned, 1),
        ),
        ("section", "llmdp"),
    )
    gradient_row_average = (mean_sum / width)[:, None]
    gradient_cross_product = (cross_sum / width)[:, None]
    hidden_state_gradient = (
        inverse_deviation
        * (
            owned_centered_gradient
            - gradient_row_average
            - standardized_owned * gradient_cross_product
        )
    ).astype(jnp.bfloat16)
    gain_gradient, grad_shift = packed_total(
        (
            jnp.sum(owned_normalized_gradient * standardized_owned, 0),
            jnp.sum(owned_normalized_gradient, 0),
        ),
        ENC,
    )
    return (embeds_recv, hidden_state_gradient, grad_weight, gain_gradient, grad_shift)


def solution(mesh):
    split = Mesh(
        mesh.devices.reshape(8, 4, mesh.shape["section"], mesh.shape["llmdp"]),
        ("enc_0", "enc_1", "section", "llmdp"),
    )
    in_specs = (
        P(ENC, ("section", "llmdp")),
        P(),
        P(),
        P(ENC, ("section", "llmdp")),
        P(ENC, None),
        P(ENC, ("section", "llmdp")),
    )
    out_specs = (
        P(ENC, ("section", "llmdp")),
        P(ENC, ("section", "llmdp")),
        P(ENC, ("section", "llmdp")),
        P(("section", "llmdp")),
        P(("section", "llmdp")),
    )
    return jax.shard_map(body, mesh=split, in_specs=in_specs, out_specs=out_specs, check_vma=False)
```

profile of v0, /device:TPU:6, one launch (start us, length us, event | category | flops | bytes accessed | tf_op | source)
XLA Modules:
  0.0 331.4 jit_solution(10360011077139938337)
XLA Ops:
  7.2 0.7 all-gather.4.cloned.1.call-update
  8.0 15.5 %all-gather = bf16[4,100,512]{2,1,0:T(8,128)(2,1)S(1)} all-gather(bf16[1,100,512]{2,1,0:T(8,128)(2,1)} %bitcast.40), channel_id=1, replica_groups=mesh['enc_0'=8,'enc_1'=4,'section'=8,'llmdp'=2] {'enc_1'}, dimensions={0}, use_global_device_ids=true | all-gather | bytes 512000 | tf_op jit(solution)/shard_map/all_gather | solution.py:15
  23.4 0.8 reshape.100
  24.3 7.8 %all-to-all-start.1 = ((bf16[32,24,512]{2,1,0:T(8,128)(2,1)}), bf16[32,24,512]{2,1,0:T(8,128)(2,1)S(1)}, u32[]{:S(2)}, u32[]{:S(2)}) async-start(bf16[32,24,512]{2,1,0:T(8,128)(2,1)} %bitcast.39), calls=%async_computation.1 | async-start | bytes 1572864 | tf_op jit(solution)/shard_map/all_to_all | solution.py:79
  33.1 18.2 %all-to-all-done.1 = bf16[32,24,512]{2,1,0:T(8,128)(2,1)S(1)} async-done(((bf16[32,24,512]{2,1,0:T(8,128)(2,1)}), bf16[32,24,512]{2,1,0:T(8,128)(2,1)S(1)}, u32[]{:S(2)}, u32[]{:S(2)}) %all-to-all-start.1) | async-done | bytes 786464 | tf_op jit(solution)/shard_map/all_to_all | solution.py:79
  51.4 1.2 gather_fusion
  52.5 79.2 %all-gather.4.cloned.1.call-done = bf16[256,3200]{0,1:T(8,128)(2,1)} async-done(((bf16[256,200]{0,1:T(8,128)(2,1)}), bf16[256,3200]{0,1:T(8,128)(2,1)}) %all-gather.4.cloned.1.call-update) | async-done | bytes 1638416 | tf_op jit(solution)/shard_map/all_gather | solution.py:51
  131.7 1.9 convert_reduce_fusion
  133.7 4.2 %convolution_convert_fusion = bf16[3200,512]{1,0:T(8,128)(2,1)} fusion(bf16[256,512]{1,0:T(8,128)(2,1)S(1)} %gather_fusion, f32[3200]{0:T(1024)S(1)} %copy-done.3, f32[3200]{0:T(1024)S(1)} %copy-done.2, f32[256]{0:T(256)S(1)} %get-tuple-element.17, f32[256]{0:T(256)S(1)} %get-tuple-element.16, bf16[256,3200]{0,1:T(8,128)(2,1)} %all-gather.4.cloned.1.call-done), kind=kOutput, calls=%fused_computation.2 | convolution fusion | flops 845414400 | bytes 5204992 | tf_op jit(solution)/shard_map/dot_general | solution.py:91
  137.9 44.4 %all-gather.6.cloned.1.call-done = bf16[3200,512]{1,0:T(8,128)(2,1)} async-done(((bf16[400,512]{1,0:T(8,128)(2,1)}), bf16[3200,512]{1,0:T(8,128)(2,1)}) %all-gather.6.cloned.1.call-update) | async-done | bytes 3276816 | tf_op jit(solution)/shard_map/all_gather | solution.py:15
  182.3 4.1 %convolution_convert_fusion.2 = bf16[256,512]{1,0:T(8,128)(2,1)S(1)} fusion(bf16[3200,512]{1,0:T(8,128)(2,1)} %all-gather.6.cloned.1.call-done, f32[3200]{0:T(1024)S(1)} %copy-done.3, f32[3200]{0:T(1024)S(1)} %copy-done.2, f32[256]{0:T(256)S(1)} %get-tuple-element.17, f32[256]{0:T(256)S(1)} %get-tuple-element.16, bf16[256,3200]{0,1:T(8,128)(2,1)S(1)} %copy-done), kind=kOutput, calls=%fused_computation.12 | convolution fusion | flops 843907072 | bytes 5204992 | tf_op jit(solution)/shard_map/dot_general | solution.py:61
  186.4 2.5 scatter_custom_fusion
  188.8 7.6 %all-to-all-start = ((bf16[32,24,512]{2,1,0:T(8,128)(2,1)}), bf16[32,24,512]{2,1,0:T(8,128)(2,1)}, u32[]{:S(2)}, u32[]{:S(2)}) async-start(bf16[32,24,512]{2,1,0:T(8,128)(2,1)} %bitcast.6), calls=%async_computation | async-start | bytes 1572864 | tf_op jit(solution)/shard_map/all_to_all | solution.py:71
  196.5 3.0 convolution_convert_fusion.1
  199.5 2.2 copy.18
  201.7 25.4 %all-to-all-done = bf16[32,24,512]{2,1,0:T(8,128)(2,1)} async-done(((bf16[32,24,512]{2,1,0:T(8,128)(2,1)}), bf16[32,24,512]{2,1,0:T(8,128)(2,1)}, u32[]{:S(2)}, u32[]{:S(2)}) %all-to-all-start) | async-done | bytes 786464 | tf_op jit(solution)/shard_map/all_to_all | solution.py:71
  227.1 7.5 %all-to-all-start.2 = ((bf16[256,16,200]{0,2,1:T(8,128)(2,1)}), bf16[256,16,200]{0,2,1:T(8,128)(2,1)S(1)}, u32[]{:S(2)}, u32[]{:S(2)}) async-start(bf16[256,16,200]{0,2,1:T(8,128)(2,1)} %bitcast.38), calls=%async_computation.2 | async-start | bytes 3276800 | tf_op jit(solution)/shard_map/all_to_all | solution.py:98
  234.6 0.8 dynamic_slice.6
  235.4 1.3 dynamic-slice.4
  237.3 2.0 fusion.1
  239.4 36.7 %all-to-all-done.2 = bf16[256,16,200]{0,2,1:T(8,128)(2,1)S(1)} async-done(((bf16[256,16,200]{0,2,1:T(8,128)(2,1)}), bf16[256,16,200]{0,2,1:T(8,128)(2,1)S(1)}, u32[]{:S(2)}, u32[]{:S(2)}) %all-to-all-start.2) | async-done | bytes 1638432 | tf_op jit(solution)/shard_map/all_to_all | solution.py:98
  276.4 1.1 multiply_reduce_fusion
  278.2 3.5 %all-to-all-start.3 = ((f32[16,1,512]{2,1,0:T(1,128)}), f32[16,1,512]{2,1,0:T(1,128)S(1)}, u32[]{:S(2)}, u32[]{:S(2)}) async-start(f32[16,1,512]{2,1,0:T(1,128)} %broadcast_in_dim.7), calls=%async_computation.3 | async-start | bytes 65536 | tf_op jit(solution)/shard_map/all_to_all | solution.py:28
  281.8 7.6 %all-to-all-done.3 = f32[16,1,512]{2,1,0:T(1,128)S(1)} async-done(((f32[16,1,512]{2,1,0:T(1,128)}), f32[16,1,512]{2,1,0:T(1,128)S(1)}, u32[]{:S(2)}, u32[]{:S(2)}) %all-to-all-start.3) | async-done | bytes 32800 | tf_op jit(solution)/shard_map/all_to_all | solution.py:28
  290.0 5.2 %all-to-all-start.4 = ((f32[32,1,400]{2,1,0:T(1,128)}), f32[32,1,400]{2,1,0:T(1,128)S(1)}, u32[]{:S(2)}, u32[]{:S(2)}) async-start(f32[32,1,400]{2,1,0:T(1,128)} %broadcast_in_dim.8), calls=%async_computation.5 | async-start | bytes 131072 | tf_op jit(solution)/shard_map/all_to_all | solution.py:28
  295.3 1.7 multiply_convert_fusion
  297.0 6.7 %all-to-all-done.4 = f32[32,1,400]{2,1,0:T(1,128)S(1)} async-done(((f32[32,1,400]{2,1,0:T(1,128)}), f32[32,1,400]{2,1,0:T(1,128)S(1)}, u32[]{:S(2)}, u32[]{:S(2)}) %all-to-all-start.4) | async-done | bytes 51232 | tf_op jit(solution)/shard_map/all_to_all | solution.py:28
  303.7 12.5 %fusion = bf16[104,512]{1,0:T(8,128)(2,1)S(1)} fusion(bf16[400,512]{1,0:T(8,128)(2,1)} %reduce-scatter.4.cloned.1.call-done), kind=kCustom, calls=%all-reduce-scatter | all-reduce-scatter fusion | flops 212993 | bytes 518144
  316.3 1.3 collective-permute-start
  318.2 3.7 %collective-permute-done = bf16[12,512]{1,0:T(8,128)(2,1)S(1)} collective-permute-done((bf16[12,512]{1,0:T(8,128)(2,1)S(1)}, bf16[12,512]{1,0:T(8,128)(2,1)S(1)}, u32[]{:S(2)}, u32[]{:S(2)}) %collective-permute-start) | collective-permute-done | bytes 12320
  322.1 0.7 dynamic-slice_convert_fusion
  322.8 2.1 copy.30
  (34 shorter events, 3.8 us)
Async XLA Ops:
  7.2 25.0 %copy-start.1 = (s32[256,1]{0,1:T(1,128)S(1)}, s32[256,1]{0,1:T(1,128)}, u32[]{:S(2)}) copy-start(s32[256,1]{0,1:T(1,128)} %param.10) | copy-start | bytes 3076
  7.2 124.6 %all-gather.4.cloned.1.call-start = ((), (), s32[]{:S(2)}) async-start(), calls=%async_computation.6 | async-start | bytes 1740800 | tf_op jit(solution)/shard_map/all_gather | solution.py:51
  7.9 174.4 %all-gather.6.cloned.1.call-start = ((), (), s32[]{:S(2)}) async-start(), calls=%async_computation.7 | async-start | bytes 3686400 | tf_op jit(solution)/shard_map/all_gather | solution.py:15
  24.3 109.4 %copy-start.2 = (f32[3200]{0:T(1024)S(1)}, f32[3200]{0:T(1024)}, u32[]{:S(2)}) copy-start(f32[3200]{0:T(1024)} %param.7) | copy-start | bytes 38404
  24.3 109.4 %copy-start.3 = (f32[3200]{0:T(1024)S(1)}, f32[3200]{0:T(1024)}, u32[]{:S(2)}) copy-start(f32[3200]{0:T(1024)} %param.8) | copy-start | bytes 38404
  24.3 27.1 %all-to-all-start.1 = ((bf16[32,24,512]{2,1,0:T(8,128)(2,1)}), bf16[32,24,512]{2,1,0:T(8,128)(2,1)S(1)}, u32[]{:S(2)}, u32[]{:S(2)}) async-start(bf16[32,24,512]{2,1,0:T(8,128)(2,1)} %bitcast.39), calls=%async_computation.1 | async-start | bytes 1572864 | tf_op jit(solution)/shard_map/all_to_all | solution.py:79
  32.1 271.6 %reduce-scatter.4.cloned.1.call-start = ((), (), s32[]{:S(2)}) async-start(), calls=%async_computation.8 | async-start | bytes 3686400 | tf_op jit(solution)/shard_map/reduce_scatter | solution.py:22
  137.9 44.4 %copy-start = (bf16[256,3200]{0,1:T(8,128)(2,1)S(1)}, bf16[256,3200]{0,1:T(8,128)(2,1)}, u32[]{:S(2)}) copy-start(bf16[256,3200]{0,1:T(8,128)(2,1)} %all-gather.4.cloned.1.call-done) | copy-start | bytes 4915204
  188.8 38.3 %all-to-all-start = ((bf16[32,24,512]{2,1,0:T(8,128)(2,1)}), bf16[32,24,512]{2,1,0:T(8,128)(2,1)}, u32[]{:S(2)}, u32[]{:S(2)}) async-start(bf16[32,24,512]{2,1,0:T(8,128)(2,1)} %bitcast.6), calls=%async_computation | async-start | bytes 1572864 | tf_op jit(solution)/shard_map/all_to_all | solution.py:71
  227.1 49.0 %all-to-all-start.2 = ((bf16[256,16,200]{0,2,1:T(8,128)(2,1)}), bf16[256,16,200]{0,2,1:T(8,128)(2,1)S(1)}, u32[]{:S(2)}, u32[]{:S(2)}) async-start(bf16[256,16,200]{0,2,1:T(8,128)(2,1)} %bitcast.38), calls=%async_computation.2 | async-start | bytes 3276800 | tf_op jit(solution)/shard_map/all_to_all | solution.py:98
  278.2 11.2 %all-to-all-start.3 = ((f32[16,1,512]{2,1,0:T(1,128)}), f32[16,1,512]{2,1,0:T(1,128)S(1)}, u32[]{:S(2)}, u32[]{:S(2)}) async-start(f32[16,1,512]{2,1,0:T(1,128)} %broadcast_in_dim.7), calls=%async_computation.3 | async-start | bytes 65536 | tf_op jit(solution)/shard_map/all_to_all | solution.py:28
  290.0 13.6 %all-to-all-start.4 = ((f32[32,1,400]{2,1,0:T(1,128)}), f32[32,1,400]{2,1,0:T(1,128)S(1)}, u32[]{:S(2)}, u32[]{:S(2)}) async-start(f32[32,1,400]{2,1,0:T(1,128)} %broadcast_in_dim.8), calls=%async_computation.5 | async-start | bytes 131072 | tf_op jit(solution)/shard_map/all_to_all | solution.py:28
  316.3 5.6 %collective-permute-start = (bf16[12,512]{1,0:T(8,128)(2,1)S(1)}, bf16[12,512]{1,0:T(8,128)(2,1)S(1)}, u32[]{:S(2)}, u32[]{:S(2)}) collective-permute-start(bf16[12,512]{1,0:T(8,128)(2,1)S(1)} %slice.27), channel_id=1, source_target_pairs={{0,16},{16,32},{32,48},{1,17},{17,33},{33,49},{2,18},{18,34},{34,5... | collective-permute-start | bytes 36872
Sparse Core Ops, SparseCore 0:
  10.1 121.6 all-gather.3
  134.4 47.8 all-gather.5
  185.1 62.8 reduce-scatter.3
where the time goes:
time: 334 us; the launch traced here: 331 us
  waiting for transfers between devices  223 us (67%)
  starting transfers between devices  33 us (10%)
  blocking collectives  28 us (8%)
  between operations  14.6 us (4%)
  local copies, waits for them, and re-layouts  13.1 us (4%)
  matrix products  11.3 us (3%)
  other arithmetic  8.74 us (3%)
    all_gather x1, waiting for transfers between devices, body(): lax.all_gather(patches, ('section', 'llmdp'), axis=1, tiled=True)  79.2 us
    all_gather x1, waiting for transfers between devices, whole_of(): x = lax.all_gather(x, axis, axis=dim, tiled=True)  44.4 us
    all_to_all x1, waiting for transfers between devices, body(): lax.all_to_all(pieces, ('section', 'llmdp'), split_axis=1, concat_axis=1,...  36.7 us
    all_to_all x1, waiting for transfers between devices, body(): lax.all_to_all(outgoing.reshape(senders, most_slots, out_cols), ENC, spli...  25.4 us
    all_to_all x1, waiting for transfers between devices, body(): lax.all_to_all(embed_grad.reshape(senders, most_slots, out_cols), ENC, sp...  18.2 us
    all_gather x1, blocking collectives, whole_of(): x = lax.all_gather(x, axis, axis=dim, tiled=True)  15.5 us
    all_to_all x2, waiting for transfers between devices, copy_for_each(): lax.all_to_all(jnp.broadcast_to(x[None], (peers, *x.shape)), axis, 0, 0,...  14.3 us
    unnamed x1, blocking collectives  12.5 us
  transfers between devices with their start and end apart: 9, of which 8 were waited for; matrix products, arithmetic and copies ran while one was open for 9% of the time, Pallas kernels for 0%

commit v1 on v0

v1 whole, which is shorter than its diff:
```python
import functools

import jax
import jax.numpy as jnp
from jax import lax
from jax.experimental import pallas as pl
from jax.experimental.pallas import tpu as pltpu
from jax.sharding import Mesh
from jax.sharding import PartitionSpec as P

ENC = ("y", "x")
COLS = ("zl", "co", "zh")
EPSILON = 1e-05
F32 = jnp.float32
BF16 = jnp.bfloat16
VMEM = pl.BlockSpec(memory_space=pltpu.VMEM)
SMEM = pl.BlockSpec(memory_space=pltpu.SMEM)
PARAMS = pltpu.CompilerParams(vmem_limit_bytes=48 * 1024 * 1024)
EXTRA = 8


def exchange(x, axes):
    return lax.all_to_all(x, axes, 0, 0, tiled=True)


def copies(x, axes):
    count = lax.axis_size(axes)
    return exchange(jnp.broadcast_to(x[None], (count, *x.shape)), axes)


def shifted(x, axes, step):
    count = lax.axis_size(axes)
    return lax.ppermute(x, axes, [(i, (i + step) % count) for i in range(count)])


def along_z(x, step):
    n_zl, n_zh = lax.axis_size("zl"), lax.axis_size("zh")
    count = n_zl * n_zh
    at = [(z % n_zl) * n_zh + z // n_zl for z in range(count)]
    return lax.ppermute(x, ("zl", "zh"), [(at[z], at[(z + step) % count]) for z in range(count)])


def core_swap(x):
    return lax.ppermute(x, "co", [(0, 1), (1, 0)])


def block_of(z, core, n_zl, n_zh):
    return (z % n_zl) * (2 * n_zh) + core * n_zh + z // n_zl


def norm_kernel(n_zl, n_zh, slots, place, mine, other, gain, shift, normed, normed_x, stats):
    n_z = n_zl * n_zh
    z, core = place[0], place[1]
    own_width, rows = mine.shape[1:]
    width = 2 * n_z * own_width
    half = own_width // slots
    n_x = normed_x.shape[0]

    def totals(k, carry):
        total, squares = carry
        for ref in (mine, other):
            x = ref[k].astype(F32)
            total = total + jnp.sum(x, 0, keepdims=True)
            squares = squares + jnp.sum(x * x, 0, keepdims=True)
        return total, squares

    zero = jnp.zeros((1, rows), F32)
    total, squares = lax.fori_loop(0, n_z, totals, (zero, zero))
    mean = total / width
    inv = lax.rsqrt(squares / width - mean * mean + EPSILON)
    stats[0:1, :] = mean
    stats[1:2, :] = inv
    normed_x[...] = jnp.zeros_like(normed_x)

    def apply(k, carry):
        source = lax.rem(z - k + n_z, n_z)
        for ref, owner in ((mine, core), (other, 1 - core)):
            b = block_of(source, owner, n_zl, n_zh)
            scale = jnp.concatenate([gain[b]] * (rows // 128), 1)
            offset = jnp.concatenate([shift[b]] * (rows // 128), 1)
            value = (ref[k].astype(F32) - mean) * inv * scale + offset
            normed[b] = value.astype(BF16)
            for part in range(slots):
                slot = b * slots + part
                piece = value[part * half : (part + 1) * half]
                normed_x[slot % n_x, slot // n_x, 0:half, :] = piece.astype(BF16)
        return carry

    lax.fori_loop(0, n_z, apply, 0)


def part_kernel(n_zl, n_zh, place, weight, d_embed, mine, other, gain, stats, keep, send):
    n_z = n_zl * n_zh
    z, core = place[0], place[1]
    own_width, rows = mine.shape[1:]
    mean, inv = stats[0:1, :], stats[1:2, :]

    def step(k, carry):
        plain, cross = carry
        target = lax.rem(z + k, n_z)
        back = lax.rem(n_z - k, n_z)
        for source, owner, out in ((mine, core, keep), (other, 1 - core, send)):
            b = block_of(target, owner, n_zl, n_zh)
            part = lax.dot_general(
                weight[b], d_embed[...], (((1,), (1,)), ((), ())), preferred_element_type=F32
            ).astype(BF16)
            out[k, 0:own_width, :] = part
            scale = jnp.concatenate([gain[b]] * (rows // 128), 1)
            scaled = part.astype(F32) * scale
            xhat = (source[back].astype(F32) - mean) * inv
            plain = plain + jnp.sum(scaled, 0, keepdims=True)
            cross = cross + jnp.sum(scaled * xhat, 0, keepdims=True)
        return plain, cross

    zero = jnp.zeros((1, rows), F32)
    plain, cross = lax.fori_loop(0, n_z, step, (zero, zero))
    high_plain, high_cross = plain.astype(BF16), cross.astype(BF16)
    tail = jnp.concatenate(
        [
            high_plain.astype(F32),
            plain - high_plain.astype(F32),
            high_cross.astype(F32),
            cross - high_cross.astype(F32),
            jnp.zeros((EXTRA - 4, rows), F32),
        ],
        0,
    ).astype(BF16)
    for k in range(n_z):
        keep[k, own_width:, :] = tail
        send[k, own_width:, :] = tail


def pair_kernel(keep, recv, *outs):
    own_width = keep.shape[1] - EXTRA
    rows = keep.shape[2]
    tail = keep[0, own_width:, :].astype(F32) + recv[0, own_width:, :].astype(F32)
    plain, cross = tail[0:1] + tail[1:2], tail[2:3] + tail[3:4]
    high_plain, high_cross = plain.astype(BF16).astype(F32), cross.astype(BF16).astype(F32)
    tail = jnp.concatenate(
        [
            high_plain,
            plain - high_plain,
            high_cross,
            cross - high_cross,
            jnp.zeros((EXTRA - 4, rows), F32),
        ],
        0,
    ).astype(BF16)
    for k, out in enumerate(outs):
        pair = keep[k, 0:own_width, :].astype(F32) + recv[k, 0:own_width, :].astype(F32)
        out[0:own_width, :] = pair.astype(BF16)
        out[own_width:, :] = tail


def body(patches, gain, shift, proj_weight, llm_rank, embed_grad):
    rows, own_width = patches.shape
    width = gain.shape[0]
    out_cols = proj_weight.shape[1]
    n_y, n_x = lax.axis_size("y"), lax.axis_size("x")
    n_zl, n_zh = lax.axis_size("zl"), lax.axis_size("zh")
    n_z = n_zl * n_zh
    senders = n_y * n_x
    slice_rows = proj_weight.shape[0]
    padded_rows = -(-slice_rows // 8) * 8
    slots = own_width // slice_rows
    most = embed_grad.shape[0] // senders
    blocks = width // own_width
    core, x_at = lax.axis_index("co"), lax.axis_index("x")
    place = jnp.stack([lax.axis_index("zh") * n_zl + lax.axis_index("zl"), core]).astype(jnp.int32)

    weight_rel = [proj_weight] + [shifted(proj_weight, "x", k) for k in range(1, n_x)]
    returned = exchange(embed_grad.reshape(senders, most, out_cols), ENC)
    ordered = jnp.stack([weight_rel[-i % n_x] for i in range(n_x)] * 2)
    weight_x = lax.dynamic_slice_in_dim(ordered, lax.rem(n_x - x_at, n_x), n_x, 0)
    weight = lax.all_gather(weight_x.reshape(n_x * slice_rows, out_cols), "y", axis=0, tiled=True)

    own_t = patches.T
    mine = jnp.stack([own_t] + [along_z(own_t, k) for k in range(1, n_z)])
    other = core_swap(mine)
    gain_wide = jnp.broadcast_to(gain.reshape(blocks, own_width, 1), (blocks, own_width, 128))
    shift_wide = jnp.broadcast_to(shift.reshape(blocks, own_width, 1), (blocks, own_width, 128))
    normed, normed_x, stats = pl.pallas_call(
        functools.partial(norm_kernel, n_zl, n_zh, slots),
        out_shape=(
            jax.ShapeDtypeStruct((blocks, own_width, rows), BF16),
            jax.ShapeDtypeStruct((n_x, n_y, padded_rows, rows), BF16),
            jax.ShapeDtypeStruct((8, rows), F32),
        ),
        in_specs=[SMEM] + [VMEM] * 4,
        out_specs=(VMEM,) * 3,
        compiler_params=PARAMS,
        name="norm",
    )(place, mine, other, gain_wide, shift_wide)
    mean, inv = stats[0], stats[1]

    target = llm_rank[:, 0]
    owners = jnp.arange(senders, dtype=jnp.int32)
    hits = (target[:, None] == owners[None, :]).astype(jnp.int32)
    rank = jnp.sum((jnp.cumsum(hits, 0) - hits) * hits, 1)
    slot = target * most + rank
    d_embed = returned.reshape(senders * most, out_cols)[slot]

    stack_x = normed_x.reshape(n_x, n_y * padded_rows, rows)

    def grad_block(step):
        lhs = lax.dynamic_index_in_dim(stack_x, lax.rem(x_at + step, n_x), 0, keepdims=False)
        return jnp.dot(lhs, d_embed, preferred_element_type=F32).astype(BF16)

    grad_x = sum(
        [shifted(grad_block(k), "x", k).astype(F32) for k in range(1, n_x)],
        grad_block(0).astype(F32),
    )
    embed = lax.dot_general(
        normed.reshape(width, rows), weight, (((0,), (0,)), ((), ())), preferred_element_type=F32
    ).astype(BF16)
    outgoing = jnp.zeros((senders * most, out_cols), BF16).at[slot].set(embed)
    embeds_recv = exchange(outgoing.reshape(senders, most, out_cols), ENC).reshape(
        senders * most, out_cols
    )

    grad_x, embeds_recv = lax.optimization_barrier((grad_x.astype(BF16), embeds_recv))
    grad_y = exchange(grad_x.reshape(n_y, padded_rows, out_cols), "y")
    grad_weight = jnp.sum(grad_y.astype(F32), 0)[:slice_rows]

    half_shape = jax.ShapeDtypeStruct((n_z, own_width + EXTRA, rows), BF16)
    keep, send = pl.pallas_call(
        functools.partial(part_kernel, n_zl, n_zh),
        out_shape=(half_shape, half_shape),
        in_specs=[SMEM] + [VMEM] * 6,
        out_specs=(VMEM,) * 2,
        compiler_params=PARAMS,
        name="part",
    )(place, weight.reshape(blocks, own_width, out_cols), d_embed, mine, other, gain_wide, stats)
    pairs = pl.pallas_call(
        pair_kernel,
        out_shape=(jax.ShapeDtypeStruct((own_width + EXTRA, rows), BF16),) * n_z,
        in_specs=[VMEM] * 2,
        out_specs=(VMEM,) * n_z,
        compiler_params=PARAMS,
        name="pair",
    )(keep, core_swap(send))
    columns = sum(
        [along_z(pairs[k], k).astype(F32) for k in range(1, n_z)], pairs[0].astype(F32)
    )
    dnormed = columns[:own_width]
    tail = columns[own_width:]
    plain = (tail[0] + tail[1]) / width
    cross = (tail[2] + tail[3]) / width

    column_start = lax.axis_index(COLS) * own_width
    gain_own = lax.dynamic_slice_in_dim(gain, column_start, own_width, 0)[:, None]
    xhat_own = (own_t.astype(F32) - mean) * inv
    hidden = (inv * (dnormed * gain_own - plain - xhat_own * cross)).astype(BF16).T
    sums = jnp.concatenate([jnp.sum(dnormed * xhat_own, 1), jnp.sum(dnormed, 1)])
    sums, grad_weight = lax.optimization_barrier((sums, grad_weight))
    sums = jnp.sum(copies(sums[None], ENC), (0, 1))
    return embeds_recv, hidden, grad_weight, sums[:own_width], sums[own_width:]


def solution(mesh):
    devices = mesh.devices
    split = Mesh(devices.reshape(8, 4, 4, 2, 2), ("y", "x", "zl", "co", "zh"))
    spec = P(ENC, COLS)
    in_specs = (spec, P(), P(), spec, P(ENC, None), spec)
    out_specs = (spec, spec, spec, P(COLS), P(COLS))
    return jax.shard_map(body, mesh=split, in_specs=in_specs, out_specs=out_specs, check_vma=False)
```

time: 334 us -> 240 us (0.72)
  waiting for transfers between devices: 223 us -> 59.3 us
  starting transfers between devices: 33 us -> 118 us
  blocking collectives: 28 us -> 0 us
  Pallas kernels: 0 us -> 10.3 us
  other arithmetic: 8.74 us -> 3.82 us
  local copies, waits for them, and re-layouts: 13.1 us -> 17 us
    all_gather x2 -> x1, waiting for transfers between devices: 124 us -> 0.02 us  [body(): lax.all_gather(weight_x.reshape(n_x * slice_rows, out_cols), 'y', axis=0,...]
    ppermute x0 -> x22, starting transfers between devices: none -> 83.7 us  [the longest x14 56.8 us: along_z(): lax.ppermute(x, ('zl', 'zh'), [(at[z], at[(z + step) % count]) for z in r...]
    all_to_all x5 -> x4, waiting for transfers between devices: 94.6 us -> 16.4 us  [exchange(): return lax.all_to_all(x, axes, 0, 0, tiled=True)]
    ppermute x0 -> x22, waiting for transfers between devices: none -> 42.9 us  [the longest x6 30.2 us: shifted(): lax.ppermute(x, axes, [(i, (i + step) % count) for i in range(count)])]
    all_gather x1 -> x0, blocking collectives: 15.5 us -> none  [whole_of(): x = lax.all_gather(x, axis, axis=dim, tiled=True)]
    unnamed x1 -> x0, blocking collectives: 12.5 us -> none
    pallas_call x0 -> x3, Pallas kernels: none -> 10.3 us  [the longest x1 5.96 us: body(): pl.pallas_call(functools.partial(part_kernel, n_zl, n_zh), out_shape=(hal...]
    unnamed x4 -> x1, waiting for transfers between devices: 4.41 us -> 0.02 us
  transfers between devices with their start and end apart: 9 -> 27, of which waited for: 8 -> 11; matrix products, arithmetic and copies ran while one was open for 9% -> 11% of each run, Pallas kernels for 0% -> 4%
where the time goes in v1:
time: 240 us; the launch traced here: 237 us
  starting transfers between devices  118 us (49%)
  waiting for transfers between devices  59.3 us (25%)
  local copies, waits for them, and re-layouts  17 us (7%)
  between operations  14.7 us (6%)
  matrix products  14.3 us (6%)
  Pallas kernels  10.3 us (4%)
  other arithmetic  3.82 us (2%)
    ppermute x14, starting transfers between devices, along_z(): lax.ppermute(x, ('zl', 'zh'), [(at[z], at[(z + step) % count]) for z in r...  56.8 us
    all_to_all x4, starting transfers between devices, exchange(): return lax.all_to_all(x, axes, 0, 0, tiled=True)  34.4 us
    ppermute x6, waiting for transfers between devices, shifted(): lax.ppermute(x, axes, [(i, (i + step) % count) for i in range(count)])  30.2 us
    ppermute x6, starting transfers between devices, shifted(): lax.ppermute(x, axes, [(i, (i + step) % count) for i in range(count)])  23 us
    all_to_all x4, waiting for transfers between devices, exchange(): return lax.all_to_all(x, axes, 0, 0, tiled=True)  16.4 us
    ppermute x14, waiting for transfers between devices, along_z(): lax.ppermute(x, ('zl', 'zh'), [(at[z], at[(z + step) % count]) for z in r...  11.7 us
    dot_general x4, matrix products, grad_block(): return jnp.dot(lhs, d_embed, preferred_element_type=F32).astype(BF16)  10.1 us
    unnamed x33, local copies, waits for them, and re-layouts  6.18 us
  transfers between devices with their start and end apart: 27, of which 11 were waited for; matrix products, arithmetic and copies ran while one was open for 11% of the time, Pallas kernels for 4%

profile of v1, /device:TPU:6, one launch (start us, length us, event | category | flops | bytes accessed | tf_op | source)
XLA Modules:
  0.0 237.5 jit_solution(2372411586365351448)
XLA Ops:
  7.2 2.7 %collective-permute-start.11 = (bf16[100,512]{1,0:T(8,128)(2,1)}, bf16[100,512]{1,0:T(8,128)(2,1)S(1)}, u32[]{:S(2)}, u32[]{:S(2)}) collective-permute-start(bf16[100,512]{1,0:T(8,128)(2,1)} %param.9), channel_id=1, source_target_pairs={{0,48},{16,0},{32,16},{48,32},{1,49},{17,1},{33,17},{49,33},{2,50}... | collective-permute-start | bytes 307208 | tf_op jit(solution)/shard_map/ppermute | solution.py:33
  10.0 8.4 %collective-permute-start.12 = (bf16[100,512]{1,0:T(8,128)(2,1)}, bf16[100,512]{1,0:T(8,128)(2,1)S(1)}, u32[]{:S(2)}, u32[]{:S(2)}) collective-permute-start(bf16[100,512]{1,0:T(8,128)(2,1)} %param.9), channel_id=1, source_target_pairs={{0,32},{16,48},{32,0},{48,16},{1,33},{17,49},{33,1},{49,17},{2,34}... | collective-permute-start | bytes 307208 | tf_op jit(solution)/shard_map/ppermute | solution.py:33
  21.3 3.9 %collective-permute-done.13 = bf16[100,512]{1,0:T(8,128)(2,1)S(1)} collective-permute-done((bf16[100,512]{1,0:T(8,128)(2,1)}, bf16[100,512]{1,0:T(8,128)(2,1)S(1)}, u32[]{:S(2)}, u32[]{:S(2)}) %collective-permute-start.13) | collective-permute-done | bytes 102432 | tf_op jit(solution)/shard_map/ppermute | solution.py:33
  29.0 3.6 %collective-permute-start.1 = (bf16[200,256]{1,0:T(8,128)(2,1)S(1)}, bf16[200,256]{1,0:T(8,128)(2,1)S(1)}, u32[]{:S(2)}, u32[]{:S(2)}) collective-permute-start(bf16[200,256]{1,0:T(8,128)(2,1)S(1)} %bitcast.99), channel_id=1, source_target_pairs={{0,8},{4,12},{8,1},{12,5},{1,9},{5,13},{9,0},{13,4},{2,10},{6,14},... | collective-permute-start | bytes 307208 | tf_op jit(solution)/shard_map/ppermute | solution.py:40
  32.6 7.3 %collective-permute-start.2 = (bf16[200,256]{1,0:T(8,128)(2,1)S(1)}, bf16[200,256]{1,0:T(8,128)(2,1)S(1)}, u32[]{:S(2)}, u32[]{:S(2)}) collective-permute-start(bf16[200,256]{1,0:T(8,128)(2,1)S(1)} %bitcast.100), channel_id=1, source_target_pairs={{0,12},{4,1},{8,5},{12,9},{1,13},{5,0},{9,4},{13,8},{2,14},{6,3},{... | collective-permute-start | bytes 307208 | tf_op jit(solution)/shard_map/ppermute | solution.py:40
  39.9 2.8 %collective-permute-start.3 = (bf16[200,256]{1,0:T(8,128)(2,1)S(1)}, bf16[200,256]{1,0:T(8,128)(2,1)S(1)}, u32[]{:S(2)}, u32[]{:S(2)}) collective-permute-start(bf16[200,256]{1,0:T(8,128)(2,1)S(1)} %bitcast.101), channel_id=1, source_target_pairs={{0,1},{4,5},{8,9},{12,13},{1,0},{5,4},{9,8},{13,12},{2,3},{6,7},{1... | collective-permute-start | bytes 307208 | tf_op jit(solution)/shard_map/ppermute | solution.py:40
  42.7 6.9 %collective-permute-start.4 = (bf16[200,256]{1,0:T(8,128)(2,1)S(1)}, bf16[200,256]{1,0:T(8,128)(2,1)S(1)}, u32[]{:S(2)}, u32[]{:S(2)}) collective-permute-start(bf16[200,256]{1,0:T(8,128)(2,1)S(1)} %bitcast.102), channel_id=1, source_target_pairs={{0,5},{4,9},{8,13},{12,0},{1,4},{5,8},{9,12},{13,1},{2,7},{6,11},{... | collective-permute-start | bytes 307208 | tf_op jit(solution)/shard_map/ppermute | solution.py:40
  49.7 11.1 %all-to-all-start = ((bf16[32,24,512]{2,1,0:T(8,128)(2,1)}), bf16[32,24,512]{2,1,0:T(8,128)(2,1)}, u32[]{:S(2)}, u32[]{:S(2)}) async-start(bf16[32,24,512]{2,1,0:T(8,128)(2,1)} %bitcast.13), calls=%async_computation | async-start | bytes 1572864 | tf_op jit(solution)/shard_map/all_to_all | solution.py:23
  60.8 3.7 %collective-permute-start.5 = (bf16[200,256]{1,0:T(8,128)(2,1)S(1)}, bf16[200,256]{1,0:T(8,128)(2,1)S(1)}, u32[]{:S(2)}, u32[]{:S(2)}) collective-permute-start(bf16[200,256]{1,0:T(8,128)(2,1)S(1)} %bitcast.103), channel_id=1, source_target_pairs={{0,9},{4,13},{8,0},{12,4},{1,8},{5,12},{9,1},{13,5},{2,11},{6,15},... | collective-permute-start | bytes 307208 | tf_op jit(solution)/shard_map/ppermute | solution.py:40
  77.5 4.2 %norm.1 = (bf16[16,200,256]{2,1,0:T(8,128)(2,1)S(1)}, bf16[4,8,104,256]{3,2,1,0:T(8,128)(2,1)}, f32[8,256]{1,0:T(8,128)S(1)}) custom-call(s32[2]{0:T(128)S(1)} %pad_add_fusion.place, bf16[8,200,256]{2,1,0:T(8,128)(2,1)S(1)} %bitcast_dynamic-update-slice_fusion.9.mine, bf16[8,200,256]{2,1,0:T(8,128)(2,1)S(1)} %collective-permute-done.7.other, ...), custom_call_target="tpu_custom_call" | custom-call | tf_op jit(solution)/shard_map/norm/pallas_call | solution.py:182
  82.9 8.0 %all-to-all-done = bf16[32,24,512]{2,1,0:T(8,128)(2,1)} async-done(((bf16[32,24,512]{2,1,0:T(8,128)(2,1)}), bf16[32,24,512]{2,1,0:T(8,128)(2,1)}, u32[]{:S(2)}, u32[]{:S(2)}) %all-to-all-start) | async-done | bytes 786464 | tf_op jit(solution)/shard_map/all_to_all | solution.py:23
  95.6 2.7 %collective-permute-start.10 = (bf16[832,512]{1,0:T(8,128)(2,1)}, bf16[832,512]{1,0:T(8,128)(2,1)}, u32[]{:S(2)}, u32[]{:S(2)}) collective-permute-start(bf16[832,512]{1,0:T(8,128)(2,1)} %convolution_convert_fusion), channel_id=1, source_target_pairs={{0,48},{16,0},{32,16},{48,32},{1,49},{17,1},{33,17},{49,33},{2,50}... | collective-permute-start | bytes 2555912 | tf_op jit(solution)/shard_map/ppermute | solution.py:33
  98.3 4.2 %convolution_convert_fusion.4 = bf16[256,512]{1,0:T(8,128)(2,1)} fusion(bf16[3200,256]{1,0:T(8,128)(2,1)} %bitcast.90, bf16[3200,512]{1,0:T(8,128)(2,1)} %all-gather.2.cloned.1.call-done), kind=kOutput, calls=%fused_computation.8 | convolution fusion | flops 838991872 | bytes 5177344 | tf_op jit(solution)/shard_map/dot_general | solution.py:213
  102.5 2.9 %scatter_custom_fusion = bf16[768,512]{1,0:T(8,128)(2,1)} fusion(s32[256]{0:T(256)} %bitcast.113, bf16[256,512]{1,0:T(8,128)(2,1)} %convolution_convert_fusion.4, bf16[]{:T(256)} %constant.62.clone.1), kind=kCustom, calls=%fused_computation.17 | custom fusion | bytes 786944 | tf_op jit(solution)/shard_map/scatter | solution.py:216
  105.4 6.7 %all-to-all-start.1 = ((bf16[32,24,512]{2,1,0:T(8,128)(2,1)}), bf16[32,24,512]{2,1,0:T(8,128)(2,1)}, u32[]{:S(2)}, u32[]{:S(2)}) async-start(bf16[32,24,512]{2,1,0:T(8,128)(2,1)} %bitcast.93), calls=%async_computation.1 | async-start | bytes 1572864 | tf_op jit(solution)/shard_map/all_to_all | solution.py:23
  114.4 3.3 %collective-permute-start.9 = (bf16[832,512]{1,0:T(8,128)(2,1)}, bf16[832,512]{1,0:T(8,128)(2,1)}, u32[]{:S(2)}, u32[]{:S(2)}) collective-permute-start(bf16[832,512]{1,0:T(8,128)(2,1)} %convolution_convert_fusion.1), channel_id=1, source_target_pairs={{0,32},{16,48},{32,0},{48,16},{1,33},{17,49},{33,1},{49,17},{2,34}... | collective-permute-start | bytes 2555912 | tf_op jit(solution)/shard_map/ppermute | solution.py:33
  120.0 4.0 %collective-permute-start.8 = (bf16[832,512]{1,0:T(8,128)(2,1)}, bf16[832,512]{1,0:T(8,128)(2,1)}, u32[]{:S(2)}, u32[]{:S(2)}) collective-permute-start(bf16[832,512]{1,0:T(8,128)(2,1)} %convolution_convert_fusion.2), channel_id=1, source_target_pairs={{0,16},{16,32},{32,48},{48,0},{1,17},{17,33},{33,49},{49,1},{2,18}... | collective-permute-start | bytes 2555912 | tf_op jit(solution)/shard_map/ppermute | solution.py:33
  124.0 6.0 %part.1 = (bf16[8,208,256]{2,1,0:T(8,128)(2,1)S(1)}, bf16[8,208,256]{2,1,0:T(8,128)(2,1)}) custom-call(s32[2]{0:T(128)S(1)} %pad_add_fusion.place, bf16[16,200,512]{2,1,0:T(8,128)(2,1)} %bitcast.92, bf16[256,512]{1,0:T(8,128)(2,1)S(1)} %gather_fusion, bf16[8,200,256]{2,1,0:T(8,128)(2,1)S(1)} %bitcast_dynamic-update-slice_fusion.9.mine, ...), custom_call_target="tpu_custom_call" | custom-call | tf_op jit(solution)/shard_map/part/pallas_call | solution.py:226
  132.8 9.9 %collective-permute-done.10 = bf16[832,512]{1,0:T(8,128)(2,1)} collective-permute-done((bf16[832,512]{1,0:T(8,128)(2,1)}, bf16[832,512]{1,0:T(8,128)(2,1)}, u32[]{:S(2)}, u32[]{:S(2)}) %collective-permute-start.10) | collective-permute-done | bytes 852000 | tf_op jit(solution)/shard_map/ppermute | solution.py:33
  142.7 16.4 %collective-permute-done.8 = bf16[832,512]{1,0:T(8,128)(2,1)} collective-permute-done((bf16[832,512]{1,0:T(8,128)(2,1)}, bf16[832,512]{1,0:T(8,128)(2,1)}, u32[]{:S(2)}, u32[]{:S(2)}) %collective-permute-start.8) | collective-permute-done | bytes 852000 | tf_op jit(solution)/shard_map/ppermute | solution.py:33
  159.1 3.2 %add_convert_fusion = bf16[832,512]{1,0:T(8,128)(2,1)} fusion(bf16[832,512]{1,0:T(8,128)(2,1)} %collective-permute-done.10, bf16[832,512]{1,0:T(8,128)(2,1)} %collective-permute-done.9, bf16[832,512]{1,0:T(8,128)(2,1)} %collective-permute-done.8, bf16[256,512]{1,0:T(8,128)(2,1)S(1)} %gather_fusion, bf16[4,832,256]{2,1,0:T(8,128)(2,1)} %bitcast.97, ...), kind=kOutput, calls=%fused_computation.3 | convolution fusion | flops 221937664 | bytes 4096004 | tf_op jit(solution)/shard_map/dot_general | solution.py:207
  162.3 4.9 %all-to-all-start.2 = ((bf16[8,104,512]{2,1,0:T(8,128)(2,1)}), bf16[8,104,512]{2,1,0:T(8,128)(2,1)}, u32[]{:S(2)}, u32[]{:S(2)}) async-start(bf16[8,104,512]{2,1,0:T(8,128)(2,1)} %bitcast.91), calls=%async_computation.2 | async-start | bytes 1703936 | tf_op jit(solution)/shard_map/all_to_all | solution.py:23
  167.4 4.5 %collective-permute-start.21 = (bf16[208,256]{1,0:T(8,128)(2,1)S(1)}, bf16[208,256]{1,0:T(8,128)(2,1)S(1)}, u32[]{:S(2)}, u32[]{:S(2)}) collective-permute-start(bf16[208,256]{1,0:T(8,128)(2,1)S(1)} %get-tuple-element.35), channel_id=1, source_target_pairs={{0,13},{4,0},{8,4},{12,8},{1,12},{5,1},{9,5},{13,9},{2,15},{6,2},{... | collective-permute-start | bytes 319496 | tf_op jit(solution)/shard_map/ppermute | solution.py:40
  171.9 4.0 %collective-permute-start.20 = (bf16[208,256]{1,0:T(8,128)(2,1)S(1)}, bf16[208,256]{1,0:T(8,128)(2,1)S(1)}, u32[]{:S(2)}, u32[]{:S(2)}) collective-permute-start(bf16[208,256]{1,0:T(8,128)(2,1)S(1)} %get-tuple-element.34), channel_id=1, source_target_pairs={{0,9},{4,13},{8,0},{12,4},{1,8},{5,12},{9,1},{13,5},{2,11},{6,15},... | collective-permute-start | bytes 319496 | tf_op jit(solution)/shard_map/ppermute | solution.py:40
  176.7 2.7 %collective-permute-start.19 = (bf16[208,256]{1,0:T(8,128)(2,1)S(1)}, bf16[208,256]{1,0:T(8,128)(2,1)S(1)}, u32[]{:S(2)}, u32[]{:S(2)}) collective-permute-start(bf16[208,256]{1,0:T(8,128)(2,1)S(1)} %get-tuple-element.33), channel_id=1, source_target_pairs={{0,5},{4,9},{8,13},{12,0},{1,4},{5,8},{9,12},{13,1},{2,7},{6,11},{... | collective-permute-start | bytes 319496 | tf_op jit(solution)/shard_map/ppermute | solution.py:40
  179.3 6.4 %collective-permute-start.18 = (bf16[208,256]{1,0:T(8,128)(2,1)S(1)}, bf16[208,256]{1,0:T(8,128)(2,1)S(1)}, u32[]{:S(2)}, u32[]{:S(2)}) collective-permute-start(bf16[208,256]{1,0:T(8,128)(2,1)S(1)} %get-tuple-element.32), channel_id=1, source_target_pairs={{0,1},{4,5},{8,9},{12,13},{1,0},{5,4},{9,8},{13,12},{2,3},{6,7},{1... | collective-permute-start | bytes 319496 | tf_op jit(solution)/shard_map/ppermute | solution.py:40
  187.7 5.1 %collective-permute-start.16 = (bf16[208,256]{1,0:T(8,128)(2,1)S(1)}, bf16[208,256]{1,0:T(8,128)(2,1)S(1)}, u32[]{:S(2)}, u32[]{:S(2)}) collective-permute-start(bf16[208,256]{1,0:T(8,128)(2,1)S(1)} %get-tuple-element.30), channel_id=1, source_target_pairs={{0,8},{4,12},{8,1},{12,5},{1,9},{5,13},{9,0},{13,4},{2,10},{6,14},... | collective-permute-start | bytes 319496 | tf_op jit(solution)/shard_map/ppermute | solution.py:40
  192.8 3.6 %collective-permute-start.15 = (bf16[208,256]{1,0:T(8,128)(2,1)S(1)}, bf16[208,256]{1,0:T(8,128)(2,1)S(1)}, u32[]{:S(2)}, u32[]{:S(2)}) collective-permute-start(bf16[208,256]{1,0:T(8,128)(2,1)S(1)} %get-tuple-element.29), channel_id=1, source_target_pairs={{0,4},{4,8},{8,12},{12,1},{1,5},{5,9},{9,13},{13,0},{2,6},{6,10},{... | collective-permute-start | bytes 319496 | tf_op jit(solution)/shard_map/ppermute | solution.py:40
  196.4 3.8 %collective-permute-done.17 = bf16[208,256]{1,0:T(8,128)(2,1)S(1)} collective-permute-done((bf16[208,256]{1,0:T(8,128)(2,1)S(1)}, bf16[208,256]{1,0:T(8,128)(2,1)S(1)}, u32[]{:S(2)}, u32[]{:S(2)}) %collective-permute-start.17) | collective-permute-done | bytes 106528 | tf_op jit(solution)/shard_map/ppermute | solution.py:40
  200.2 3.1 %collective-permute-done.16 = bf16[208,256]{1,0:T(8,128)(2,1)S(1)} collective-permute-done((bf16[208,256]{1,0:T(8,128)(2,1)S(1)}, bf16[208,256]{1,0:T(8,128)(2,1)S(1)}, u32[]{:S(2)}, u32[]{:S(2)}) %collective-permute-start.16) | collective-permute-done | bytes 106528 | tf_op jit(solution)/shard_map/ppermute | solution.py:40
  207.7 11.7 %all-to-all-start.3 = ((f32[32,1,400]{2,1,0:T(1,128)}), f32[32,1,400]{2,1,0:T(1,128)S(1)}, u32[]{:S(2)}, u32[]{:S(2)}) async-start(f32[32,1,400]{2,1,0:T(1,128)} %broadcast_in_dim.33), calls=%async_computation.3 | async-start | bytes 131072 | tf_op jit(solution)/shard_map/all_to_all | solution.py:23
  219.5 8.4 %all-to-all-done.3 = f32[32,1,400]{2,1,0:T(1,128)S(1)} async-done(((f32[32,1,400]{2,1,0:T(1,128)}), f32[32,1,400]{2,1,0:T(1,128)S(1)}, u32[]{:S(2)}, u32[]{:S(2)}) %all-to-all-start.3) | async-done | bytes 51232 | tf_op jit(solution)/shard_map/all_to_all | solution.py:23
  (93 shorter events, 43.0 us)
Async XLA Ops:
  7.2 91.1 %all-gather.2.cloned.1.call-start = ((), (), s32[]{:S(2)}) async-start(), calls=%async_computation.4 | async-start | bytes 3686400 | tf_op jit(solution)/shard_map/all_gather | solution.py:175
  7.2 14.0 %collective-permute-start.11 = (bf16[100,512]{1,0:T(8,128)(2,1)}, bf16[100,512]{1,0:T(8,128)(2,1)S(1)}, u32[]{:S(2)}, u32[]{:S(2)}) collective-permute-start(bf16[100,512]{1,0:T(8,128)(2,1)} %param.9), channel_id=1, source_target_pairs={{0,48},{16,0},{32,16},{48,32},{1,49},{17,1},{33,17},{49,33},{2,50}... | collective-permute-start | bytes 307208 | tf_op jit(solution)/shard_map/ppermute | solution.py:33
  10.0 11.3 %collective-permute-start.12 = (bf16[100,512]{1,0:T(8,128)(2,1)}, bf16[100,512]{1,0:T(8,128)(2,1)S(1)}, u32[]{:S(2)}, u32[]{:S(2)}) collective-permute-start(bf16[100,512]{1,0:T(8,128)(2,1)} %param.9), channel_id=1, source_target_pairs={{0,32},{16,48},{32,0},{48,16},{1,33},{17,49},{33,1},{49,17},{2,34}... | collective-permute-start | bytes 307208 | tf_op jit(solution)/shard_map/ppermute | solution.py:33
  18.4 6.8 %collective-permute-start.13 = (bf16[100,512]{1,0:T(8,128)(2,1)}, bf16[100,512]{1,0:T(8,128)(2,1)S(1)}, u32[]{:S(2)}, u32[]{:S(2)}) collective-permute-start(bf16[100,512]{1,0:T(8,128)(2,1)} %param.9), channel_id=1, source_target_pairs={{0,16},{16,32},{32,48},{48,0},{1,17},{17,33},{33,49},{49,1},{2,18}... | collective-permute-start | bytes 307208 | tf_op jit(solution)/shard_map/ppermute | solution.py:33
  21.2 5.8 %copy-start.3 = (bf16[256,200]{0,1:T(8,128)(2,1)S(1)}, bf16[256,200]{0,1:T(8,128)(2,1)}, u32[]{:S(2)}) copy-start(bf16[256,200]{0,1:T(8,128)(2,1)} %param.6) | copy-start | bytes 307204
  27.0 46.0 %copy-start.7 = (s32[256,1]{0,1:T(1,128)S(1)}, s32[256,1]{0,1:T(1,128)}, u32[]{:S(2)}) copy-start(s32[256,1]{0,1:T(1,128)} %param.10) | copy-start | bytes 3076
  27.1 33.8 %collective-permute-start = (bf16[200,256]{1,0:T(8,128)(2,1)S(1)}, bf16[200,256]{1,0:T(8,128)(2,1)S(1)}, u32[]{:S(2)}, u32[]{:S(2)}) collective-permute-start(bf16[200,256]{1,0:T(8,128)(2,1)S(1)} %bitcast.98), channel_id=1, source_target_pairs={{0,4},{4,8},{8,12},{12,1},{1,5},{5,9},{9,13},{13,0},{2,6},{6,10},{... | collective-permute-start | bytes 307208 | tf_op jit(solution)/shard_map/ppermute | solution.py:40
  29.0 35.5 %collective-permute-start.1 = (bf16[200,256]{1,0:T(8,128)(2,1)S(1)}, bf16[200,256]{1,0:T(8,128)(2,1)S(1)}, u32[]{:S(2)}, u32[]{:S(2)}) collective-permute-start(bf16[200,256]{1,0:T(8,128)(2,1)S(1)} %bitcast.99), channel_id=1, source_target_pairs={{0,8},{4,12},{8,1},{12,5},{1,9},{5,13},{9,0},{13,4},{2,10},{6,14},... | collective-permute-start | bytes 307208 | tf_op jit(solution)/shard_map/ppermute | solution.py:40
  32.6 34.4 %collective-permute-start.2 = (bf16[200,256]{1,0:T(8,128)(2,1)S(1)}, bf16[200,256]{1,0:T(8,128)(2,1)S(1)}, u32[]{:S(2)}, u32[]{:S(2)}) collective-permute-start(bf16[200,256]{1,0:T(8,128)(2,1)S(1)} %bitcast.100), channel_id=1, source_target_pairs={{0,12},{4,1},{8,5},{12,9},{1,13},{5,0},{9,4},{13,8},{2,14},{6,3},{... | collective-permute-start | bytes 307208 | tf_op jit(solution)/shard_map/ppermute | solution.py:40
  39.9 27.2 %collective-permute-start.3 = (bf16[200,256]{1,0:T(8,128)(2,1)S(1)}, bf16[200,256]{1,0:T(8,128)(2,1)S(1)}, u32[]{:S(2)}, u32[]{:S(2)}) collective-permute-start(bf16[200,256]{1,0:T(8,128)(2,1)S(1)} %bitcast.101), channel_id=1, source_target_pairs={{0,1},{4,5},{8,9},{12,13},{1,0},{5,4},{9,8},{13,12},{2,3},{6,7},{1... | collective-permute-start | bytes 307208 | tf_op jit(solution)/shard_map/ppermute | solution.py:40
  42.7 24.3 %collective-permute-start.4 = (bf16[200,256]{1,0:T(8,128)(2,1)S(1)}, bf16[200,256]{1,0:T(8,128)(2,1)S(1)}, u32[]{:S(2)}, u32[]{:S(2)}) collective-permute-start(bf16[200,256]{1,0:T(8,128)(2,1)S(1)} %bitcast.102), channel_id=1, source_target_pairs={{0,5},{4,9},{8,13},{12,0},{1,4},{5,8},{9,12},{13,1},{2,7},{6,11},{... | collective-permute-start | bytes 307208 | tf_op jit(solution)/shard_map/ppermute | solution.py:40
  49.7 24.2 %copy-start.5 = (f32[3200]{0:T(1024)S(1)}, f32[3200]{0:T(1024)}, u32[]{:S(2)}) copy-start(f32[3200]{0:T(1024)} %param.7) | copy-start | bytes 38404
  49.7 24.3 %copy-start.6 = (f32[3200]{0:T(1024)S(1)}, f32[3200]{0:T(1024)}, u32[]{:S(2)}) copy-start(f32[3200]{0:T(1024)} %param.8) | copy-start | bytes 38404
  49.7 41.2 %all-to-all-start = ((bf16[32,24,512]{2,1,0:T(8,128)(2,1)}), bf16[32,24,512]{2,1,0:T(8,128)(2,1)}, u32[]{:S(2)}, u32[]{:S(2)}) async-start(bf16[32,24,512]{2,1,0:T(8,128)(2,1)} %bitcast.13), calls=%async_computation | async-start | bytes 1572864 | tf_op jit(solution)/shard_map/all_to_all | solution.py:23
  60.8 8.1 %collective-permute-start.5 = (bf16[200,256]{1,0:T(8,128)(2,1)S(1)}, bf16[200,256]{1,0:T(8,128)(2,1)S(1)}, u32[]{:S(2)}, u32[]{:S(2)}) collective-permute-start(bf16[200,256]{1,0:T(8,128)(2,1)S(1)} %bitcast.103), channel_id=1, source_target_pairs={{0,9},{4,13},{8,0},{12,4},{1,8},{5,12},{9,1},{13,5},{2,11},{6,15},... | collective-permute-start | bytes 307208 | tf_op jit(solution)/shard_map/ppermute | solution.py:40
  64.5 6.6 %collective-permute-start.6 = (bf16[200,256]{1,0:T(8,128)(2,1)S(1)}, bf16[200,256]{1,0:T(8,128)(2,1)S(1)}, u32[]{:S(2)}, u32[]{:S(2)}) collective-permute-start(bf16[200,256]{1,0:T(8,128)(2,1)S(1)} %bitcast.104), channel_id=1, source_target_pairs={{0,13},{4,0},{8,4},{12,8},{1,12},{5,1},{9,5},{13,9},{2,15},{6,2},{... | collective-permute-start | bytes 307208 | tf_op jit(solution)/shard_map/ppermute | solution.py:40
  71.1 4.2 %collective-permute-start.7 = (bf16[8,200,256]{2,1,0:T(8,128)(2,1)S(1)}, bf16[8,200,256]{2,1,0:T(8,128)(2,1)S(1)}, u32[]{:S(2)}, u32[]{:S(2)}) collective-permute-start(bf16[8,200,256]{2,1,0:T(8,128)(2,1)S(1)} %bitcast_dynamic-update-slice_fusion.9.mine), channel_id=1, source_target_pairs={{0,2},{2,0},{1,3},{3,1},{4,6},{6,4},{5,7},{7,5},{8,10},{10,8},{9,1... | collective-permute-start | bytes 2457608 | tf_op jit(solution)/shard_map/ppermute | solution.py:44
  95.6 47.1 %collective-permute-start.10 = (bf16[832,512]{1,0:T(8,128)(2,1)}, bf16[832,512]{1,0:T(8,128)(2,1)}, u32[]{:S(2)}, u32[]{:S(2)}) collective-permute-start(bf16[832,512]{1,0:T(8,128)(2,1)} %convolution_convert_fusion), channel_id=1, source_target_pairs={{0,48},{16,0},{32,16},{48,32},{1,49},{17,1},{33,17},{49,33},{2,50}... | collective-permute-start | bytes 2555912 | tf_op jit(solution)/shard_map/ppermute | solution.py:33
  105.4 57.0 %all-to-all-start.1 = ((bf16[32,24,512]{2,1,0:T(8,128)(2,1)}), bf16[32,24,512]{2,1,0:T(8,128)(2,1)}, u32[]{:S(2)}, u32[]{:S(2)}) async-start(bf16[32,24,512]{2,1,0:T(8,128)(2,1)} %bitcast.93), calls=%async_computation.1 | async-start | bytes 1572864 | tf_op jit(solution)/shard_map/all_to_all | solution.py:23
  114.4 28.3 %collective-permute-start.9 = (bf16[832,512]{1,0:T(8,128)(2,1)}, bf16[832,512]{1,0:T(8,128)(2,1)}, u32[]{:S(2)}, u32[]{:S(2)}) collective-permute-start(bf16[832,512]{1,0:T(8,128)(2,1)} %convolution_convert_fusion.1), channel_id=1, source_target_pairs={{0,32},{16,48},{32,0},{48,16},{1,33},{17,49},{33,1},{49,17},{2,34}... | collective-permute-start | bytes 2555912 | tf_op jit(solution)/shard_map/ppermute | solution.py:33
  120.0 39.1 %collective-permute-start.8 = (bf16[832,512]{1,0:T(8,128)(2,1)}, bf16[832,512]{1,0:T(8,128)(2,1)}, u32[]{:S(2)}, u32[]{:S(2)}) collective-permute-start(bf16[832,512]{1,0:T(8,128)(2,1)} %convolution_convert_fusion.2), channel_id=1, source_target_pairs={{0,16},{16,32},{32,48},{48,0},{1,17},{17,33},{33,49},{49,1},{2,18}... | collective-permute-start | bytes 2555912 | tf_op jit(solution)/shard_map/ppermute | solution.py:33
  130.9 36.3 %collective-permute-start.14 = (bf16[8,208,256]{2,1,0:T(8,128)(2,1)}, bf16[8,208,256]{2,1,0:T(8,128)(2,1)S(1)}, u32[]{:S(2)}, u32[]{:S(2)}) collective-permute-start(bf16[8,208,256]{2,1,0:T(8,128)(2,1)} %get-tuple-element.27), channel_id=1, source_target_pairs={{0,2},{2,0},{1,3},{3,1},{4,6},{6,4},{5,7},{7,5},{8,10},{10,8},{9,1... | collective-permute-start | bytes 2555912 | tf_op jit(solution)/shard_map/ppermute | solution.py:44
  162.3 42.8 %all-to-all-start.2 = ((bf16[8,104,512]{2,1,0:T(8,128)(2,1)}), bf16[8,104,512]{2,1,0:T(8,128)(2,1)}, u32[]{:S(2)}, u32[]{:S(2)}) async-start(bf16[8,104,512]{2,1,0:T(8,128)(2,1)} %bitcast.91), calls=%async_computation.2 | async-start | bytes 1703936 | tf_op jit(solution)/shard_map/all_to_all | solution.py:23
  167.2 37.1 %copy-start.4 = (bf16[256,200]{0,1:T(8,128)(2,1)S(1)}, bf16[256,200]{0,1:T(8,128)(2,1)}, u32[]{:S(2)}) copy-start(bf16[256,200]{0,1:T(8,128)(2,1)} %param.6) | copy-start | bytes 307204
  167.4 20.2 %collective-permute-start.21 = (bf16[208,256]{1,0:T(8,128)(2,1)S(1)}, bf16[208,256]{1,0:T(8,128)(2,1)S(1)}, u32[]{:S(2)}, u32[]{:S(2)}) collective-permute-start(bf16[208,256]{1,0:T(8,128)(2,1)S(1)} %get-tuple-element.35), channel_id=1, source_target_pairs={{0,13},{4,0},{8,4},{12,8},{1,12},{5,1},{9,5},{13,9},{2,15},{6,2},{... | collective-permute-start | bytes 319496 | tf_op jit(solution)/shard_map/ppermute | solution.py:40
  171.9 20.9 %collective-permute-start.20 = (bf16[208,256]{1,0:T(8,128)(2,1)S(1)}, bf16[208,256]{1,0:T(8,128)(2,1)S(1)}, u32[]{:S(2)}, u32[]{:S(2)}) collective-permute-start(bf16[208,256]{1,0:T(8,128)(2,1)S(1)} %get-tuple-element.34), channel_id=1, source_target_pairs={{0,9},{4,13},{8,0},{12,4},{1,8},{5,12},{9,1},{13,5},{2,11},{6,15},... | collective-permute-start | bytes 319496 | tf_op jit(solution)/shard_map/ppermute | solution.py:40
  176.7 19.7 %collective-permute-start.19 = (bf16[208,256]{1,0:T(8,128)(2,1)S(1)}, bf16[208,256]{1,0:T(8,128)(2,1)S(1)}, u32[]{:S(2)}, u32[]{:S(2)}) collective-permute-start(bf16[208,256]{1,0:T(8,128)(2,1)S(1)} %get-tuple-element.33), channel_id=1, source_target_pairs={{0,5},{4,9},{8,13},{12,0},{1,4},{5,8},{9,12},{13,1},{2,7},{6,11},{... | collective-permute-start | bytes 319496 | tf_op jit(solution)/shard_map/ppermute | solution.py:40
  179.3 17.1 %collective-permute-start.18 = (bf16[208,256]{1,0:T(8,128)(2,1)S(1)}, bf16[208,256]{1,0:T(8,128)(2,1)S(1)}, u32[]{:S(2)}, u32[]{:S(2)}) collective-permute-start(bf16[208,256]{1,0:T(8,128)(2,1)S(1)} %get-tuple-element.32), channel_id=1, source_target_pairs={{0,1},{4,5},{8,9},{12,13},{1,0},{5,4},{9,8},{13,12},{2,3},{6,7},{1... | collective-permute-start | bytes 319496 | tf_op jit(solution)/shard_map/ppermute | solution.py:40
  185.7 14.5 %collective-permute-start.17 = (bf16[208,256]{1,0:T(8,128)(2,1)S(1)}, bf16[208,256]{1,0:T(8,128)(2,1)S(1)}, u32[]{:S(2)}, u32[]{:S(2)}) collective-permute-start(bf16[208,256]{1,0:T(8,128)(2,1)S(1)} %get-tuple-element.31), channel_id=1, source_target_pairs={{0,12},{4,1},{8,5},{12,9},{1,13},{5,0},{9,4},{13,8},{2,14},{6,3},{... | collective-permute-start | bytes 319496 | tf_op jit(solution)/shard_map/ppermute | solution.py:40
  187.7 15.6 %collective-permute-start.16 = (bf16[208,256]{1,0:T(8,128)(2,1)S(1)}, bf16[208,256]{1,0:T(8,128)(2,1)S(1)}, u32[]{:S(2)}, u32[]{:S(2)}) collective-permute-start(bf16[208,256]{1,0:T(8,128)(2,1)S(1)} %get-tuple-element.30), channel_id=1, source_target_pairs={{0,8},{4,12},{8,1},{12,5},{1,9},{5,13},{9,0},{13,4},{2,10},{6,14},... | collective-permute-start | bytes 319496 | tf_op jit(solution)/shard_map/ppermute | solution.py:40
  192.8 11.3 %collective-permute-start.15 = (bf16[208,256]{1,0:T(8,128)(2,1)S(1)}, bf16[208,256]{1,0:T(8,128)(2,1)S(1)}, u32[]{:S(2)}, u32[]{:S(2)}) collective-permute-start(bf16[208,256]{1,0:T(8,128)(2,1)S(1)} %get-tuple-element.29), channel_id=1, source_target_pairs={{0,4},{4,8},{8,12},{12,1},{1,5},{5,9},{9,13},{13,0},{2,6},{6,10},{... | collective-permute-start | bytes 319496 | tf_op jit(solution)/shard_map/ppermute | solution.py:40
  207.7 20.1 %all-to-all-start.3 = ((f32[32,1,400]{2,1,0:T(1,128)}), f32[32,1,400]{2,1,0:T(1,128)S(1)}, u32[]{:S(2)}, u32[]{:S(2)}) async-start(f32[32,1,400]{2,1,0:T(1,128)} %broadcast_in_dim.33), calls=%async_computation.3 | async-start | bytes 131072 | tf_op jit(solution)/shard_map/all_to_all | solution.py:23
  (4 other events, 8.5 us)
Sparse Core Ops, SparseCore 0:
  27.2 65.9 all-gather.1

commit v2 on v1

v2 whole, which is shorter than its diff:
```python
import functools

import jax
import jax.numpy as jnp
from jax import lax
from jax.experimental import pallas as pl
from jax.experimental.pallas import tpu as pltpu
from jax.sharding import Mesh
from jax.sharding import PartitionSpec as P

ENC = ("y", "x")
COLS = ("zl", "co", "zh")
EPSILON = 1e-05
F32 = jnp.float32
BF16 = jnp.bfloat16
VMEM = pl.BlockSpec(memory_space=pltpu.VMEM)
SMEM = pl.BlockSpec(memory_space=pltpu.SMEM)
PARAMS = pltpu.CompilerParams(vmem_limit_bytes=48 * 1024 * 1024)
EXTRA = 8


def exchange(x, axes):
    return lax.all_to_all(x, axes, 0, 0, tiled=True)


def copies(x, axes):
    count = lax.axis_size(axes)
    return exchange(jnp.broadcast_to(x[None], (count, *x.shape)), axes)


def shifted(x, axes, step):
    count = lax.axis_size(axes)
    return lax.ppermute(x, axes, [(i, (i + step) % count) for i in range(count)])


def along_z(x, step):
    n_zl, n_zh = lax.axis_size("zl"), lax.axis_size("zh")
    count = n_zl * n_zh
    at = [(z % n_zl) * n_zh + z // n_zl for z in range(count)]
    return lax.ppermute(x, ("zl", "zh"), [(at[z], at[(z + step) % count]) for z in range(count)])


def core_swap(x):
    return lax.ppermute(x, "co", [(0, 1), (1, 0)])


def block_of(i, core, n_zh):
    return (i // n_zh) * (2 * n_zh) + core * n_zh + i % n_zh


def wide(column, rows):
    return jnp.concatenate([column] * (rows // column.shape[1]), 1)


def norm_kernel(n_zh, place, mine, other, gain, shift, normed, stats):
    core = place[1]
    n_z, own_width, rows = mine.shape
    width = 2 * n_z * own_width

    def totals(i, carry):
        total, squares = carry
        for ref in (mine, other):
            x = ref[i].astype(F32)
            total = total + jnp.sum(x, 0, keepdims=True)
            squares = squares + jnp.sum(x * x, 0, keepdims=True)
        return total, squares

    zero = jnp.zeros((1, rows), F32)
    total, squares = lax.fori_loop(0, n_z, totals, (zero, zero))
    mean = total / width
    inv = lax.rsqrt(squares / width - mean * mean + EPSILON)
    stats[0:1, :] = mean
    stats[1:2, :] = inv
    for i in range(n_z):
        for ref, owner in ((mine, core), (other, 1 - core)):
            b = block_of(i, owner, n_zh)
            value = (ref[i].astype(F32) - mean) * inv * wide(gain[b], rows) + wide(shift[b], rows)
            normed[b] = value.astype(BF16)


def high_low(plain, cross):
    high_plain, high_cross = plain.astype(BF16).astype(F32), cross.astype(BF16).astype(F32)
    pad = jnp.zeros((EXTRA - 4, plain.shape[1]), F32)
    return jnp.concatenate(
        [high_plain, plain - high_plain, high_cross, cross - high_cross, pad], 0
    ).astype(BF16)


def part_kernel(n_zh, place, weight, d_embed, mine, other, gain, stats, keep, send):
    core = place[1]
    n_z, own_width, rows = mine.shape
    mean, inv = stats[0:1, :], stats[1:2, :]
    plain = cross = jnp.zeros((1, rows), F32)
    for i in range(n_z):
        for source, owner, out in ((mine, core, keep), (other, 1 - core, send)):
            b = block_of(i, owner, n_zh)
            part = lax.dot_general(
                weight[b], d_embed[...], (((1,), (1,)), ((), ())), preferred_element_type=F32
            ).astype(BF16)
            out[i, 0:own_width, :] = part
            scaled = part.astype(F32) * wide(gain[b], rows)
            xhat = (source[i].astype(F32) - mean) * inv
            plain = plain + jnp.sum(scaled, 0, keepdims=True)
            cross = cross + jnp.sum(scaled * xhat, 0, keepdims=True)
    tail = high_low(plain, cross)
    for i in range(n_z):
        keep[i, own_width:, :] = tail
        send[i, own_width:, :] = tail


def pair_kernel(n_zl, n_zh, place, keep, recv, *outs):
    n_z, own_width = keep.shape[0], keep.shape[1] - EXTRA
    tail = keep[0, own_width:, :].astype(F32) + recv[0, own_width:, :].astype(F32)
    tail = high_low(tail[0:1] + tail[1:2], tail[2:3] + tail[3:4])
    for k, out in enumerate(outs):
        target = lax.rem(place[0] + k, n_z)
        i = lax.rem(target, n_zl) * n_zh + target // n_zl
        pair = keep[i, 0:own_width, :].astype(F32) + recv[i, 0:own_width, :].astype(F32)
        out[0:own_width, :] = pair.astype(BF16)
        out[own_width:, :] = tail


def body(patches, gain, shift, proj_weight, llm_rank, embed_grad):
    rows, own_width = patches.shape
    width = gain.shape[0]
    out_cols = proj_weight.shape[1]
    n_y, n_x = lax.axis_size("y"), lax.axis_size("x")
    n_zl, n_zh = lax.axis_size("zl"), lax.axis_size("zh")
    n_z = n_zl * n_zh
    senders = n_y * n_x
    slice_rows = proj_weight.shape[0]
    most = embed_grad.shape[0] // senders
    blocks = width // own_width
    core, x_at = lax.axis_index("co"), lax.axis_index("x")
    place = jnp.stack([lax.axis_index("zh") * n_zl + lax.axis_index("zl"), core]).astype(jnp.int32)

    own_t = patches.T
    mine = copies(own_t, ("zl", "zh"))
    other = core_swap(mine)

    weight_rel = [proj_weight] + [shifted(proj_weight, "x", k) for k in range(1, n_x)]
    ordered = jnp.stack([weight_rel[-i % n_x] for i in range(n_x)] * 2)
    weight_x = lax.dynamic_slice_in_dim(ordered, lax.rem(n_x - x_at, n_x), n_x, 0)
    weight = lax.all_gather(weight_x.reshape(n_x * slice_rows, out_cols), "y", axis=0, tiled=True)

    embed_grad, mine = lax.optimization_barrier((embed_grad, mine))
    returned = exchange(embed_grad.reshape(senders, most, out_cols), ENC)

    gain_wide = jnp.broadcast_to(gain.reshape(blocks, own_width, 1), (blocks, own_width, 128))
    shift_wide = jnp.broadcast_to(shift.reshape(blocks, own_width, 1), (blocks, own_width, 128))
    normed, stats = pl.pallas_call(
        functools.partial(norm_kernel, n_zh),
        out_shape=(
            jax.ShapeDtypeStruct((blocks, own_width, rows), BF16),
            jax.ShapeDtypeStruct((8, rows), F32),
        ),
        in_specs=[SMEM] + [VMEM] * 4,
        out_specs=(VMEM,) * 2,
        compiler_params=PARAMS,
        name="norm",
    )(place, mine, other, gain_wide, shift_wide)
    mean, inv = stats[0], stats[1]
    normed = normed.reshape(width, rows)

    target = llm_rank[:, 0]
    owners = jnp.arange(senders, dtype=jnp.int32)
    hits = (target[:, None] == owners[None, :]).astype(jnp.int32)
    rank = jnp.sum((jnp.cumsum(hits, 0) - hits) * hits, 1)
    slot = target * most + rank
    d_embed = returned.reshape(senders * most, out_cols)[slot]

    grad_part = jnp.dot(normed, d_embed, preferred_element_type=F32).astype(BF16)
    grad_y = lax.psum_scatter(grad_part, "y", scatter_dimension=0, tiled=True)
    grad_y = grad_y.reshape(n_x, slice_rows, out_cols)

    def grad_block(step):
        return lax.dynamic_index_in_dim(grad_y, lax.rem(x_at + step, n_x), 0, keepdims=False)

    grad_weight = sum(
        [shifted(grad_block(k), "x", k).astype(F32) for k in range(1, n_x)],
        grad_block(0).astype(F32),
    )

    half_shape = jax.ShapeDtypeStruct((n_z, own_width + EXTRA, rows), BF16)
    keep, send = pl.pallas_call(
        functools.partial(part_kernel, n_zh),
        out_shape=(half_shape, half_shape),
        in_specs=[SMEM] + [VMEM] * 6,
        out_specs=(VMEM,) * 2,
        compiler_params=PARAMS,
        name="part",
    )(place, weight.reshape(blocks, own_width, out_cols), d_embed, mine, other, gain_wide, stats)
    recv = core_swap(send)

    weight_after, keep = lax.optimization_barrier((weight, keep))
    embed = lax.dot_general(
        normed, weight_after, (((0,), (0,)), ((), ())), preferred_element_type=F32
    ).astype(BF16)
    outgoing = jnp.zeros((senders * most, out_cols), BF16).at[slot].set(embed)
    embeds_recv = exchange(outgoing.reshape(senders, most, out_cols), ENC).reshape(
        senders * most, out_cols
    )

    pairs = pl.pallas_call(
        functools.partial(pair_kernel, n_zl, n_zh),
        out_shape=(jax.ShapeDtypeStruct((own_width + EXTRA, rows), BF16),) * n_z,
        in_specs=[SMEM] + [VMEM] * 2,
        out_specs=(VMEM,) * n_z,
        compiler_params=PARAMS,
        name="pair",
    )(place, keep, recv)
    columns = sum(
        [along_z(pairs[k], k).astype(F32) for k in range(1, n_z)], pairs[0].astype(F32)
    )
    dnormed = columns[:own_width]
    tail = columns[own_width:]
    plain = (tail[0] + tail[1]) / width
    cross = (tail[2] + tail[3]) / width

    column_start = lax.axis_index(COLS) * own_width
    gain_own = lax.dynamic_slice_in_dim(gain, column_start, own_width, 0)[:, None]
    xhat_own = (own_t.astype(F32) - mean) * inv
    hidden = (inv * (dnormed * gain_own - plain - xhat_own * cross)).astype(BF16).T
    sums = jnp.concatenate([jnp.sum(dnormed * xhat_own, 1), jnp.sum(dnormed, 1)])
    sums, embeds_recv = lax.optimization_barrier((sums, embeds_recv))
    sums = jnp.sum(copies(sums[None], ENC), (0, 1))
    return embeds_recv, hidden, grad_weight, sums[:own_width], sums[own_width:]


def solution(mesh):
    devices = mesh.devices
    split = Mesh(devices.reshape(8, 4, 4, 2, 2), ("y", "x", "zl", "co", "zh"))
    spec = P(ENC, COLS)
    in_specs = (spec, P(), P(), spec, P(ENC, None), spec)
    out_specs = (spec, spec, spec, P(COLS), P(COLS))
    return jax.shard_map(body, mesh=split, in_specs=in_specs, out_specs=out_specs, check_vma=False)
```

time: 240 us -> 202 us (0.84)
  starting transfers between devices: 118 us -> 78 us
  blocking collectives: 0 us -> 27.7 us
  waiting for transfers between devices: 59.3 us -> 46.8 us
  matrix products: 14.3 us -> 5.24 us
  Pallas kernels: 10.3 us -> 7.82 us
    ppermute x14 -> x7, starting transfers between devices: 56.8 us -> 26.2 us  [along_z(): lax.ppermute(x, ('zl', 'zh'), [(at[z], at[(z + step) % count]) for z in r...]
    all_to_all x0 -> x1, blocking collectives: none -> 27.7 us  [exchange(): return lax.all_to_all(x, axes, 0, 0, tiled=True)]
    ppermute x6, waiting for transfers between devices: 30.2 us -> 6.84 us  [shifted(): lax.ppermute(x, axes, [(i, (i + step) % count) for i in range(count)])]
    all_to_all x4 -> x3, waiting for transfers between devices: 16.4 us -> 28.6 us  [exchange(): return lax.all_to_all(x, axes, 0, 0, tiled=True)]
    all_to_all x4 -> x3, starting transfers between devices: 34.4 us -> 24.7 us  [exchange(): return lax.all_to_all(x, axes, 0, 0, tiled=True)]
    dot_general x5 -> x2, matrix products: 14.3 us -> 5.24 us  [the longest x1 4.18 us: body(): jnp.dot(normed, d_embed, preferred_element_type=F32).astype(BF16)]
    pallas_call x3, Pallas kernels: 10.3 us -> 7.82 us  [the longest x1 4.65 us: body(): pl.pallas_call(functools.partial(part_kernel, n_zh), out_shape=(half_shap...]
    ppermute x14 -> x7, waiting for transfers between devices: 11.7 us -> 10.3 us  [along_z(): lax.ppermute(x, ('zl', 'zh'), [(at[z], at[(z + step) % count]) for z in r...]
  transfers between devices with their start and end apart: 27 -> 20, of which waited for: 11 -> 9; matrix products, arithmetic and copies ran while one was open for 11% -> 9% of each run, Pallas kernels for 4% -> 4%
where the time goes in v2:
time: 202 us; the launch traced here: 200 us
  starting transfers between devices  78 us (39%)
  waiting for transfers between devices  46.8 us (23%)
  blocking collectives  27.7 us (14%)
  local copies, waits for them, and re-layouts  16.8 us (8%)
  between operations  14.6 us (7%)
  Pallas kernels  7.82 us (4%)
  matrix products  5.24 us (3%)
  other arithmetic  2.59 us (1%)
    all_to_all x3, waiting for transfers between devices, exchange(): return lax.all_to_all(x, axes, 0, 0, tiled=True)  28.6 us
    all_to_all x1, blocking collectives, exchange(): return lax.all_to_all(x, axes, 0, 0, tiled=True)  27.7 us
    ppermute x7, starting transfers between devices, along_z(): lax.ppermute(x, ('zl', 'zh'), [(at[z], at[(z + step) % count]) for z in r...  26.2 us
    all_to_all x3, starting transfers between devices, exchange(): return lax.all_to_all(x, axes, 0, 0, tiled=True)  24.7 us
    ppermute x6, starting transfers between devices, shifted(): lax.ppermute(x, axes, [(i, (i + step) % count) for i in range(count)])  23.2 us
    ppermute x7, waiting for transfers between devices, along_z(): lax.ppermute(x, ('zl', 'zh'), [(at[z], at[(z + step) % count]) for z in r...  10.3 us
    ppermute x6, waiting for transfers between devices, shifted(): lax.ppermute(x, axes, [(i, (i + step) % count) for i in range(count)])  6.84 us
    unnamed x30, local copies, waits for them, and re-layouts  4.89 us
  transfers between devices with their start and end apart: 20, of which 9 were waited for; matrix products, arithmetic and copies ran while one was open for 9% of the time, Pallas kernels for 4%

profile of v2, /device:TPU:6, one launch (start us, length us, event | category | flops | bytes accessed | tf_op | source)
XLA Modules:
  0.0 199.5 jit_solution(10052349296917607833)
XLA Ops:
  7.2 2.7 %collective-permute-start = (bf16[100,512]{1,0:T(8,128)(2,1)}, bf16[100,512]{1,0:T(8,128)(2,1)S(1)}, u32[]{:S(2)}, u32[]{:S(2)}) collective-permute-start(bf16[100,512]{1,0:T(8,128)(2,1)} %param.9), channel_id=1, source_target_pairs={{0,48},{16,0},{32,16},{48,32},{1,49},{17,1},{33,17},{49,33},{2,50}... | collective-permute-start | bytes 307208 | tf_op jit(solution)/shard_map/ppermute | solution.py:33
  10.0 8.4 %collective-permute-start.1 = (bf16[100,512]{1,0:T(8,128)(2,1)}, bf16[100,512]{1,0:T(8,128)(2,1)S(1)}, u32[]{:S(2)}, u32[]{:S(2)}) collective-permute-start(bf16[100,512]{1,0:T(8,128)(2,1)} %param.9), channel_id=1, source_target_pairs={{0,32},{16,48},{32,0},{48,16},{1,33},{17,49},{33,1},{49,17},{2,34}... | collective-permute-start | bytes 307208 | tf_op jit(solution)/shard_map/ppermute | solution.py:33
  18.4 1.9 collective-permute-start.2
  21.3 3.9 %collective-permute-done.2 = bf16[100,512]{1,0:T(8,128)(2,1)S(1)} collective-permute-done((bf16[100,512]{1,0:T(8,128)(2,1)}, bf16[100,512]{1,0:T(8,128)(2,1)S(1)}, u32[]{:S(2)}, u32[]{:S(2)}) %collective-permute-start.2) | collective-permute-done | bytes 102432 | tf_op jit(solution)/shard_map/ppermute | solution.py:33
  27.1 27.7 %all_to_all.20.mine = bf16[8,200,256]{2,1,0:T(8,128)(2,1)S(1)} all-to-all(bf16[8,200,256]{2,1,0:T(8,128)(2,1)S(1)} %broadcast_in_dim.14), channel_id=1, replica_groups=mesh['y'=8,'x'=4,'zl'=4,'co'=2,'zh'=2] {'zl','zh'}, dimensions={0} | all-to-all | bytes 1638400 | tf_op jit(solution)/shard_map/all_to_all | solution.py:23
  54.9 10.0 %all-to-all-start.1 = ((bf16[32,24,512]{2,1,0:T(8,128)(2,1)}), bf16[32,24,512]{2,1,0:T(8,128)(2,1)}, u32[]{:S(2)}, u32[]{:S(2)}) async-start(bf16[32,24,512]{2,1,0:T(8,128)(2,1)} %bitcast.8), calls=%async_computation.1 | async-start | bytes 1572864 | tf_op jit(solution)/shard_map/all_to_all | solution.py:23
  64.9 1.9 collective-permute-start.3
  69.6 1.7 broadcast_in_dim.18.shift
  71.3 2.4 %norm.1 = (bf16[16,200,256]{2,1,0:T(8,128)(2,1)S(1)}, f32[8,256]{1,0:T(8,128)S(1)}) custom-call(s32[2]{0:T(128)S(1)} %pad_add_fusion.place, bf16[8,200,256]{2,1,0:T(8,128)(2,1)S(1)} %all_to_all.20.mine, bf16[8,200,256]{2,1,0:T(8,128)(2,1)S(1)} %collective-permute-done.3.other, f32[16,200,128]{2,1,0:T(8,128)S(1)} %broadcast_in_dim.16.gain, ...), custom_call_target="tpu_custom_call" | custom-call | tf_op jit(solution)/shard_map/norm/pallas_call | solution.py:151
  74.9 20.2 %all-to-all-done.1 = bf16[32,24,512]{2,1,0:T(8,128)(2,1)} async-done(((bf16[32,24,512]{2,1,0:T(8,128)(2,1)}), bf16[32,24,512]{2,1,0:T(8,128)(2,1)}, u32[]{:S(2)}, u32[]{:S(2)}) %all-to-all-start.1) | async-done | bytes 786464 | tf_op jit(solution)/shard_map/all_to_all | solution.py:23
  95.1 2.4 %gather_fusion = bf16[256,512]{1,0:T(8,128)(2,1)S(1)} fusion(bf16[768,512]{1,0:T(8,128)(2,1)} %bitcast.9, s32[1024]{0:T(1024)S(1)} %pad_clamp_fusion), kind=kCustom, calls=%fused_computation | custom fusion | bytes 525312 | tf_op jit(solution)/shard_map/gather | solution.py:170
  97.6 4.2 %convolution_convert_fusion = bf16[3200,512]{1,0:T(8,128)(2,1)} fusion(bf16[3200,256]{1,0:T(8,128)(2,1)} %bitcast.65, bf16[256,512]{1,0:T(8,128)(2,1)S(1)} %gather_fusion), kind=kOutput, calls=%fused_computation.2 | convolution fusion | flops 840499200 | bytes 5177344 | tf_op jit(solution)/shard_map/dot_general | solution.py:172
  101.8 4.7 %part.1 = (bf16[8,208,256]{2,1,0:T(8,128)(2,1)S(1)}, bf16[8,208,256]{2,1,0:T(8,128)(2,1)}) custom-call(s32[2]{0:T(128)S(1)} %pad_add_fusion.place, bf16[16,200,512]{2,1,0:T(8,128)(2,1)} %bitcast.67, bf16[256,512]{1,0:T(8,128)(2,1)S(1)} %gather_fusion, bf16[8,200,256]{2,1,0:T(8,128)(2,1)S(1)} %all_to_all.20.mine, ...), custom_call_target="tpu_custom_call" | custom-call | tf_op jit(solution)/shard_map/part/pallas_call | solution.py:185
  107.4 1.9 collective-permute-start.4
  110.4 2.7 %scatter_custom_fusion = bf16[768,512]{1,0:T(8,128)(2,1)} fusion(s32[256]{0:T(256)} %bitcast.77, bf16[256,512]{1,0:T(8,128)(2,1)S(1)} %convolution_convert_fusion.1, bf16[]{:T(256)} %constant.62.clone.1), kind=kCustom, calls=%fused_computation.4 | custom fusion | bytes 786944 | tf_op jit(solution)/shard_map/scatter | solution.py:199
  113.2 5.0 %all-to-all-start.2 = ((bf16[32,24,512]{2,1,0:T(8,128)(2,1)}), bf16[32,24,512]{2,1,0:T(8,128)(2,1)S(1)}, u32[]{:S(2)}, u32[]{:S(2)}) async-start(bf16[32,24,512]{2,1,0:T(8,128)(2,1)} %bitcast.18), calls=%async_computation.2 | async-start | bytes 1572864 | tf_op jit(solution)/shard_map/all_to_all | solution.py:23
  118.9 2.9 %collective-permute-start.11 = (bf16[208,256]{1,0:T(8,128)(2,1)S(1)}, bf16[208,256]{1,0:T(8,128)(2,1)S(1)}, u32[]{:S(2)}, u32[]{:S(2)}) collective-permute-start(bf16[208,256]{1,0:T(8,128)(2,1)S(1)} %get-tuple-element.36), channel_id=1, source_target_pairs={{0,13},{4,0},{8,4},{12,8},{1,12},{5,1},{9,5},{13,9},{2,15},{6,2},{... | collective-permute-start | bytes 319496 | tf_op jit(solution)/shard_map/ppermute | solution.py:40
  121.8 3.3 %collective-permute-start.10 = (bf16[208,256]{1,0:T(8,128)(2,1)S(1)}, bf16[208,256]{1,0:T(8,128)(2,1)S(1)}, u32[]{:S(2)}, u32[]{:S(2)}) collective-permute-start(bf16[208,256]{1,0:T(8,128)(2,1)S(1)} %get-tuple-element.35), channel_id=1, source_target_pairs={{0,9},{4,13},{8,0},{12,4},{1,8},{5,12},{9,1},{13,5},{2,11},{6,15},... | collective-permute-start | bytes 319496 | tf_op jit(solution)/shard_map/ppermute | solution.py:40
  126.0 5.7 %collective-permute-start.9 = (bf16[208,256]{1,0:T(8,128)(2,1)S(1)}, bf16[208,256]{1,0:T(8,128)(2,1)S(1)}, u32[]{:S(2)}, u32[]{:S(2)}) collective-permute-start(bf16[208,256]{1,0:T(8,128)(2,1)S(1)} %get-tuple-element.34), channel_id=1, source_target_pairs={{0,5},{4,9},{8,13},{12,0},{1,4},{5,8},{9,12},{13,1},{2,7},{6,11},{... | collective-permute-start | bytes 319496 | tf_op jit(solution)/shard_map/ppermute | solution.py:40
  131.7 4.3 %collective-permute-start.8 = (bf16[208,256]{1,0:T(8,128)(2,1)S(1)}, bf16[208,256]{1,0:T(8,128)(2,1)S(1)}, u32[]{:S(2)}, u32[]{:S(2)}) collective-permute-start(bf16[208,256]{1,0:T(8,128)(2,1)S(1)} %get-tuple-element.33), channel_id=1, source_target_pairs={{0,1},{4,5},{8,9},{12,13},{1,0},{5,4},{9,8},{13,12},{2,3},{6,7},{1... | collective-permute-start | bytes 319496 | tf_op jit(solution)/shard_map/ppermute | solution.py:40
  136.0 4.1 %collective-permute-start.7 = (bf16[208,256]{1,0:T(8,128)(2,1)S(1)}, bf16[208,256]{1,0:T(8,128)(2,1)S(1)}, u32[]{:S(2)}, u32[]{:S(2)}) collective-permute-start(bf16[208,256]{1,0:T(8,128)(2,1)S(1)} %get-tuple-element.32), channel_id=1, source_target_pairs={{0,12},{4,1},{8,5},{12,9},{1,13},{5,0},{9,4},{13,8},{2,14},{6,3},{... | collective-permute-start | bytes 319496 | tf_op jit(solution)/shard_map/ppermute | solution.py:40
  140.1 4.0 %collective-permute-start.6 = (bf16[208,256]{1,0:T(8,128)(2,1)S(1)}, bf16[208,256]{1,0:T(8,128)(2,1)S(1)}, u32[]{:S(2)}, u32[]{:S(2)}) collective-permute-start(bf16[208,256]{1,0:T(8,128)(2,1)S(1)} %get-tuple-element.31), channel_id=1, source_target_pairs={{0,8},{4,12},{8,1},{12,5},{1,9},{5,13},{9,0},{13,4},{2,10},{6,14},... | collective-permute-start | bytes 319496 | tf_op jit(solution)/shard_map/ppermute | solution.py:40
  144.1 1.9 collective-permute-start.5
  146.3 4.5 %collective-permute-done.7 = bf16[208,256]{1,0:T(8,128)(2,1)S(1)} collective-permute-done((bf16[208,256]{1,0:T(8,128)(2,1)S(1)}, bf16[208,256]{1,0:T(8,128)(2,1)S(1)}, u32[]{:S(2)}, u32[]{:S(2)}) %collective-permute-start.7) | collective-permute-done | bytes 106528 | tf_op jit(solution)/shard_map/ppermute | solution.py:40
  150.9 4.1 %collective-permute-done.6 = bf16[208,256]{1,0:T(8,128)(2,1)S(1)} collective-permute-done((bf16[208,256]{1,0:T(8,128)(2,1)S(1)}, bf16[208,256]{1,0:T(8,128)(2,1)S(1)}, u32[]{:S(2)}, u32[]{:S(2)}) %collective-permute-start.6) | collective-permute-done | bytes 106528 | tf_op jit(solution)/shard_map/ppermute | solution.py:40
  154.9 1.4 collective-permute-done.5
  158.0 9.8 %all-to-all-start.3 = ((f32[32,1,400]{2,1,0:T(1,128)}), f32[32,1,400]{2,1,0:T(1,128)S(1)}, u32[]{:S(2)}, u32[]{:S(2)}) async-start(f32[32,1,400]{2,1,0:T(1,128)} %broadcast_in_dim.40), calls=%async_computation.4 | async-start | bytes 131072 | tf_op jit(solution)/shard_map/all_to_all | solution.py:23
  167.8 8.4 %all-to-all-done.3 = f32[32,1,400]{2,1,0:T(1,128)S(1)} async-done(((f32[32,1,400]{2,1,0:T(1,128)}), f32[32,1,400]{2,1,0:T(1,128)S(1)}, u32[]{:S(2)}, u32[]{:S(2)}) %all-to-all-start.3) | async-done | bytes 51232 | tf_op jit(solution)/shard_map/all_to_all | solution.py:23
  177.4 2.4 %collective-permute-start.14 = (bf16[100,512]{1,0:T(8,128)(2,1)S(1)}, bf16[100,512]{1,0:T(8,128)(2,1)S(1)}, u32[]{:S(2)}, u32[]{:S(2)}) collective-permute-start(bf16[100,512]{1,0:T(8,128)(2,1)S(1)} %get-tuple-element.44), channel_id=1, source_target_pairs={{0,48},{16,0},{32,16},{48,32},{1,49},{17,1},{33,17},{49,33},{2,50}... | collective-permute-start | bytes 307208 | tf_op jit(solution)/shard_map/ppermute | solution.py:33
  179.8 4.7 %collective-permute-start.13 = (bf16[100,512]{1,0:T(8,128)(2,1)S(1)}, bf16[100,512]{1,0:T(8,128)(2,1)S(1)}, u32[]{:S(2)}, u32[]{:S(2)}) collective-permute-start(bf16[100,512]{1,0:T(8,128)(2,1)S(1)} %get-tuple-element.45), channel_id=1, source_target_pairs={{0,32},{16,48},{32,0},{48,16},{1,33},{17,49},{33,1},{49,17},{2,34}... | collective-permute-start | bytes 307208 | tf_op jit(solution)/shard_map/ppermute | solution.py:33
  184.5 3.0 %collective-permute-start.12 = (bf16[100,512]{1,0:T(8,128)(2,1)S(1)}, bf16[100,512]{1,0:T(8,128)(2,1)S(1)}, u32[]{:S(2)}, u32[]{:S(2)}) collective-permute-start(bf16[100,512]{1,0:T(8,128)(2,1)S(1)} %get-tuple-element.43), channel_id=1, source_target_pairs={{0,16},{16,32},{32,48},{48,0},{1,17},{17,33},{33,49},{49,1},{2,18}... | collective-permute-start | bytes 307208 | tf_op jit(solution)/shard_map/ppermute | solution.py:33
  188.1 2.9 %collective-permute-done.12 = bf16[100,512]{1,0:T(8,128)(2,1)S(1)} collective-permute-done((bf16[100,512]{1,0:T(8,128)(2,1)S(1)}, bf16[100,512]{1,0:T(8,128)(2,1)S(1)}, u32[]{:S(2)}, u32[]{:S(2)}) %collective-permute-start.12) | collective-permute-done | bytes 102432 | tf_op jit(solution)/shard_map/ppermute | solution.py:33
  (77 shorter events, 15.8 us)
Async XLA Ops:
  7.2 94.6 %all-gather.2.cloned.1.call-start = ((), (), s32[]{:S(2)}) async-start(), calls=%async_computation.5 | async-start | bytes 3686400 | tf_op jit(solution)/shard_map/all_gather | solution.py:144
  7.2 14.0 %collective-permute-start = (bf16[100,512]{1,0:T(8,128)(2,1)}, bf16[100,512]{1,0:T(8,128)(2,1)S(1)}, u32[]{:S(2)}, u32[]{:S(2)}) collective-permute-start(bf16[100,512]{1,0:T(8,128)(2,1)} %param.9), channel_id=1, source_target_pairs={{0,48},{16,0},{32,16},{48,32},{1,49},{17,1},{33,17},{49,33},{2,50}... | collective-permute-start | bytes 307208 | tf_op jit(solution)/shard_map/ppermute | solution.py:33
  10.0 11.3 %collective-permute-start.1 = (bf16[100,512]{1,0:T(8,128)(2,1)}, bf16[100,512]{1,0:T(8,128)(2,1)S(1)}, u32[]{:S(2)}, u32[]{:S(2)}) collective-permute-start(bf16[100,512]{1,0:T(8,128)(2,1)} %param.9), channel_id=1, source_target_pairs={{0,32},{16,48},{32,0},{48,16},{1,33},{17,49},{33,1},{49,17},{2,34}... | collective-permute-start | bytes 307208 | tf_op jit(solution)/shard_map/ppermute | solution.py:33
  18.4 6.8 %collective-permute-start.2 = (bf16[100,512]{1,0:T(8,128)(2,1)}, bf16[100,512]{1,0:T(8,128)(2,1)S(1)}, u32[]{:S(2)}, u32[]{:S(2)}) collective-permute-start(bf16[100,512]{1,0:T(8,128)(2,1)} %param.9), channel_id=1, source_target_pairs={{0,16},{16,32},{32,48},{48,0},{1,17},{17,33},{33,49},{49,1},{2,18}... | collective-permute-start | bytes 307208 | tf_op jit(solution)/shard_map/ppermute | solution.py:33
  21.2 5.8 %copy-start.5 = (bf16[256,200]{0,1:T(8,128)(2,1)S(1)}, bf16[256,200]{0,1:T(8,128)(2,1)}, u32[]{:S(2)}) copy-start(bf16[256,200]{0,1:T(8,128)(2,1)} %param.6) | copy-start | bytes 307204
  27.1 39.8 %copy-start.9 = (s32[256,1]{0,1:T(1,128)S(1)}, s32[256,1]{0,1:T(1,128)}, u32[]{:S(2)}) copy-start(s32[256,1]{0,1:T(1,128)} %param.10) | copy-start | bytes 3076
  27.1 40.6 %copy-start.7 = (f32[3200]{0:T(1024)S(1)}, f32[3200]{0:T(1024)}, u32[]{:S(2)}) copy-start(f32[3200]{0:T(1024)} %param.7) | copy-start | bytes 38404
  27.1 40.7 %copy-start.8 = (f32[3200]{0:T(1024)S(1)}, f32[3200]{0:T(1024)}, u32[]{:S(2)}) copy-start(f32[3200]{0:T(1024)} %param.8) | copy-start | bytes 38404
  54.9 40.3 %all-to-all-start.1 = ((bf16[32,24,512]{2,1,0:T(8,128)(2,1)}), bf16[32,24,512]{2,1,0:T(8,128)(2,1)}, u32[]{:S(2)}, u32[]{:S(2)}) async-start(bf16[32,24,512]{2,1,0:T(8,128)(2,1)} %bitcast.8), calls=%async_computation.1 | async-start | bytes 1572864 | tf_op jit(solution)/shard_map/all_to_all | solution.py:23
  64.9 111.4 %reduce-scatter.2.cloned.1.call-start = ((), (), s32[]{:S(2)}) async-start(), calls=%async_computation.6 | async-start | bytes 3686400 | tf_op jit(solution)/shard_map/reduce_scatter | solution.py:173
  64.9 4.2 %collective-permute-start.3 = (bf16[8,200,256]{2,1,0:T(8,128)(2,1)S(1)}, bf16[8,200,256]{2,1,0:T(8,128)(2,1)S(1)}, u32[]{:S(2)}, u32[]{:S(2)}) collective-permute-start(bf16[8,200,256]{2,1,0:T(8,128)(2,1)S(1)} %all_to_all.20.mine), channel_id=1, source_target_pairs={{0,2},{2,0},{1,3},{3,1},{4,6},{6,4},{5,7},{7,5},{8,10},{10,8},{9,1... | collective-permute-start | bytes 2457608 | tf_op jit(solution)/shard_map/ppermute | solution.py:44
  68.1 3.2 %copy-start.10 = (s32[256,1]{0,1:T(1,128)}, s32[256,1]{0,1:T(1,128)S(1)}, u32[]{:S(2)}) copy-start(s32[256,1]{0,1:T(1,128)S(1)} %compare_select_fusion) | copy-start | bytes 3076
  73.8 1.2 copy-start
  101.8 7.5 %copy-start.1 = (bf16[16,200,256]{2,1,0:T(8,128)(2,1)S(1)}, bf16[16,200,256]{2,1,0:T(8,128)(2,1)}, u32[]{:S(2)}) copy-start(bf16[16,200,256]{2,1,0:T(8,128)(2,1)} %copy-done) | copy-start | bytes 4915204
  101.8 7.5 %copy-start.4 = (bf16[3200,512]{1,0:T(8,128)(2,1)S(1)}, bf16[3200,512]{1,0:T(8,128)(2,1)}, u32[]{:S(2)}) copy-start(bf16[3200,512]{1,0:T(8,128)(2,1)} %all-gather.2.cloned.1.call-done) | copy-start | bytes 9830404
  106.5 0.9 copy-start.2
  107.4 10.7 %collective-permute-start.4 = (bf16[8,208,256]{2,1,0:T(8,128)(2,1)}, bf16[8,208,256]{2,1,0:T(8,128)(2,1)S(1)}, u32[]{:S(2)}, u32[]{:S(2)}) collective-permute-start(bf16[8,208,256]{2,1,0:T(8,128)(2,1)} %get-tuple-element.28), channel_id=1, source_target_pairs={{0,2},{2,0},{1,3},{3,1},{4,6},{6,4},{5,7},{7,5},{8,10},{10,8},{9,1... | collective-permute-start | bytes 2555912 | tf_op jit(solution)/shard_map/ppermute | solution.py:44
  110.4 7.7 %copy-start.3 = (bf16[8,208,256]{2,1,0:T(8,128)(2,1)S(1)}, bf16[8,208,256]{2,1,0:T(8,128)(2,1)}, u32[]{:S(2)}) copy-start(bf16[8,208,256]{2,1,0:T(8,128)(2,1)} %copy-done.2) | copy-start | bytes 2555908
  113.2 44.2 %all-to-all-start.2 = ((bf16[32,24,512]{2,1,0:T(8,128)(2,1)}), bf16[32,24,512]{2,1,0:T(8,128)(2,1)S(1)}, u32[]{:S(2)}, u32[]{:S(2)}) async-start(bf16[32,24,512]{2,1,0:T(8,128)(2,1)} %bitcast.18), calls=%async_computation.2 | async-start | bytes 1572864 | tf_op jit(solution)/shard_map/all_to_all | solution.py:23
  118.1 38.3 %copy-start.6 = (bf16[256,200]{0,1:T(8,128)(2,1)S(1)}, bf16[256,200]{0,1:T(8,128)(2,1)}, u32[]{:S(2)}) copy-start(bf16[256,200]{0,1:T(8,128)(2,1)} %param.6) | copy-start | bytes 307204
  118.9 21.2 %collective-permute-start.11 = (bf16[208,256]{1,0:T(8,128)(2,1)S(1)}, bf16[208,256]{1,0:T(8,128)(2,1)S(1)}, u32[]{:S(2)}, u32[]{:S(2)}) collective-permute-start(bf16[208,256]{1,0:T(8,128)(2,1)S(1)} %get-tuple-element.36), channel_id=1, source_target_pairs={{0,13},{4,0},{8,4},{12,8},{1,12},{5,1},{9,5},{13,9},{2,15},{6,2},{... | collective-permute-start | bytes 319496 | tf_op jit(solution)/shard_map/ppermute | solution.py:40
  121.8 22.3 %collective-permute-start.10 = (bf16[208,256]{1,0:T(8,128)(2,1)S(1)}, bf16[208,256]{1,0:T(8,128)(2,1)S(1)}, u32[]{:S(2)}, u32[]{:S(2)}) collective-permute-start(bf16[208,256]{1,0:T(8,128)(2,1)S(1)} %get-tuple-element.35), channel_id=1, source_target_pairs={{0,9},{4,13},{8,0},{12,4},{1,8},{5,12},{9,1},{13,5},{2,11},{6,15},... | collective-permute-start | bytes 319496 | tf_op jit(solution)/shard_map/ppermute | solution.py:40
  126.0 20.1 %collective-permute-start.9 = (bf16[208,256]{1,0:T(8,128)(2,1)S(1)}, bf16[208,256]{1,0:T(8,128)(2,1)S(1)}, u32[]{:S(2)}, u32[]{:S(2)}) collective-permute-start(bf16[208,256]{1,0:T(8,128)(2,1)S(1)} %get-tuple-element.34), channel_id=1, source_target_pairs={{0,5},{4,9},{8,13},{12,0},{1,4},{5,8},{9,12},{13,1},{2,7},{6,11},{... | collective-permute-start | bytes 319496 | tf_op jit(solution)/shard_map/ppermute | solution.py:40
  131.7 14.6 %collective-permute-start.8 = (bf16[208,256]{1,0:T(8,128)(2,1)S(1)}, bf16[208,256]{1,0:T(8,128)(2,1)S(1)}, u32[]{:S(2)}, u32[]{:S(2)}) collective-permute-start(bf16[208,256]{1,0:T(8,128)(2,1)S(1)} %get-tuple-element.33), channel_id=1, source_target_pairs={{0,1},{4,5},{8,9},{12,13},{1,0},{5,4},{9,8},{13,12},{2,3},{6,7},{1... | collective-permute-start | bytes 319496 | tf_op jit(solution)/shard_map/ppermute | solution.py:40
  136.0 14.8 %collective-permute-start.7 = (bf16[208,256]{1,0:T(8,128)(2,1)S(1)}, bf16[208,256]{1,0:T(8,128)(2,1)S(1)}, u32[]{:S(2)}, u32[]{:S(2)}) collective-permute-start(bf16[208,256]{1,0:T(8,128)(2,1)S(1)} %get-tuple-element.32), channel_id=1, source_target_pairs={{0,12},{4,1},{8,5},{12,9},{1,13},{5,0},{9,4},{13,8},{2,14},{6,3},{... | collective-permute-start | bytes 319496 | tf_op jit(solution)/shard_map/ppermute | solution.py:40
  140.1 14.8 %collective-permute-start.6 = (bf16[208,256]{1,0:T(8,128)(2,1)S(1)}, bf16[208,256]{1,0:T(8,128)(2,1)S(1)}, u32[]{:S(2)}, u32[]{:S(2)}) collective-permute-start(bf16[208,256]{1,0:T(8,128)(2,1)S(1)} %get-tuple-element.31), channel_id=1, source_target_pairs={{0,8},{4,12},{8,1},{12,5},{1,9},{5,13},{9,0},{13,4},{2,10},{6,14},... | collective-permute-start | bytes 319496 | tf_op jit(solution)/shard_map/ppermute | solution.py:40
  144.1 12.2 %collective-permute-start.5 = (bf16[208,256]{1,0:T(8,128)(2,1)S(1)}, bf16[208,256]{1,0:T(8,128)(2,1)S(1)}, u32[]{:S(2)}, u32[]{:S(2)}) collective-permute-start(bf16[208,256]{1,0:T(8,128)(2,1)S(1)} %get-tuple-element.30), channel_id=1, source_target_pairs={{0,4},{4,8},{8,12},{12,1},{1,5},{5,9},{9,13},{13,0},{2,6},{6,10},{... | collective-permute-start | bytes 319496 | tf_op jit(solution)/shard_map/ppermute | solution.py:40
  158.0 18.2 %all-to-all-start.3 = ((f32[32,1,400]{2,1,0:T(1,128)}), f32[32,1,400]{2,1,0:T(1,128)S(1)}, u32[]{:S(2)}, u32[]{:S(2)}) async-start(f32[32,1,400]{2,1,0:T(1,128)} %broadcast_in_dim.40), calls=%async_computation.4 | async-start | bytes 131072 | tf_op jit(solution)/shard_map/all_to_all | solution.py:23
  177.4 10.8 %collective-permute-start.14 = (bf16[100,512]{1,0:T(8,128)(2,1)S(1)}, bf16[100,512]{1,0:T(8,128)(2,1)S(1)}, u32[]{:S(2)}, u32[]{:S(2)}) collective-permute-start(bf16[100,512]{1,0:T(8,128)(2,1)S(1)} %get-tuple-element.44), channel_id=1, source_target_pairs={{0,48},{16,0},{32,16},{48,32},{1,49},{17,1},{33,17},{49,33},{2,50}... | collective-permute-start | bytes 307208 | tf_op jit(solution)/shard_map/ppermute | solution.py:33
  179.8 8.4 %collective-permute-start.13 = (bf16[100,512]{1,0:T(8,128)(2,1)S(1)}, bf16[100,512]{1,0:T(8,128)(2,1)S(1)}, u32[]{:S(2)}, u32[]{:S(2)}) collective-permute-start(bf16[100,512]{1,0:T(8,128)(2,1)S(1)} %get-tuple-element.45), channel_id=1, source_target_pairs={{0,32},{16,48},{32,0},{48,16},{1,33},{17,49},{33,1},{49,17},{2,34}... | collective-permute-start | bytes 307208 | tf_op jit(solution)/shard_map/ppermute | solution.py:33
  184.5 6.6 %collective-permute-start.12 = (bf16[100,512]{1,0:T(8,128)(2,1)S(1)}, bf16[100,512]{1,0:T(8,128)(2,1)S(1)}, u32[]{:S(2)}, u32[]{:S(2)}) collective-permute-start(bf16[100,512]{1,0:T(8,128)(2,1)S(1)} %get-tuple-element.43), channel_id=1, source_target_pairs={{0,16},{16,32},{32,48},{48,0},{1,17},{17,33},{33,49},{49,1},{2,18}... | collective-permute-start | bytes 307208 | tf_op jit(solution)/shard_map/ppermute | solution.py:33
Sparse Core Ops, SparseCore 0:
  27.2 65.0 all-gather.1
  101.9 59.1 reduce-scatter.1

commit v3 on v2

v3 whole, which is shorter than its diff:
```python
import functools

import jax
import jax.numpy as jnp
from jax import lax
from jax.experimental import pallas as pl
from jax.experimental.pallas import tpu as pltpu
from jax.sharding import Mesh
from jax.sharding import PartitionSpec as P

ENC = ("y", "x")
COLS = ("zl", "co", "zh")
ZED = ("zh", "zl")
EPSILON = 1e-05
F32 = jnp.float32
BF16 = jnp.bfloat16
VMEM = pl.BlockSpec(memory_space=pltpu.VMEM)
SMEM = pl.BlockSpec(memory_space=pltpu.SMEM)
PARAMS = pltpu.CompilerParams(vmem_limit_bytes=48 * 1024 * 1024)
EXTRA = 8


def exchange(x, axes):
    return lax.all_to_all(x, axes, 0, 0, tiled=True)


def copies(x, axes):
    count = lax.axis_size(axes)
    return exchange(jnp.broadcast_to(x[None], (count, *x.shape)), axes)


def shifted(x, axes, step):
    count = lax.axis_size(axes)
    return lax.ppermute(x, axes, [(i, (i + step) % count) for i in range(count)])


def core_swap(x):
    return lax.ppermute(x, "co", [(0, 1), (1, 0)])


def block_of(z, core, n_zl, n_zh):
    return (z % n_zl) * (2 * n_zh) + core * n_zh + z // n_zl


def wide(column, rows):
    return jnp.concatenate([column] * (rows // column.shape[1]), 1)


def norm_kernel(n_zl, n_zh, core_at, mine, other, gain, shift, normed, stats):
    core = core_at[0]
    n_z, own_width, rows = mine.shape
    width = 2 * n_z * own_width

    def totals(i, carry):
        total, squares = carry
        for ref in (mine, other):
            x = ref[i].astype(F32)
            total = total + jnp.sum(x, 0, keepdims=True)
            squares = squares + jnp.sum(x * x, 0, keepdims=True)
        return total, squares

    zero = jnp.zeros((1, rows), F32)
    total, squares = lax.fori_loop(0, n_z, totals, (zero, zero))
    mean = total / width
    inv = lax.rsqrt(squares / width - mean * mean + EPSILON)
    stats[0:1, :] = mean
    stats[1:2, :] = inv
    for i in range(n_z):
        for ref, owner in ((mine, core), (other, 1 - core)):
            b = block_of(i, owner, n_zl, n_zh)
            value = (ref[i].astype(F32) - mean) * inv * wide(gain[b], rows) + wide(shift[b], rows)
            normed[b] = value.astype(BF16)


def high_low(plain, cross):
    high_plain, high_cross = plain.astype(BF16).astype(F32), cross.astype(BF16).astype(F32)
    pad = jnp.zeros((EXTRA - 4, plain.shape[1]), F32)
    return jnp.concatenate(
        [high_plain, plain - high_plain, high_cross, cross - high_cross, pad], 0
    ).astype(BF16)


def part_kernel(n_zl, n_zh, core_at, weight_a, weight_b, d_embed, mine, other, gain, stats, keep, send):
    core = core_at[0]
    n_z, own_width, rows = mine.shape
    mean, inv = stats[0:1, :], stats[1:2, :]
    plain = cross = jnp.zeros((1, rows), F32)
    for i in range(n_z):
        for source, owner, out in ((mine, core, keep), (other, 1 - core, send)):
            b = block_of(i, owner, n_zl, n_zh)
            part = sum(
                lax.dot_general(
                    weight[b], d_embed[h], (((1,), (1,)), ((), ())), preferred_element_type=F32
                )
                for h, weight in enumerate((weight_a, weight_b))
            ).astype(BF16)
            out[i, 0:own_width, :] = part
            scaled = part.astype(F32) * wide(gain[b], rows)
            xhat = (source[i].astype(F32) - mean) * inv
            plain = plain + jnp.sum(scaled, 0, keepdims=True)
            cross = cross + jnp.sum(scaled * xhat, 0, keepdims=True)
    tail = high_low(plain, cross)
    for i in range(n_z):
        keep[i, own_width:, :] = tail
        send[i, own_width:, :] = tail


def pair_kernel(keep, recv, out):
    n_z, own_width = keep.shape[0], keep.shape[1] - EXTRA
    tail = keep[0, own_width:, :].astype(F32) + recv[0, own_width:, :].astype(F32)
    tail = high_low(tail[0:1] + tail[1:2], tail[2:3] + tail[3:4])
    for i in range(n_z):
        pair = keep[i, 0:own_width, :].astype(F32) + recv[i, 0:own_width, :].astype(F32)
        out[i, 0:own_width, :] = pair.astype(BF16)
        out[i, own_width:, :] = tail


def body(patches, gain, shift, proj_weight, llm_rank, embed_grad):
    rows, own_width = patches.shape
    width = gain.shape[0]
    out_cols = proj_weight.shape[1]
    n_y, n_x = lax.axis_size("y"), lax.axis_size("x")
    n_zl, n_zh = lax.axis_size("zl"), lax.axis_size("zh")
    n_z = n_zl * n_zh
    senders = n_y * n_x
    slice_rows = proj_weight.shape[0]
    most = embed_grad.shape[0] // senders
    blocks = width // own_width
    core, x_at = lax.axis_index("co"), lax.axis_index("x")
    core_at = core.astype(jnp.int32).reshape(1)
    half = out_cols // 2

    weight_rel = [proj_weight] + [shifted(proj_weight, "x", k) for k in range(1, n_x)]
    ordered = jnp.stack([weight_rel[-i % n_x] for i in range(n_x)] * 2)
    weight_x = lax.dynamic_slice_in_dim(ordered, lax.rem(n_x - x_at, n_x), n_x, 0)
    weight_x = weight_x.reshape(n_x * slice_rows, out_cols)
    weights = [
        lax.all_gather(weight_x[:, h * half : (h + 1) * half], "y", axis=0, tiled=True)
        for h in range(2)
    ]

    returned = exchange(embed_grad.reshape(senders, most, out_cols), ENC)
    own_t = patches.T
    own_t, _ = lax.optimization_barrier((own_t, weight_x))
    mine = lax.all_gather(own_t, ZED, axis=0)
    other = core_swap(mine)

    gain_wide = jnp.broadcast_to(gain.reshape(blocks, own_width, 1), (blocks, own_width, 128))
    shift_wide = jnp.broadcast_to(shift.reshape(blocks, own_width, 1), (blocks, own_width, 128))
    normed, stats = pl.pallas_call(
        functools.partial(norm_kernel, n_zl, n_zh),
        out_shape=(
            jax.ShapeDtypeStruct((blocks, own_width, rows), BF16),
            jax.ShapeDtypeStruct((8, rows), F32),
        ),
        in_specs=[SMEM] + [VMEM] * 4,
        out_specs=(VMEM,) * 2,
        compiler_params=PARAMS,
        name="norm",
    )(core_at, mine, other, gain_wide, shift_wide)
    mean, inv = stats[0], stats[1]
    normed = normed.reshape(width, rows)

    target = llm_rank[:, 0]
    owners = jnp.arange(senders, dtype=jnp.int32)
    hits = (target[:, None] == owners[None, :]).astype(jnp.int32)
    rank = jnp.sum((jnp.cumsum(hits, 0) - hits) * hits, 1)
    slot = target * most + rank
    d_embed = returned.reshape(senders * most, out_cols)[slot]
    d_halves = [d_embed[:, h * half : (h + 1) * half] for h in range(2)]

    grad_ys = []
    for h in range(2):
        grad_part = jnp.dot(normed, d_halves[h], preferred_element_type=F32).astype(BF16)
        grad_ys.append(lax.psum_scatter(grad_part, "y", scatter_dimension=0, tiled=True))

    def outgoing(h):
        embed = lax.dot_general(
            normed, weights[h], (((0,), (0,)), ((), ())), preferred_element_type=F32
        ).astype(BF16)
        placed = jnp.zeros((senders * most, half), BF16).at[slot].set(embed)
        return placed.reshape(senders, most, half)

    first, _ = lax.optimization_barrier((outgoing(0), d_embed))
    first = exchange(first, ENC)
    second, first = lax.optimization_barrier((outgoing(1), first))
    second = exchange(second, ENC)

    half_shape = jax.ShapeDtypeStruct((n_z, own_width + EXTRA, rows), BF16)
    keep, send = pl.pallas_call(
        functools.partial(part_kernel, n_zl, n_zh),
        out_shape=(half_shape, half_shape),
        in_specs=[SMEM] + [VMEM] * 7,
        out_specs=(VMEM,) * 2,
        compiler_params=PARAMS,
        name="part",
    )(
        core_at,
        weights[0].reshape(blocks, own_width, half),
        weights[1].reshape(blocks, own_width, half),
        jnp.stack(d_halves),
        mine,
        other,
        gain_wide,
        stats,
    )
    pairs = pl.pallas_call(
        pair_kernel,
        out_shape=half_shape,
        in_specs=[VMEM] * 2,
        out_specs=VMEM,
        compiler_params=PARAMS,
        name="pair",
    )(keep, core_swap(send))
    pairs, second = lax.optimization_barrier((pairs, second))
    columns = jnp.sum(exchange(pairs, ZED).astype(F32), 0)
    dnormed = columns[:own_width]
    tail = columns[own_width:]
    plain = (tail[0] + tail[1]) / width
    cross = (tail[2] + tail[3]) / width

    column_start = lax.axis_index(COLS) * own_width
    gain_own = lax.dynamic_slice_in_dim(gain, column_start, own_width, 0)[:, None]
    xhat_own = (own_t.astype(F32) - mean) * inv
    hidden = (inv * (dnormed * gain_own - plain - xhat_own * cross)).astype(BF16).T
    sums = jnp.concatenate([jnp.sum(dnormed * xhat_own, 1), jnp.sum(dnormed, 1)])
    grad_ys[1], sums = lax.optimization_barrier((grad_ys[1], sums))
    sums = jnp.sum(copies(sums[None], ENC), (0, 1))

    def reduced(grad_y):
        grad_y = grad_y.reshape(n_x, slice_rows, half)

        def block(step):
            return lax.dynamic_index_in_dim(grad_y, lax.rem(x_at + step, n_x), 0, keepdims=False)

        return sum(
            [shifted(block(k), "x", k).astype(F32) for k in range(1, n_x)], block(0).astype(F32)
        )

    grad_weight = jnp.concatenate([reduced(grad_y) for grad_y in grad_ys], 1)
    embeds_recv = jnp.concatenate([first, second], 2).reshape(senders * most, out_cols)
    return embeds_recv, hidden, grad_weight, sums[:own_width], sums[own_width:]


def solution(mesh):
    devices = mesh.devices
    split = Mesh(devices.reshape(8, 4, 4, 2, 2), ("y", "x", "zl", "co", "zh"))
    spec = P(ENC, COLS)
    in_specs = (spec, P(), P(), spec, P(ENC, None), spec)
    out_specs = (spec, spec, spec, P(COLS), P(COLS))
    return jax.shard_map(body, mesh=split, in_specs=in_specs, out_specs=out_specs, check_vma=False)
```

time: 202 us -> 260 us (1.29)
  waiting for transfers between devices: 46.8 us -> 95.1 us
  blocking collectives: 27.7 us -> 32.8 us
  local copies, waits for them, and re-layouts: 16.8 us -> 20.4 us
  starting transfers between devices: 78 us -> 74.8 us
    all_gather x0 -> x1, blocking collectives: none -> 32.8 us  [body(): mine = lax.all_gather(own_t, ZED, axis=0)]
    reduce_scatter x1 -> x2, waiting for transfers between devices: 0.01 us -> 30.2 us  [body(): lax.psum_scatter(grad_part, 'y', scatter_dimension=0, tiled=True)]
    all_gather x1 -> x2, waiting for transfers between devices: 0.02 us -> 28.8 us  [body(): lax.all_gather(weight_x[:, h * half:(h + 1) * half], 'y', axis=0, tiled=T...]
    all_to_all x1 -> x0, blocking collectives: 27.7 us -> none  [exchange(): return lax.all_to_all(x, axes, 0, 0, tiled=True)]
    ppermute x7 -> x0, starting transfers between devices: 26.2 us -> none  [along_z(): lax.ppermute(x, ('zl', 'zh'), [(at[z], at[(z + step) % count]) for z in r...]
    all_to_all x3 -> x5, starting transfers between devices: 24.7 us -> 37.5 us  [exchange(): return lax.all_to_all(x, axes, 0, 0, tiled=True)]
    ppermute x7 -> x0, waiting for transfers between devices: 10.3 us -> none  [along_z(): lax.ppermute(x, ('zl', 'zh'), [(at[z], at[(z + step) % count]) for z in r...]
    ppermute x6 -> x9, starting transfers between devices: 23.2 us -> 33.3 us  [shifted(): lax.ppermute(x, axes, [(i, (i + step) % count) for i in range(count)])]
  transfers between devices with their start and end apart: 20 -> 20, of which waited for: 9 -> 8; matrix products, arithmetic and copies ran while one was open for 9% -> 10% of each run, Pallas kernels for 4% -> 4%
where the time goes in v3:
time: 260 us; the launch traced here: 258 us
  waiting for transfers between devices  95.1 us (37%)
  starting transfers between devices  74.8 us (29%)
  blocking collectives  32.8 us (13%)
  local copies, waits for them, and re-layouts  20.4 us (8%)
  between operations  14.2 us (5%)
  Pallas kernels  9.36 us (4%)
  matrix products  6.95 us (3%)
  other arithmetic  4.55 us (2%)
    all_to_all x5, starting transfers between devices, exchange(): return lax.all_to_all(x, axes, 0, 0, tiled=True)  37.5 us
    ppermute x9, starting transfers between devices, shifted(): lax.ppermute(x, axes, [(i, (i + step) % count) for i in range(count)])  33.3 us
    all_gather x1, blocking collectives, body(): mine = lax.all_gather(own_t, ZED, axis=0)  32.8 us
    all_to_all x5, waiting for transfers between devices, exchange(): return lax.all_to_all(x, axes, 0, 0, tiled=True)  30.3 us
    reduce_scatter x2, waiting for transfers between devices, body(): lax.psum_scatter(grad_part, 'y', scatter_dimension=0, tiled=True)  30.2 us
    all_gather x2, waiting for transfers between devices, body(): lax.all_gather(weight_x[:, h * half:(h + 1) * half], 'y', axis=0, tiled=T...  28.8 us
    unnamed x31, local copies, waits for them, and re-layouts  5.38 us
  transfers between devices with their start and end apart: 20, of which 8 were waited for; matrix products, arithmetic and copies ran while one was open for 10% of the time, Pallas kernels for 4%

profile of v3, /device:TPU:6, one launch (start us, length us, event | category | flops | bytes accessed | tf_op | source)
XLA Modules:
  0.0 258.1 jit_solution(15447742787408579969)
XLA Ops:
  7.2 2.7 %collective-permute-start = (bf16[100,512]{1,0:T(8,128)(2,1)}, bf16[100,512]{1,0:T(8,128)(2,1)S(1)}, u32[]{:S(2)}, u32[]{:S(2)}) collective-permute-start(bf16[100,512]{1,0:T(8,128)(2,1)} %param.9), channel_id=1, source_target_pairs={{0,48},{16,0},{32,16},{48,32},{1,49},{17,1},{33,17},{49,33},{2,50}... | collective-permute-start | bytes 307208 | tf_op jit(solution)/shard_map/ppermute | solution.py:34
  10.0 8.4 %collective-permute-start.1 = (bf16[100,512]{1,0:T(8,128)(2,1)}, bf16[100,512]{1,0:T(8,128)(2,1)S(1)}, u32[]{:S(2)}, u32[]{:S(2)}) collective-permute-start(bf16[100,512]{1,0:T(8,128)(2,1)} %param.9), channel_id=1, source_target_pairs={{0,32},{16,48},{32,0},{48,16},{1,33},{17,49},{33,1},{49,17},{2,34}... | collective-permute-start | bytes 307208 | tf_op jit(solution)/shard_map/ppermute | solution.py:34
  18.4 1.9 collective-permute-start.2
  21.3 3.9 %collective-permute-done.2 = bf16[100,512]{1,0:T(8,128)(2,1)S(1)} collective-permute-done((bf16[100,512]{1,0:T(8,128)(2,1)}, bf16[100,512]{1,0:T(8,128)(2,1)S(1)}, u32[]{:S(2)}, u32[]{:S(2)}) %collective-permute-start.2) | collective-permute-done | bytes 102432 | tf_op jit(solution)/shard_map/ppermute | solution.py:34
  27.8 6.2 %all-to-all-start = ((bf16[32,24,512]{2,1,0:T(8,128)(2,1)}), bf16[32,24,512]{2,1,0:T(8,128)(2,1)}, u32[]{:S(2)}, u32[]{:S(2)}) async-start(bf16[32,24,512]{2,1,0:T(8,128)(2,1)} %bitcast.15), calls=%async_computation | async-start | bytes 1572864 | tf_op jit(solution)/shard_map/all_to_all | solution.py:24
  34.1 32.8 %all-gather = bf16[1600,256]{1,0:T(8,128)(2,1)S(1)} all-gather(bf16[200,256]{1,0:T(8,128)(2,1)S(1)} %bitcast.91), channel_id=2, replica_groups=mesh['y'=8,'x'=4,'zl'=4,'co'=2,'zh'=2] {'zh','zl'}, dimensions={0}, use_global_device_ids=true | all-gather | bytes 921600 | tf_op jit(solution)/shard_map/all_gather | solution.py:145
  66.9 1.9 collective-permute-start.3
  73.4 2.4 norm.1
  77.0 2.6 gather_fusion
  81.3 2.8 %convolution_convert_fusion.2 = bf16[256,256]{1,0:T(8,128)(2,1)} fusion(bf16[3200,256]{1,0:T(8,128)(2,1)S(1)} %bitcast.84, bf16[3200,256]{1,0:T(8,128)(2,1)} %all-gather.6.cloned.1.call-done), kind=kOutput, calls=%fused_computation.6 | convolution fusion | flops 419495936 | bytes 3407872 | tf_op jit(solution)/shard_map/dot_general | solution.py:178
  84.1 2.6 %scatter_custom_fusion.1 = bf16[768,256]{1,0:T(8,128)(2,1)} fusion(s32[256]{0:T(256)S(1)} %bitcast.100, bf16[256,256]{1,0:T(8,128)(2,1)} %convolution_convert_fusion.2, bf16[]{:T(256)} %constant.59.clone.1), kind=kCustom, calls=%fused_computation.14 | custom fusion | bytes 393728 | tf_op jit(solution)/shard_map/scatter | solution.py:181
  86.7 9.8 %all-to-all-start.1 = ((bf16[32,24,256]{2,1,0:T(8,128)(2,1)}), bf16[32,24,256]{2,1,0:T(8,128)(2,1)}, u32[]{:S(2)}, u32[]{:S(2)}) async-start(bf16[32,24,256]{2,1,0:T(8,128)(2,1)} %bitcast.89), calls=%async_computation.1 | async-start | bytes 786432 | tf_op jit(solution)/shard_map/all_to_all | solution.py:24
  98.4 28.8 %all-gather.4.cloned.1.call-done = bf16[3200,256]{1,0:T(8,128)(2,1)} async-done(((bf16[400,256]{1,0:T(8,128)(2,1)}), bf16[3200,256]{1,0:T(8,128)(2,1)}) %all-gather.4.cloned.1.call-update) | async-done | bytes 1638416 | tf_op jit(solution)/shard_map/all_gather | solution.py:138
  128.6 4.6 %part.1 = (bf16[8,208,256]{2,1,0:T(8,128)(2,1)S(1)}, bf16[8,208,256]{2,1,0:T(8,128)(2,1)}) custom-call(s32[1]{0:T(128)} %bitcast.5.core_at, bf16[16,200,256]{2,1,0:T(8,128)(2,1)S(1)} %bitcast.87, bf16[16,200,256]{2,1,0:T(8,128)(2,1)} %bitcast.88, bf16[2,256,256]{2,1,0:T(8,128)(2,1)S(1)} %pad_maximum_fusion.1.d_embed, bf16[8,200,256]{2,1,0:T(8,128)(2,1)S(1)} %bitcast.82, ...), custom_call_target="tpu_custom_call" | custom-call | tf_op jit(solution)/shard_map/part/pallas_call | solution.py:190
  134.2 1.9 collective-permute-start.4
  136.8 2.2 scatter_custom_fusion
  139.0 6.7 %all-to-all-start.2 = ((bf16[32,24,256]{2,1,0:T(8,128)(2,1)}), bf16[32,24,256]{2,1,0:T(8,128)(2,1)S(1)}, u32[]{:S(2)}, u32[]{:S(2)}) async-start(bf16[32,24,256]{2,1,0:T(8,128)(2,1)} %bitcast.13), calls=%async_computation.2 | async-start | bytes 786432 | tf_op jit(solution)/shard_map/all_to_all | solution.py:24
  145.7 2.3 pair.1
  148.0 15.9 %all-to-all-done.2 = bf16[32,24,256]{2,1,0:T(8,128)(2,1)S(1)} async-done(((bf16[32,24,256]{2,1,0:T(8,128)(2,1)}), bf16[32,24,256]{2,1,0:T(8,128)(2,1)S(1)}, u32[]{:S(2)}, u32[]{:S(2)}) %all-to-all-start.2) | async-done | bytes 393248 | tf_op jit(solution)/shard_map/all_to_all | solution.py:24
  163.9 7.5 %all-to-all-start.3 = ((bf16[8,208,256]{2,1,0:T(8,128)(2,1)}), bf16[8,208,256]{2,1,0:T(8,128)(2,1)S(1)}, u32[]{:S(2)}, u32[]{:S(2)}) async-start(bf16[8,208,256]{2,1,0:T(8,128)(2,1)} %pair.1), calls=%async_computation.3 | async-start | bytes 1703936 | tf_op jit(solution)/shard_map/all_to_all | solution.py:24
  172.1 2.0 pad_maximum_fusion
  174.1 3.2 %reduce-scatter.3.cloned.1.call-done = bf16[400,256]{1,0:T(8,128)(2,1)} async-done(((bf16[3200,256]{1,0:T(8,128)(2,1)}), bf16[400,256]{1,0:T(8,128)(2,1)}) %reduce-scatter.3.cloned.1.call-update) | async-done | bytes 204816 | tf_op jit(solution)/shard_map/reduce_scatter | solution.py:175
  178.3 3.2 %collective-permute-start.7 = (bf16[100,256]{1,0:T(8,128)(2,1)S(1)}, bf16[100,256]{1,0:T(8,128)(2,1)S(1)}, u32[]{:S(2)}, u32[]{:S(2)}) collective-permute-start(bf16[100,256]{1,0:T(8,128)(2,1)S(1)} %get-tuple-element.37), channel_id=1, source_target_pairs={{0,48},{16,0},{32,16},{48,32},{1,49},{17,1},{33,17},{49,33},{2,50}... | collective-permute-start | bytes 153608 | tf_op jit(solution)/shard_map/ppermute | solution.py:34
  181.5 2.6 collective-permute-start.6
  184.1 4.5 %collective-permute-start.5 = (bf16[100,256]{1,0:T(8,128)(2,1)S(1)}, bf16[100,256]{1,0:T(8,128)(2,1)S(1)}, u32[]{:S(2)}, u32[]{:S(2)}) collective-permute-start(bf16[100,256]{1,0:T(8,128)(2,1)S(1)} %get-tuple-element.36), channel_id=1, source_target_pairs={{0,16},{16,32},{32,48},{48,0},{1,17},{17,33},{33,49},{49,1},{2,18}... | collective-permute-start | bytes 153608 | tf_op jit(solution)/shard_map/ppermute | solution.py:34
  188.6 6.9 %all-to-all-done.3 = bf16[8,208,256]{2,1,0:T(8,128)(2,1)S(1)} async-done(((bf16[8,208,256]{2,1,0:T(8,128)(2,1)}), bf16[8,208,256]{2,1,0:T(8,128)(2,1)S(1)}, u32[]{:S(2)}, u32[]{:S(2)}) %all-to-all-start.3) | async-done | bytes 852000 | tf_op jit(solution)/shard_map/all_to_all | solution.py:24
  196.4 27.0 %reduce-scatter.5.cloned.1.call-done = bf16[400,256]{1,0:T(8,128)(2,1)} async-done(((bf16[3200,256]{1,0:T(8,128)(2,1)}), bf16[400,256]{1,0:T(8,128)(2,1)}) %reduce-scatter.5.cloned.1.call-update) | async-done | bytes 204816 | tf_op jit(solution)/shard_map/reduce_scatter | solution.py:175
  224.4 2.7 %collective-permute-start.10 = (bf16[100,256]{1,0:T(8,128)(2,1)S(1)}, bf16[100,256]{1,0:T(8,128)(2,1)S(1)}, u32[]{:S(2)}, u32[]{:S(2)}) collective-permute-start(bf16[100,256]{1,0:T(8,128)(2,1)S(1)} %get-tuple-element.40), channel_id=1, source_target_pairs={{0,48},{16,0},{32,16},{48,32},{1,49},{17,1},{33,17},{49,33},{2,50}... | collective-permute-start | bytes 153608 | tf_op jit(solution)/shard_map/ppermute | solution.py:34
  227.2 3.3 %collective-permute-start.9 = (bf16[100,256]{1,0:T(8,128)(2,1)S(1)}, bf16[100,256]{1,0:T(8,128)(2,1)S(1)}, u32[]{:S(2)}, u32[]{:S(2)}) collective-permute-start(bf16[100,256]{1,0:T(8,128)(2,1)S(1)} %get-tuple-element.41), channel_id=1, source_target_pairs={{0,32},{16,48},{32,0},{48,16},{1,33},{17,49},{33,1},{49,17},{2,34}... | collective-permute-start | bytes 153608 | tf_op jit(solution)/shard_map/ppermute | solution.py:34
  230.5 4.0 %collective-permute-start.8 = (bf16[100,256]{1,0:T(8,128)(2,1)S(1)}, bf16[100,256]{1,0:T(8,128)(2,1)S(1)}, u32[]{:S(2)}, u32[]{:S(2)}) collective-permute-start(bf16[100,256]{1,0:T(8,128)(2,1)S(1)} %get-tuple-element.39), channel_id=1, source_target_pairs={{0,16},{16,32},{32,48},{48,0},{1,17},{17,33},{33,49},{49,1},{2,18}... | collective-permute-start | bytes 153608 | tf_op jit(solution)/shard_map/ppermute | solution.py:34
  235.2 7.3 %all-to-all-start.4 = ((f32[32,1,400]{2,1,0:T(1,128)}), f32[32,1,400]{2,1,0:T(1,128)S(1)}, u32[]{:S(2)}, u32[]{:S(2)}) async-start(f32[32,1,400]{2,1,0:T(1,128)} %broadcast_in_dim.14), calls=%async_computation.6 | async-start | bytes 131072 | tf_op jit(solution)/shard_map/all_to_all | solution.py:24
  243.3 7.6 %all-to-all-done.4 = f32[32,1,400]{2,1,0:T(1,128)S(1)} async-done(((f32[32,1,400]{2,1,0:T(1,128)}), f32[32,1,400]{2,1,0:T(1,128)S(1)}, u32[]{:S(2)}, u32[]{:S(2)}) %all-to-all-start.4) | async-done | bytes 51232 | tf_op jit(solution)/shard_map/all_to_all | solution.py:24
  (89 shorter events, 21.8 us)
Async XLA Ops:
  7.2 74.2 %all-gather.6.cloned.1.call-start = ((), (), s32[]{:S(2)}) async-start(), calls=%async_computation.8 | async-start | bytes 1843200 | tf_op jit(solution)/shard_map/all_gather | solution.py:138
  7.2 14.0 %collective-permute-start = (bf16[100,512]{1,0:T(8,128)(2,1)}, bf16[100,512]{1,0:T(8,128)(2,1)S(1)}, u32[]{:S(2)}, u32[]{:S(2)}) collective-permute-start(bf16[100,512]{1,0:T(8,128)(2,1)} %param.9), channel_id=1, source_target_pairs={{0,48},{16,0},{32,16},{48,32},{1,49},{17,1},{33,17},{49,33},{2,50}... | collective-permute-start | bytes 307208 | tf_op jit(solution)/shard_map/ppermute | solution.py:34
  10.0 11.3 %collective-permute-start.1 = (bf16[100,512]{1,0:T(8,128)(2,1)}, bf16[100,512]{1,0:T(8,128)(2,1)S(1)}, u32[]{:S(2)}, u32[]{:S(2)}) collective-permute-start(bf16[100,512]{1,0:T(8,128)(2,1)} %param.9), channel_id=1, source_target_pairs={{0,32},{16,48},{32,0},{48,16},{1,33},{17,49},{33,1},{49,17},{2,34}... | collective-permute-start | bytes 307208 | tf_op jit(solution)/shard_map/ppermute | solution.py:34
  18.4 6.8 %collective-permute-start.2 = (bf16[100,512]{1,0:T(8,128)(2,1)}, bf16[100,512]{1,0:T(8,128)(2,1)S(1)}, u32[]{:S(2)}, u32[]{:S(2)}) collective-permute-start(bf16[100,512]{1,0:T(8,128)(2,1)} %param.9), channel_id=1, source_target_pairs={{0,16},{16,32},{32,48},{48,0},{1,17},{17,33},{33,49},{49,1},{2,18}... | collective-permute-start | bytes 307208 | tf_op jit(solution)/shard_map/ppermute | solution.py:34
  26.2 7.9 %copy-start.7 = (bf16[256,200]{0,1:T(8,128)(2,1)S(1)}, bf16[256,200]{0,1:T(8,128)(2,1)}, u32[]{:S(2)}) copy-start(bf16[256,200]{0,1:T(8,128)(2,1)} %param.6) | copy-start | bytes 307204
  27.1 41.8 %copy-start.11 = (s32[256,1]{0,1:T(1,128)S(1)}, s32[256,1]{0,1:T(1,128)}, u32[]{:S(2)}) copy-start(s32[256,1]{0,1:T(1,128)} %param.10) | copy-start | bytes 3076
  27.1 42.6 %copy-start.9 = (f32[3200]{0:T(1024)S(1)}, f32[3200]{0:T(1024)}, u32[]{:S(2)}) copy-start(f32[3200]{0:T(1024)} %param.7) | copy-start | bytes 38404
  27.1 42.8 %copy-start.10 = (f32[3200]{0:T(1024)S(1)}, f32[3200]{0:T(1024)}, u32[]{:S(2)}) copy-start(f32[3200]{0:T(1024)} %param.8) | copy-start | bytes 38404
  27.1 100.1 %all-gather.4.cloned.1.call-start = ((), (), s32[]{:S(2)}) async-start(), calls=%async_computation.7 | async-start | bytes 1843200 | tf_op jit(solution)/shard_map/all_gather | solution.py:138
  27.8 49.1 %all-to-all-start = ((bf16[32,24,512]{2,1,0:T(8,128)(2,1)}), bf16[32,24,512]{2,1,0:T(8,128)(2,1)}, u32[]{:S(2)}, u32[]{:S(2)}) async-start(bf16[32,24,512]{2,1,0:T(8,128)(2,1)} %bitcast.15), calls=%async_computation | async-start | bytes 1572864 | tf_op jit(solution)/shard_map/all_to_all | solution.py:24
  34.1 143.3 %reduce-scatter.3.cloned.1.call-start = ((), (), s32[]{:S(2)}) async-start(), calls=%async_computation.9 | async-start | bytes 1843200 | tf_op jit(solution)/shard_map/reduce_scatter | solution.py:175
  66.9 4.2 %collective-permute-start.3 = (bf16[8,200,256]{2,1,0:T(8,128)(2,1)S(1)}, bf16[8,200,256]{2,1,0:T(8,128)(2,1)S(1)}, u32[]{:S(2)}, u32[]{:S(2)}) collective-permute-start(bf16[8,200,256]{2,1,0:T(8,128)(2,1)S(1)} %bitcast.80), channel_id=1, source_target_pairs={{0,2},{2,0},{1,3},{3,1},{4,6},{6,4},{5,7},{7,5},{8,10},{10,8},{9,1... | collective-permute-start | bytes 2457608 | tf_op jit(solution)/shard_map/ppermute | solution.py:38
  71.6 4.2 %copy-start = (f32[16,200,128]{2,1,0:T(8,128)}, f32[16,200,128]{2,1,0:T(8,128)S(1)}, u32[]{:S(2)}) copy-start(f32[16,200,128]{2,1,0:T(8,128)S(1)} %broadcast_in_dim.11.gain) | copy-start | bytes 4915204
  75.8 1.2 copy-start.1
  77.0 2.6 copy-start.2
  86.7 52.3 %all-to-all-start.1 = ((bf16[32,24,256]{2,1,0:T(8,128)(2,1)}), bf16[32,24,256]{2,1,0:T(8,128)(2,1)}, u32[]{:S(2)}, u32[]{:S(2)}) async-start(bf16[32,24,256]{2,1,0:T(8,128)(2,1)} %bitcast.89), calls=%async_computation.1 | async-start | bytes 786432 | tf_op jit(solution)/shard_map/all_to_all | solution.py:24
  96.5 126.9 %reduce-scatter.5.cloned.1.call-start = ((), (), s32[]{:S(2)}) async-start(), calls=%async_computation.10 | async-start | bytes 1843200 | tf_op jit(solution)/shard_map/reduce_scatter | solution.py:175
  127.2 1.4 copy-start.3
  128.6 7.5 %copy-start.6 = (bf16[3200,256]{1,0:T(8,128)(2,1)S(1)}, bf16[3200,256]{1,0:T(8,128)(2,1)}, u32[]{:S(2)}) copy-start(bf16[3200,256]{1,0:T(8,128)(2,1)} %all-gather.4.cloned.1.call-done) | copy-start | bytes 4915204
  133.3 0.9 copy-start.4
  134.2 11.5 %collective-permute-start.4 = (bf16[8,208,256]{2,1,0:T(8,128)(2,1)}, bf16[8,208,256]{2,1,0:T(8,128)(2,1)}, u32[]{:S(2)}, u32[]{:S(2)}) collective-permute-start(bf16[8,208,256]{2,1,0:T(8,128)(2,1)} %get-tuple-element.23), channel_id=1, source_target_pairs={{0,2},{2,0},{1,3},{3,1},{4,6},{6,4},{5,7},{7,5},{8,10},{10,8},{9,1... | collective-permute-start | bytes 2555912 | tf_op jit(solution)/shard_map/ppermute | solution.py:38
  136.8 8.9 %copy-start.5 = (bf16[8,208,256]{2,1,0:T(8,128)(2,1)S(1)}, bf16[8,208,256]{2,1,0:T(8,128)(2,1)}, u32[]{:S(2)}) copy-start(bf16[8,208,256]{2,1,0:T(8,128)(2,1)} %copy-done.4) | copy-start | bytes 2555908
  139.0 24.9 %all-to-all-start.2 = ((bf16[32,24,256]{2,1,0:T(8,128)(2,1)}), bf16[32,24,256]{2,1,0:T(8,128)(2,1)S(1)}, u32[]{:S(2)}, u32[]{:S(2)}) async-start(bf16[32,24,256]{2,1,0:T(8,128)(2,1)} %bitcast.13), calls=%async_computation.2 | async-start | bytes 786432 | tf_op jit(solution)/shard_map/all_to_all | solution.py:24
  163.9 31.6 %all-to-all-start.3 = ((bf16[8,208,256]{2,1,0:T(8,128)(2,1)}), bf16[8,208,256]{2,1,0:T(8,128)(2,1)S(1)}, u32[]{:S(2)}, u32[]{:S(2)}) async-start(bf16[8,208,256]{2,1,0:T(8,128)(2,1)} %pair.1), calls=%async_computation.3 | async-start | bytes 1703936 | tf_op jit(solution)/shard_map/all_to_all | solution.py:24
  172.1 23.4 %copy-start.8 = (bf16[256,200]{0,1:T(8,128)(2,1)S(1)}, bf16[256,200]{0,1:T(8,128)(2,1)}, u32[]{:S(2)}) copy-start(bf16[256,200]{0,1:T(8,128)(2,1)} %param.6) | copy-start | bytes 307204
  178.3 52.2 %collective-permute-start.7 = (bf16[100,256]{1,0:T(8,128)(2,1)S(1)}, bf16[100,256]{1,0:T(8,128)(2,1)S(1)}, u32[]{:S(2)}, u32[]{:S(2)}) collective-permute-start(bf16[100,256]{1,0:T(8,128)(2,1)S(1)} %get-tuple-element.37), channel_id=1, source_target_pairs={{0,48},{16,0},{32,16},{48,32},{1,49},{17,1},{33,17},{49,33},{2,50}... | collective-permute-start | bytes 153608 | tf_op jit(solution)/shard_map/ppermute | solution.py:34
  181.5 53.0 %collective-permute-start.6 = (bf16[100,256]{1,0:T(8,128)(2,1)S(1)}, bf16[100,256]{1,0:T(8,128)(2,1)S(1)}, u32[]{:S(2)}, u32[]{:S(2)}) collective-permute-start(bf16[100,256]{1,0:T(8,128)(2,1)S(1)} %get-tuple-element.38), channel_id=1, source_target_pairs={{0,32},{16,48},{32,0},{48,16},{1,33},{17,49},{33,1},{49,17},{2,34}... | collective-permute-start | bytes 153608 | tf_op jit(solution)/shard_map/ppermute | solution.py:34
  184.1 50.4 %collective-permute-start.5 = (bf16[100,256]{1,0:T(8,128)(2,1)S(1)}, bf16[100,256]{1,0:T(8,128)(2,1)S(1)}, u32[]{:S(2)}, u32[]{:S(2)}) collective-permute-start(bf16[100,256]{1,0:T(8,128)(2,1)S(1)} %get-tuple-element.36), channel_id=1, source_target_pairs={{0,16},{16,32},{32,48},{48,0},{1,17},{17,33},{33,49},{49,1},{2,18}... | collective-permute-start | bytes 153608 | tf_op jit(solution)/shard_map/ppermute | solution.py:34
  224.4 18.1 %collective-permute-start.10 = (bf16[100,256]{1,0:T(8,128)(2,1)S(1)}, bf16[100,256]{1,0:T(8,128)(2,1)S(1)}, u32[]{:S(2)}, u32[]{:S(2)}) collective-permute-start(bf16[100,256]{1,0:T(8,128)(2,1)S(1)} %get-tuple-element.40), channel_id=1, source_target_pairs={{0,48},{16,0},{32,16},{48,32},{1,49},{17,1},{33,17},{49,33},{2,50}... | collective-permute-start | bytes 153608 | tf_op jit(solution)/shard_map/ppermute | solution.py:34
  227.2 15.3 %collective-permute-start.9 = (bf16[100,256]{1,0:T(8,128)(2,1)S(1)}, bf16[100,256]{1,0:T(8,128)(2,1)S(1)}, u32[]{:S(2)}, u32[]{:S(2)}) collective-permute-start(bf16[100,256]{1,0:T(8,128)(2,1)S(1)} %get-tuple-element.41), channel_id=1, source_target_pairs={{0,32},{16,48},{32,0},{48,16},{1,33},{17,49},{33,1},{49,17},{2,34}... | collective-permute-start | bytes 153608 | tf_op jit(solution)/shard_map/ppermute | solution.py:34
  230.5 12.1 %collective-permute-start.8 = (bf16[100,256]{1,0:T(8,128)(2,1)S(1)}, bf16[100,256]{1,0:T(8,128)(2,1)S(1)}, u32[]{:S(2)}, u32[]{:S(2)}) collective-permute-start(bf16[100,256]{1,0:T(8,128)(2,1)S(1)} %get-tuple-element.39), channel_id=1, source_target_pairs={{0,16},{16,32},{32,48},{48,0},{1,17},{17,33},{33,49},{49,1},{2,18}... | collective-permute-start | bytes 153608 | tf_op jit(solution)/shard_map/ppermute | solution.py:34
  235.2 15.7 %all-to-all-start.4 = ((f32[32,1,400]{2,1,0:T(1,128)}), f32[32,1,400]{2,1,0:T(1,128)S(1)}, u32[]{:S(2)}, u32[]{:S(2)}) async-start(f32[32,1,400]{2,1,0:T(1,128)} %broadcast_in_dim.14), calls=%async_computation.6 | async-start | bytes 131072 | tf_op jit(solution)/shard_map/all_to_all | solution.py:24
Sparse Core Ops, SparseCore 0:
  27.2 47.8 all-gather.5
  77.7 49.4 all-gather.3
  130.1 47.2 reduce-scatter.2
  180.0 43.3 reduce-scatter.4

commit v4 on v2

--- a/solution.py
+++ b/solution.py
@@ -10,6 +10,7 @@
 
 ENC = ("y", "x")
 COLS = ("zl", "co", "zh")
+ZED = ("zh", "zl")
 EPSILON = 1e-05
 F32 = jnp.float32
 BF16 = jnp.bfloat16
@@ -44,16 +45,16 @@
     return lax.ppermute(x, "co", [(0, 1), (1, 0)])
 
 
-def block_of(i, core, n_zh):
-    return (i // n_zh) * (2 * n_zh) + core * n_zh + i % n_zh
+def block_of(z, core, n_zl, n_zh):
+    return (z % n_zl) * (2 * n_zh) + core * n_zh + z // n_zl
 
 
 def wide(column, rows):
     return jnp.concatenate([column] * (rows // column.shape[1]), 1)
 
 
-def norm_kernel(n_zh, place, mine, other, gain, shift, normed, stats):
-    core = place[1]
+def norm_kernel(n_zl, n_zh, at, mine, other, gain, shift, normed, stats):
+    core = at[0]
     n_z, own_width, rows = mine.shape
     width = 2 * n_z * own_width
 
@@ -73,7 +74,7 @@
     stats[1:2, :] = inv
     for i in range(n_z):
         for ref, owner in ((mine, core), (other, 1 - core)):
-            b = block_of(i, owner, n_zh)
+            b = block_of(i, owner, n_zl, n_zh)
             value = (ref[i].astype(F32) - mean) * inv * wide(gain[b], rows) + wide(shift[b], rows)
             normed[b] = value.astype(BF16)
 
@@ -86,14 +87,14 @@
     ).astype(BF16)
 
 
-def part_kernel(n_zh, place, weight, d_embed, mine, other, gain, stats, keep, send):
-    core = place[1]
+def part_kernel(n_zl, n_zh, at, weight, d_embed, mine, other, gain, stats, keep, send):
+    core = at[0]
     n_z, own_width, rows = mine.shape
     mean, inv = stats[0:1, :], stats[1:2, :]
     plain = cross = jnp.zeros((1, rows), F32)
     for i in range(n_z):
         for source, owner, out in ((mine, core, keep), (other, 1 - core, send)):
-            b = block_of(i, owner, n_zh)
+            b = block_of(i, owner, n_zl, n_zh)
             part = lax.dot_general(
                 weight[b], d_embed[...], (((1,), (1,)), ((), ())), preferred_element_type=F32
             ).astype(BF16)
@@ -108,13 +109,12 @@
         send[i, own_width:, :] = tail
 
 
-def pair_kernel(n_zl, n_zh, place, keep, recv, *outs):
+def pair_kernel(at, keep, recv, *outs):
     n_z, own_width = keep.shape[0], keep.shape[1] - EXTRA
     tail = keep[0, own_width:, :].astype(F32) + recv[0, own_width:, :].astype(F32)
     tail = high_low(tail[0:1] + tail[1:2], tail[2:3] + tail[3:4])
     for k, out in enumerate(outs):
-        target = lax.rem(place[0] + k, n_z)
-        i = lax.rem(target, n_zl) * n_zh + target // n_zl
+        i = lax.rem(at[1] + k, n_z)
         pair = keep[i, 0:own_width, :].astype(F32) + recv[i, 0:own_width, :].astype(F32)
         out[0:own_width, :] = pair.astype(BF16)
         out[own_width:, :] = tail
@@ -132,24 +132,24 @@
     most = embed_grad.shape[0] // senders
     blocks = width // own_width
     core, x_at = lax.axis_index("co"), lax.axis_index("x")
-    place = jnp.stack([lax.axis_index("zh") * n_zl + lax.axis_index("zl"), core]).astype(jnp.int32)
-
-    own_t = patches.T
-    mine = copies(own_t, ("zl", "zh"))
-    other = core_swap(mine)
+    at = jnp.stack([core, lax.axis_index(ZED)]).astype(jnp.int32)
 
     weight_rel = [proj_weight] + [shifted(proj_weight, "x", k) for k in range(1, n_x)]
     ordered = jnp.stack([weight_rel[-i % n_x] for i in range(n_x)] * 2)
     weight_x = lax.dynamic_slice_in_dim(ordered, lax.rem(n_x - x_at, n_x), n_x, 0)
-    weight = lax.all_gather(weight_x.reshape(n_x * slice_rows, out_cols), "y", axis=0, tiled=True)
-
-    embed_grad, mine = lax.optimization_barrier((embed_grad, mine))
+    weight_x = weight_x.reshape(n_x * slice_rows, out_cols)
+    weight = lax.all_gather(weight_x, "y", axis=0, tiled=True)
+
     returned = exchange(embed_grad.reshape(senders, most, out_cols), ENC)
+    own_t = patches.T
+    own_t, _ = lax.optimization_barrier((own_t, weight_x))
+    mine = lax.all_gather(own_t, ZED, axis=0)
+    other = core_swap(mine)
 
     gain_wide = jnp.broadcast_to(gain.reshape(blocks, own_width, 1), (blocks, own_width, 128))
     shift_wide = jnp.broadcast_to(shift.reshape(blocks, own_width, 1), (blocks, own_width, 128))
     normed, stats = pl.pallas_call(
-        functools.partial(norm_kernel, n_zh),
+        functools.partial(norm_kernel, n_zl, n_zh),
         out_shape=(
             jax.ShapeDtypeStruct((blocks, own_width, rows), BF16),
             jax.ShapeDtypeStruct((8, rows), F32),
@@ -158,7 +158,7 @@
         out_specs=(VMEM,) * 2,
         compiler_params=PARAMS,
         name="norm",
-    )(place, mine, other, gain_wide, shift_wide)
+    )(at, mine, other, gain_wide, shift_wide)
     mean, inv = stats[0], stats[1]
     normed = normed.reshape(width, rows)
 
@@ -171,25 +171,18 @@
 
     grad_part = jnp.dot(normed, d_embed, preferred_element_type=F32).astype(BF16)
     grad_y = lax.psum_scatter(grad_part, "y", scatter_dimension=0, tiled=True)
-    grad_y = grad_y.reshape(n_x, slice_rows, out_cols)
-
-    def grad_block(step):
-        return lax.dynamic_index_in_dim(grad_y, lax.rem(x_at + step, n_x), 0, keepdims=False)
-
-    grad_weight = sum(
-        [shifted(grad_block(k), "x", k).astype(F32) for k in range(1, n_x)],
-        grad_block(0).astype(F32),
-    )
 
     half_shape = jax.ShapeDtypeStruct((n_z, own_width + EXTRA, rows), BF16)
     keep, send = pl.pallas_call(
-        functools.partial(part_kernel, n_zh),
+        functools.partial(part_kernel, n_zl, n_zh),
         out_shape=(half_shape, half_shape),
         in_specs=[SMEM] + [VMEM] * 6,
         out_specs=(VMEM,) * 2,
         compiler_params=PARAMS,
         name="part",
-    )(place, weight.reshape(blocks, own_width, out_cols), d_embed, mine, other, gain_wide, stats)
+    )(
+        at, weight.reshape(blocks, own_width, out_cols), d_embed, mine, other, gain_wide, stats
+    )
     recv = core_swap(send)
 
     weight_after, keep = lax.optimization_barrier((weight, keep))
@@ -202,13 +195,13 @@
     )
 
     pairs = pl.pallas_call(
-        functools.partial(pair_kernel, n_zl, n_zh),
+        pair_kernel,
         out_shape=(jax.ShapeDtypeStruct((own_width + EXTRA, rows), BF16),) * n_z,
         in_specs=[SMEM] + [VMEM] * 2,
         out_specs=(VMEM,) * n_z,
         compiler_params=PARAMS,
         name="pair",
-    )(place, keep, recv)
+    )(at, keep, recv)
     columns = sum(
         [along_z(pairs[k], k).astype(F32) for k in range(1, n_z)], pairs[0].astype(F32)
     )
@@ -222,8 +215,19 @@
     xhat_own = (own_t.astype(F32) - mean) * inv
     hidden = (inv * (dnormed * gain_own - plain - xhat_own * cross)).astype(BF16).T
     sums = jnp.concatenate([jnp.sum(dnormed * xhat_own, 1), jnp.sum(dnormed, 1)])
+    grad_y, sums = lax.optimization_barrier((grad_y, sums))
     sums, embeds_recv = lax.optimization_barrier((sums, embeds_recv))
     sums = jnp.sum(copies(sums[None], ENC), (0, 1))
+
+    grad_y = grad_y.reshape(n_x, slice_rows, out_cols)
+
+    def grad_block(step):
+        return lax.dynamic_index_in_dim(grad_y, lax.rem(x_at + step, n_x), 0, keepdims=False)
+
+    grad_weight = sum(
+        [shifted(grad_block(k), "x", k).astype(F32) for k in range(1, n_x)],
+        grad_block(0).astype(F32),
+    )
     return embeds_recv, hidden, grad_weight, sums[:own_width], sums[own_width:]
 
 

time: 202 us -> 188 us (0.931)
  waiting for transfers between devices: 46.8 us -> 27.1 us
  blocking collectives: 27.7 us -> 32.8 us
  starting transfers between devices: 78 us -> 80.1 us
    all_gather x0 -> x1, blocking collectives: none -> 32.8 us  [body(): mine = lax.all_gather(own_t, ZED, axis=0)]
    all_to_all x3, waiting for transfers between devices: 28.6 us -> 0.01 us  [exchange(): return lax.all_to_all(x, axes, 0, 0, tiled=True)]
    all_to_all x1 -> x0, blocking collectives: 27.7 us -> none  [exchange(): return lax.all_to_all(x, axes, 0, 0, tiled=True)]
    reduce_scatter x1, waiting for transfers between devices: 0.01 us -> 8.51 us  [body(): grad_y = lax.psum_scatter(grad_part, 'y', scatter_dimension=0, tiled=True)]
    ppermute x7, starting transfers between devices: 26.2 us -> 29.6 us  [along_z(): lax.ppermute(x, ('zl', 'zh'), [(at[z], at[(z + step) % count]) for z in r...]
    ppermute x6, waiting for transfers between devices: 6.84 us -> 9.09 us  [shifted(): lax.ppermute(x, axes, [(i, (i + step) % count) for i in range(count)])]
    ppermute x7, waiting for transfers between devices: 10.3 us -> 8.17 us  [along_z(): lax.ppermute(x, ('zl', 'zh'), [(at[z], at[(z + step) % count]) for z in r...]
  transfers between devices with their start and end apart: 20 -> 20, of which waited for: 9 -> 7; matrix products, arithmetic and copies ran while one was open for 9% -> 10% of each run, Pallas kernels for 4% -> 4%
where the time goes in v4:
time: 188 us; the launch traced here: 187 us
  starting transfers between devices  80.1 us (43%)
  blocking collectives  32.8 us (17%)
  waiting for transfers between devices  27.1 us (14%)
  local copies, waits for them, and re-layouts  16.7 us (9%)
  between operations  14.6 us (8%)
  Pallas kernels  7.87 us (4%)
  matrix products  5.24 us (3%)
  other arithmetic  2.6 us (1%)
    all_gather x1, blocking collectives, body(): mine = lax.all_gather(own_t, ZED, axis=0)  32.8 us
    ppermute x7, starting transfers between devices, along_z(): lax.ppermute(x, ('zl', 'zh'), [(at[z], at[(z + step) % count]) for z in r...  29.6 us
    all_to_all x3, starting transfers between devices, exchange(): return lax.all_to_all(x, axes, 0, 0, tiled=True)  24.8 us
    ppermute x6, starting transfers between devices, shifted(): lax.ppermute(x, axes, [(i, (i + step) % count) for i in range(count)])  21.7 us
    ppermute x6, waiting for transfers between devices, shifted(): lax.ppermute(x, axes, [(i, (i + step) % count) for i in range(count)])  9.09 us
    reduce_scatter x1, waiting for transfers between devices, body(): grad_y = lax.psum_scatter(grad_part, 'y', scatter_dimension=0, tiled=True)  8.51 us
    ppermute x7, waiting for transfers between devices, along_z(): lax.ppermute(x, ('zl', 'zh'), [(at[z], at[(z + step) % count]) for z in r...  8.17 us
    unnamed x30, local copies, waits for them, and re-layouts  4.89 us
  transfers between devices with their start and end apart: 20, of which 7 were waited for; matrix products, arithmetic and copies ran while one was open for 10% of the time, Pallas kernels for 4%

profile of v4, /device:TPU:6, one launch (start us, length us, event | category | flops | bytes accessed | tf_op | source)
XLA Modules:
  0.0 187.0 jit_solution(8801446778343281576)
XLA Ops:
  7.2 2.7 %collective-permute-start = (bf16[100,512]{1,0:T(8,128)(2,1)}, bf16[100,512]{1,0:T(8,128)(2,1)S(1)}, u32[]{:S(2)}, u32[]{:S(2)}) collective-permute-start(bf16[100,512]{1,0:T(8,128)(2,1)} %param.9), channel_id=1, source_target_pairs={{0,48},{16,0},{32,16},{48,32},{1,49},{17,1},{33,17},{49,33},{2,50}... | collective-permute-start | bytes 307208 | tf_op jit(solution)/shard_map/ppermute | solution.py:34
  10.0 8.4 %collective-permute-start.1 = (bf16[100,512]{1,0:T(8,128)(2,1)}, bf16[100,512]{1,0:T(8,128)(2,1)S(1)}, u32[]{:S(2)}, u32[]{:S(2)}) collective-permute-start(bf16[100,512]{1,0:T(8,128)(2,1)} %param.9), channel_id=1, source_target_pairs={{0,32},{16,48},{32,0},{48,16},{1,33},{17,49},{33,1},{49,17},{2,34}... | collective-permute-start | bytes 307208 | tf_op jit(solution)/shard_map/ppermute | solution.py:34
  18.4 1.9 %collective-permute-start.2 = (bf16[100,512]{1,0:T(8,128)(2,1)}, bf16[100,512]{1,0:T(8,128)(2,1)S(1)}, u32[]{:S(2)}, u32[]{:S(2)}) collective-permute-start(bf16[100,512]{1,0:T(8,128)(2,1)} %param.9), channel_id=1, source_target_pairs={{0,16},{16,32},{32,48},{48,0},{1,17},{17,33},{33,49},{49,1},{2,18}... | collective-permute-start | bytes 307208 | tf_op jit(solution)/shard_map/ppermute | solution.py:34
  21.3 3.9 %collective-permute-done.2 = bf16[100,512]{1,0:T(8,128)(2,1)S(1)} collective-permute-done((bf16[100,512]{1,0:T(8,128)(2,1)}, bf16[100,512]{1,0:T(8,128)(2,1)S(1)}, u32[]{:S(2)}, u32[]{:S(2)}) %collective-permute-start.2) | collective-permute-done | bytes 102432 | tf_op jit(solution)/shard_map/ppermute | solution.py:34
  27.1 6.2 %all-to-all-start = ((bf16[32,24,512]{2,1,0:T(8,128)(2,1)}), bf16[32,24,512]{2,1,0:T(8,128)(2,1)}, u32[]{:S(2)}, u32[]{:S(2)}) async-start(bf16[32,24,512]{2,1,0:T(8,128)(2,1)} %bitcast.9), calls=%async_computation | async-start | bytes 1572864 | tf_op jit(solution)/shard_map/all_to_all | solution.py:24
  33.6 32.8 %all-gather = bf16[1600,256]{1,0:T(8,128)(2,1)S(1)} all-gather(bf16[200,256]{1,0:T(8,128)(2,1)S(1)} %bitcast.71), channel_id=2, replica_groups=mesh['y'=8,'x'=4,'zl'=4,'co'=2,'zh'=2] {'zh','zl'}, dimensions={0}, use_global_device_ids=true | all-gather | bytes 921600 | tf_op jit(solution)/shard_map/all_gather | solution.py:146
  66.4 1.9 %collective-permute-start.3 = (bf16[8,200,256]{2,1,0:T(8,128)(2,1)S(1)}, bf16[8,200,256]{2,1,0:T(8,128)(2,1)S(1)}, u32[]{:S(2)}, u32[]{:S(2)}) collective-permute-start(bf16[8,200,256]{2,1,0:T(8,128)(2,1)S(1)} %bitcast.64), channel_id=1, source_target_pairs={{0,2},{2,0},{1,3},{3,1},{4,6},{6,4},{5,7},{7,5},{8,10},{10,8},{9,1... | collective-permute-start | bytes 2457608 | tf_op jit(solution)/shard_map/ppermute | solution.py:45
  69.4 1.2 collective-permute-done.3.other
  71.1 1.7 broadcast_in_dim.15.shift
  72.8 2.5 %norm.1 = (bf16[16,200,256]{2,1,0:T(8,128)(2,1)S(1)}, f32[8,256]{1,0:T(8,128)S(1)}) custom-call(s32[2]{0:T(128)S(1)} %pad_add_fusion.at, bf16[8,200,256]{2,1,0:T(8,128)(2,1)S(1)} %bitcast.65, bf16[8,200,256]{2,1,0:T(8,128)(2,1)S(1)} %collective-permute-done.3.other, f32[16,200,128]{2,1,0:T(8,128)S(1)} %broadcast_in_dim.13.gain, ...), custom_call_target="tpu_custom_call" | custom-call | tf_op jit(solution)/shard_map/norm/pallas_call | solution.py:151
  75.3 1.2 copy-done
  76.4 2.5 %gather_fusion = bf16[256,512]{1,0:T(8,128)(2,1)S(1)} fusion(bf16[768,512]{1,0:T(8,128)(2,1)} %bitcast.10, s32[1024]{0:T(1024)S(1)} %pad_clamp_fusion), kind=kCustom, calls=%fused_computation | custom fusion | bytes 525312 | tf_op jit(solution)/shard_map/gather | solution.py:170
  78.9 4.2 %convolution_convert_fusion = bf16[3200,512]{1,0:T(8,128)(2,1)} fusion(bf16[3200,256]{1,0:T(8,128)(2,1)} %bitcast.67, bf16[256,512]{1,0:T(8,128)(2,1)S(1)} %gather_fusion), kind=kOutput, calls=%fused_computation.2 | convolution fusion | flops 840499200 | bytes 5177344 | tf_op jit(solution)/shard_map/dot_general | solution.py:172
  83.2 4.7 %part.1 = (bf16[8,208,256]{2,1,0:T(8,128)(2,1)S(1)}, bf16[8,208,256]{2,1,0:T(8,128)(2,1)}) custom-call(s32[2]{0:T(128)S(1)} %pad_add_fusion.at, bf16[16,200,512]{2,1,0:T(8,128)(2,1)} %bitcast.69, bf16[256,512]{1,0:T(8,128)(2,1)S(1)} %gather_fusion, bf16[8,200,256]{2,1,0:T(8,128)(2,1)S(1)} %bitcast.66, bf16[8,200,256]{2,1,0:T(8,128)(2,1)S(1)} %collective-permute-done.3.other, ...), custom_call_target="tpu_custom_call" | custom-call | tf_op jit(solution)/shard_map/part/pallas_call | solution.py:176
  88.7 2.0 %collective-permute-start.4 = (bf16[8,208,256]{2,1,0:T(8,128)(2,1)}, bf16[8,208,256]{2,1,0:T(8,128)(2,1)S(1)}, u32[]{:S(2)}, u32[]{:S(2)}) collective-permute-start(bf16[8,208,256]{2,1,0:T(8,128)(2,1)} %get-tuple-element.29), channel_id=1, source_target_pairs={{0,2},{2,0},{1,3},{3,1},{4,6},{6,4},{5,7},{7,5},{8,10},{10,8},{9,1... | collective-permute-start | bytes 2555912 | tf_op jit(solution)/shard_map/ppermute | solution.py:45
  91.8 2.7 %scatter_custom_fusion = bf16[768,512]{1,0:T(8,128)(2,1)} fusion(s32[256]{0:T(256)} %bitcast.80, bf16[256,512]{1,0:T(8,128)(2,1)S(1)} %convolution_convert_fusion.1, bf16[]{:T(256)} %constant.62.clone.1), kind=kCustom, calls=%fused_computation.4 | custom fusion | bytes 786944 | tf_op jit(solution)/shard_map/scatter | solution.py:192
  94.6 9.8 %all-to-all-start.1 = ((bf16[32,24,512]{2,1,0:T(8,128)(2,1)}), bf16[32,24,512]{2,1,0:T(8,128)(2,1)S(1)}, u32[]{:S(2)}, u32[]{:S(2)}) async-start(bf16[32,24,512]{2,1,0:T(8,128)(2,1)} %bitcast.19), calls=%async_computation.2 | async-start | bytes 1572864 | tf_op jit(solution)/shard_map/all_to_all | solution.py:24
  105.2 8.2 %collective-permute-start.10 = (bf16[208,256]{1,0:T(8,128)(2,1)S(1)}, bf16[208,256]{1,0:T(8,128)(2,1)S(1)}, u32[]{:S(2)}, u32[]{:S(2)}) collective-permute-start(bf16[208,256]{1,0:T(8,128)(2,1)S(1)} %get-tuple-element.36), channel_id=1, source_target_pairs={{0,9},{4,13},{8,0},{12,4},{1,8},{5,12},{9,1},{13,5},{2,11},{6,15},... | collective-permute-start | bytes 319496 | tf_op jit(solution)/shard_map/ppermute | solution.py:41
  113.4 2.5 %collective-permute-start.11 = (bf16[208,256]{1,0:T(8,128)(2,1)S(1)}, bf16[208,256]{1,0:T(8,128)(2,1)S(1)}, u32[]{:S(2)}, u32[]{:S(2)}) collective-permute-start(bf16[208,256]{1,0:T(8,128)(2,1)S(1)} %get-tuple-element.37), channel_id=1, source_target_pairs={{0,13},{4,0},{8,4},{12,8},{1,12},{5,1},{9,5},{13,9},{2,15},{6,2},{... | collective-permute-start | bytes 319496 | tf_op jit(solution)/shard_map/ppermute | solution.py:41
  116.7 3.4 %collective-permute-start.5 = (bf16[208,256]{1,0:T(8,128)(2,1)S(1)}, bf16[208,256]{1,0:T(8,128)(2,1)S(1)}, u32[]{:S(2)}, u32[]{:S(2)}) collective-permute-start(bf16[208,256]{1,0:T(8,128)(2,1)S(1)} %get-tuple-element.31), channel_id=1, source_target_pairs={{0,4},{4,8},{8,12},{12,1},{1,5},{5,9},{9,13},{13,0},{2,6},{6,10},{... | collective-permute-start | bytes 319496 | tf_op jit(solution)/shard_map/ppermute | solution.py:41
  120.1 2.8 %collective-permute-start.6 = (bf16[208,256]{1,0:T(8,128)(2,1)S(1)}, bf16[208,256]{1,0:T(8,128)(2,1)S(1)}, u32[]{:S(2)}, u32[]{:S(2)}) collective-permute-start(bf16[208,256]{1,0:T(8,128)(2,1)S(1)} %get-tuple-element.32), channel_id=1, source_target_pairs={{0,8},{4,12},{8,1},{12,5},{1,9},{5,13},{9,0},{13,4},{2,10},{6,14},... | collective-permute-start | bytes 319496 | tf_op jit(solution)/shard_map/ppermute | solution.py:41
  122.9 2.4 %collective-permute-start.7 = (bf16[208,256]{1,0:T(8,128)(2,1)S(1)}, bf16[208,256]{1,0:T(8,128)(2,1)S(1)}, u32[]{:S(2)}, u32[]{:S(2)}) collective-permute-start(bf16[208,256]{1,0:T(8,128)(2,1)S(1)} %get-tuple-element.33), channel_id=1, source_target_pairs={{0,12},{4,1},{8,5},{12,9},{1,13},{5,0},{9,4},{13,8},{2,14},{6,3},{... | collective-permute-start | bytes 319496 | tf_op jit(solution)/shard_map/ppermute | solution.py:41
  125.4 7.9 %collective-permute-start.8 = (bf16[208,256]{1,0:T(8,128)(2,1)S(1)}, bf16[208,256]{1,0:T(8,128)(2,1)S(1)}, u32[]{:S(2)}, u32[]{:S(2)}) collective-permute-start(bf16[208,256]{1,0:T(8,128)(2,1)S(1)} %get-tuple-element.34), channel_id=1, source_target_pairs={{0,1},{4,5},{8,9},{12,13},{1,0},{5,4},{9,8},{13,12},{2,3},{6,7},{1... | collective-permute-start | bytes 319496 | tf_op jit(solution)/shard_map/ppermute | solution.py:41
  133.3 2.4 %collective-permute-start.9 = (bf16[208,256]{1,0:T(8,128)(2,1)S(1)}, bf16[208,256]{1,0:T(8,128)(2,1)S(1)}, u32[]{:S(2)}, u32[]{:S(2)}) collective-permute-start(bf16[208,256]{1,0:T(8,128)(2,1)S(1)} %get-tuple-element.35), channel_id=1, source_target_pairs={{0,5},{4,9},{8,13},{12,0},{1,4},{5,8},{9,12},{13,1},{2,7},{6,11},{... | collective-permute-start | bytes 319496 | tf_op jit(solution)/shard_map/ppermute | solution.py:41
  135.8 3.5 %collective-permute-done.8 = bf16[208,256]{1,0:T(8,128)(2,1)S(1)} collective-permute-done((bf16[208,256]{1,0:T(8,128)(2,1)S(1)}, bf16[208,256]{1,0:T(8,128)(2,1)S(1)}, u32[]{:S(2)}, u32[]{:S(2)}) %collective-permute-start.8) | collective-permute-done | bytes 106528 | tf_op jit(solution)/shard_map/ppermute | solution.py:41
  139.3 4.6 %collective-permute-done.9 = bf16[208,256]{1,0:T(8,128)(2,1)S(1)} collective-permute-done((bf16[208,256]{1,0:T(8,128)(2,1)S(1)}, bf16[208,256]{1,0:T(8,128)(2,1)S(1)}, u32[]{:S(2)}, u32[]{:S(2)}) %collective-permute-start.9) | collective-permute-done | bytes 106528 | tf_op jit(solution)/shard_map/ppermute | solution.py:41
  144.9 8.5 %reduce-scatter.2.cloned.1.call-done = bf16[400,512]{1,0:T(8,128)(2,1)} async-done(((bf16[3200,512]{1,0:T(8,128)(2,1)}), bf16[400,512]{1,0:T(8,128)(2,1)}) %reduce-scatter.2.cloned.1.call-update) | async-done | bytes 409616 | tf_op jit(solution)/shard_map/reduce_scatter | solution.py:173
  155.2 8.8 %all-to-all-start.2 = ((f32[32,1,400]{2,1,0:T(1,128)}), f32[32,1,400]{2,1,0:T(1,128)S(1)}, u32[]{:S(2)}, u32[]{:S(2)}) async-start(f32[32,1,400]{2,1,0:T(1,128)} %broadcast_in_dim.33), calls=%async_computation.3 | async-start | bytes 131072 | tf_op jit(solution)/shard_map/all_to_all | solution.py:24
  164.0 2.1 %collective-permute-start.12 = (bf16[100,512]{1,0:T(8,128)(2,1)S(1)}, bf16[100,512]{1,0:T(8,128)(2,1)S(1)}, u32[]{:S(2)}, u32[]{:S(2)}) collective-permute-start(bf16[100,512]{1,0:T(8,128)(2,1)S(1)} %get-tuple-element.45), channel_id=1, source_target_pairs={{0,16},{16,32},{32,48},{48,0},{1,17},{17,33},{33,49},{49,1},{2,18}... | collective-permute-start | bytes 307208 | tf_op jit(solution)/shard_map/ppermute | solution.py:34
  166.1 4.6 %collective-permute-start.13 = (bf16[100,512]{1,0:T(8,128)(2,1)S(1)}, bf16[100,512]{1,0:T(8,128)(2,1)S(1)}, u32[]{:S(2)}, u32[]{:S(2)}) collective-permute-start(bf16[100,512]{1,0:T(8,128)(2,1)S(1)} %get-tuple-element.47), channel_id=1, source_target_pairs={{0,32},{16,48},{32,0},{48,16},{1,33},{17,49},{33,1},{49,17},{2,34}... | collective-permute-start | bytes 307208 | tf_op jit(solution)/shard_map/ppermute | solution.py:34
  170.7 1.9 %collective-permute-start.14 = (bf16[100,512]{1,0:T(8,128)(2,1)S(1)}, bf16[100,512]{1,0:T(8,128)(2,1)S(1)}, u32[]{:S(2)}, u32[]{:S(2)}) collective-permute-start(bf16[100,512]{1,0:T(8,128)(2,1)S(1)} %get-tuple-element.46), channel_id=1, source_target_pairs={{0,48},{16,0},{32,16},{48,32},{1,49},{17,1},{33,17},{49,33},{2,50}... | collective-permute-start | bytes 307208 | tf_op jit(solution)/shard_map/ppermute | solution.py:34
  174.3 4.3 %collective-permute-done.14 = bf16[100,512]{1,0:T(8,128)(2,1)S(1)} collective-permute-done((bf16[100,512]{1,0:T(8,128)(2,1)S(1)}, bf16[100,512]{1,0:T(8,128)(2,1)S(1)}, u32[]{:S(2)}, u32[]{:S(2)}) %collective-permute-start.14) | collective-permute-done | bytes 102432 | tf_op jit(solution)/shard_map/ppermute | solution.py:34
  (76 shorter events, 14.1 us)
Async XLA Ops:
  7.2 76.0 %all-gather.3.cloned.1.call-start = ((), (), s32[]{:S(2)}) async-start(), calls=%async_computation.5 | async-start | bytes 3686400 | tf_op jit(solution)/shard_map/all_gather | solution.py:141
  7.2 14.0 %collective-permute-start = (bf16[100,512]{1,0:T(8,128)(2,1)}, bf16[100,512]{1,0:T(8,128)(2,1)S(1)}, u32[]{:S(2)}, u32[]{:S(2)}) collective-permute-start(bf16[100,512]{1,0:T(8,128)(2,1)} %param.9), channel_id=1, source_target_pairs={{0,48},{16,0},{32,16},{48,32},{1,49},{17,1},{33,17},{49,33},{2,50}... | collective-permute-start | bytes 307208 | tf_op jit(solution)/shard_map/ppermute | solution.py:34
  10.0 11.3 %collective-permute-start.1 = (bf16[100,512]{1,0:T(8,128)(2,1)}, bf16[100,512]{1,0:T(8,128)(2,1)S(1)}, u32[]{:S(2)}, u32[]{:S(2)}) collective-permute-start(bf16[100,512]{1,0:T(8,128)(2,1)} %param.9), channel_id=1, source_target_pairs={{0,32},{16,48},{32,0},{48,16},{1,33},{17,49},{33,1},{49,17},{2,34}... | collective-permute-start | bytes 307208 | tf_op jit(solution)/shard_map/ppermute | solution.py:34
  18.4 6.8 %collective-permute-start.2 = (bf16[100,512]{1,0:T(8,128)(2,1)}, bf16[100,512]{1,0:T(8,128)(2,1)S(1)}, u32[]{:S(2)}, u32[]{:S(2)}) collective-permute-start(bf16[100,512]{1,0:T(8,128)(2,1)} %param.9), channel_id=1, source_target_pairs={{0,16},{16,32},{32,48},{48,0},{1,17},{17,33},{33,49},{49,1},{2,18}... | collective-permute-start | bytes 307208 | tf_op jit(solution)/shard_map/ppermute | solution.py:34
  26.1 7.2 %copy-start.7 = (f32[3200]{0:T(1024)S(1)}, f32[3200]{0:T(1024)}, u32[]{:S(2)}) copy-start(f32[3200]{0:T(1024)} %param.7) | copy-start | bytes 38404
  26.2 7.3 %copy-start.8 = (f32[3200]{0:T(1024)S(1)}, f32[3200]{0:T(1024)}, u32[]{:S(2)}) copy-start(f32[3200]{0:T(1024)} %param.8) | copy-start | bytes 38404
  26.2 7.4 %copy-start.5 = (bf16[256,200]{0,1:T(8,128)(2,1)S(1)}, bf16[256,200]{0,1:T(8,128)(2,1)}, u32[]{:S(2)}) copy-start(bf16[256,200]{0,1:T(8,128)(2,1)} %param.6) | copy-start | bytes 307204
  27.0 41.3 %copy-start.9 = (s32[256,1]{0,1:T(1,128)S(1)}, s32[256,1]{0,1:T(1,128)}, u32[]{:S(2)}) copy-start(s32[256,1]{0,1:T(1,128)} %param.10) | copy-start | bytes 3076
  27.1 49.4 %all-to-all-start = ((bf16[32,24,512]{2,1,0:T(8,128)(2,1)}), bf16[32,24,512]{2,1,0:T(8,128)(2,1)}, u32[]{:S(2)}, u32[]{:S(2)}) async-start(bf16[32,24,512]{2,1,0:T(8,128)(2,1)} %bitcast.9), calls=%async_computation | async-start | bytes 1572864 | tf_op jit(solution)/shard_map/all_to_all | solution.py:24
  33.3 120.1 %reduce-scatter.2.cloned.1.call-start = ((), (), s32[]{:S(2)}) async-start(), calls=%async_computation.4 | async-start | bytes 3686400 | tf_op jit(solution)/shard_map/reduce_scatter | solution.py:173
  66.4 4.2 %collective-permute-start.3 = (bf16[8,200,256]{2,1,0:T(8,128)(2,1)S(1)}, bf16[8,200,256]{2,1,0:T(8,128)(2,1)S(1)}, u32[]{:S(2)}, u32[]{:S(2)}) collective-permute-start(bf16[8,200,256]{2,1,0:T(8,128)(2,1)S(1)} %bitcast.64), channel_id=1, source_target_pairs={{0,2},{2,0},{1,3},{3,1},{4,6},{6,4},{5,7},{7,5},{8,10},{10,8},{9,1... | collective-permute-start | bytes 2457608 | tf_op jit(solution)/shard_map/ppermute | solution.py:45
  69.3 3.4 %copy-start.10 = (s32[256,1]{0,1:T(1,128)}, s32[256,1]{0,1:T(1,128)S(1)}, u32[]{:S(2)}) copy-start(s32[256,1]{0,1:T(1,128)S(1)} %compare_select_fusion) | copy-start | bytes 3076
  75.2 1.2 copy-start
  83.1 7.6 %copy-start.1 = (bf16[16,200,256]{2,1,0:T(8,128)(2,1)S(1)}, bf16[16,200,256]{2,1,0:T(8,128)(2,1)}, u32[]{:S(2)}) copy-start(bf16[16,200,256]{2,1,0:T(8,128)(2,1)} %copy-done) | copy-start | bytes 4915204
  83.1 7.6 %copy-start.4 = (bf16[3200,512]{1,0:T(8,128)(2,1)S(1)}, bf16[3200,512]{1,0:T(8,128)(2,1)}, u32[]{:S(2)}) copy-start(bf16[3200,512]{1,0:T(8,128)(2,1)} %all-gather.3.cloned.1.call-done) | copy-start | bytes 9830404
  87.8 0.9 copy-start.2
  88.7 15.7 %collective-permute-start.4 = (bf16[8,208,256]{2,1,0:T(8,128)(2,1)}, bf16[8,208,256]{2,1,0:T(8,128)(2,1)S(1)}, u32[]{:S(2)}, u32[]{:S(2)}) collective-permute-start(bf16[8,208,256]{2,1,0:T(8,128)(2,1)} %get-tuple-element.29), channel_id=1, source_target_pairs={{0,2},{2,0},{1,3},{3,1},{4,6},{6,4},{5,7},{7,5},{8,10},{10,8},{9,1... | collective-permute-start | bytes 2555912 | tf_op jit(solution)/shard_map/ppermute | solution.py:45
  91.8 12.6 %copy-start.3 = (bf16[8,208,256]{2,1,0:T(8,128)(2,1)S(1)}, bf16[8,208,256]{2,1,0:T(8,128)(2,1)}, u32[]{:S(2)}) copy-start(bf16[8,208,256]{2,1,0:T(8,128)(2,1)} %copy-done.2) | copy-start | bytes 2555908
  94.6 59.9 %all-to-all-start.1 = ((bf16[32,24,512]{2,1,0:T(8,128)(2,1)}), bf16[32,24,512]{2,1,0:T(8,128)(2,1)S(1)}, u32[]{:S(2)}, u32[]{:S(2)}) async-start(bf16[32,24,512]{2,1,0:T(8,128)(2,1)} %bitcast.19), calls=%async_computation.2 | async-start | bytes 1572864 | tf_op jit(solution)/shard_map/all_to_all | solution.py:24
  104.4 39.6 %copy-start.6 = (bf16[256,200]{0,1:T(8,128)(2,1)S(1)}, bf16[256,200]{0,1:T(8,128)(2,1)}, u32[]{:S(2)}) copy-start(bf16[256,200]{0,1:T(8,128)(2,1)} %param.6) | copy-start | bytes 307204
  105.2 20.2 %collective-permute-start.10 = (bf16[208,256]{1,0:T(8,128)(2,1)S(1)}, bf16[208,256]{1,0:T(8,128)(2,1)S(1)}, u32[]{:S(2)}, u32[]{:S(2)}) collective-permute-start(bf16[208,256]{1,0:T(8,128)(2,1)S(1)} %get-tuple-element.36), channel_id=1, source_target_pairs={{0,9},{4,13},{8,0},{12,4},{1,8},{5,12},{9,1},{13,5},{2,11},{6,15},... | collective-permute-start | bytes 319496 | tf_op jit(solution)/shard_map/ppermute | solution.py:41
  113.4 19.8 %collective-permute-start.11 = (bf16[208,256]{1,0:T(8,128)(2,1)S(1)}, bf16[208,256]{1,0:T(8,128)(2,1)S(1)}, u32[]{:S(2)}, u32[]{:S(2)}) collective-permute-start(bf16[208,256]{1,0:T(8,128)(2,1)S(1)} %get-tuple-element.37), channel_id=1, source_target_pairs={{0,13},{4,0},{8,4},{12,8},{1,12},{5,1},{9,5},{13,9},{2,15},{6,2},{... | collective-permute-start | bytes 319496 | tf_op jit(solution)/shard_map/ppermute | solution.py:41
  116.7 19.0 %collective-permute-start.5 = (bf16[208,256]{1,0:T(8,128)(2,1)S(1)}, bf16[208,256]{1,0:T(8,128)(2,1)S(1)}, u32[]{:S(2)}, u32[]{:S(2)}) collective-permute-start(bf16[208,256]{1,0:T(8,128)(2,1)S(1)} %get-tuple-element.31), channel_id=1, source_target_pairs={{0,4},{4,8},{8,12},{12,1},{1,5},{5,9},{9,13},{13,0},{2,6},{6,10},{... | collective-permute-start | bytes 319496 | tf_op jit(solution)/shard_map/ppermute | solution.py:41
  120.1 15.7 %collective-permute-start.6 = (bf16[208,256]{1,0:T(8,128)(2,1)S(1)}, bf16[208,256]{1,0:T(8,128)(2,1)S(1)}, u32[]{:S(2)}, u32[]{:S(2)}) collective-permute-start(bf16[208,256]{1,0:T(8,128)(2,1)S(1)} %get-tuple-element.32), channel_id=1, source_target_pairs={{0,8},{4,12},{8,1},{12,5},{1,9},{5,13},{9,0},{13,4},{2,10},{6,14},... | collective-permute-start | bytes 319496 | tf_op jit(solution)/shard_map/ppermute | solution.py:41
  122.9 12.8 %collective-permute-start.7 = (bf16[208,256]{1,0:T(8,128)(2,1)S(1)}, bf16[208,256]{1,0:T(8,128)(2,1)S(1)}, u32[]{:S(2)}, u32[]{:S(2)}) collective-permute-start(bf16[208,256]{1,0:T(8,128)(2,1)S(1)} %get-tuple-element.33), channel_id=1, source_target_pairs={{0,12},{4,1},{8,5},{12,9},{1,13},{5,0},{9,4},{13,8},{2,14},{6,3},{... | collective-permute-start | bytes 319496 | tf_op jit(solution)/shard_map/ppermute | solution.py:41
  125.4 13.9 %collective-permute-start.8 = (bf16[208,256]{1,0:T(8,128)(2,1)S(1)}, bf16[208,256]{1,0:T(8,128)(2,1)S(1)}, u32[]{:S(2)}, u32[]{:S(2)}) collective-permute-start(bf16[208,256]{1,0:T(8,128)(2,1)S(1)} %get-tuple-element.34), channel_id=1, source_target_pairs={{0,1},{4,5},{8,9},{12,13},{1,0},{5,4},{9,8},{13,12},{2,3},{6,7},{1... | collective-permute-start | bytes 319496 | tf_op jit(solution)/shard_map/ppermute | solution.py:41
  133.3 10.6 %collective-permute-start.9 = (bf16[208,256]{1,0:T(8,128)(2,1)S(1)}, bf16[208,256]{1,0:T(8,128)(2,1)S(1)}, u32[]{:S(2)}, u32[]{:S(2)}) collective-permute-start(bf16[208,256]{1,0:T(8,128)(2,1)S(1)} %get-tuple-element.35), channel_id=1, source_target_pairs={{0,5},{4,9},{8,13},{12,0},{1,4},{5,8},{9,12},{13,1},{2,7},{6,11},{... | collective-permute-start | bytes 319496 | tf_op jit(solution)/shard_map/ppermute | solution.py:41
  155.2 17.5 %all-to-all-start.2 = ((f32[32,1,400]{2,1,0:T(1,128)}), f32[32,1,400]{2,1,0:T(1,128)S(1)}, u32[]{:S(2)}, u32[]{:S(2)}) async-start(f32[32,1,400]{2,1,0:T(1,128)} %broadcast_in_dim.33), calls=%async_computation.3 | async-start | bytes 131072 | tf_op jit(solution)/shard_map/all_to_all | solution.py:24
  164.0 9.4 %collective-permute-start.12 = (bf16[100,512]{1,0:T(8,128)(2,1)S(1)}, bf16[100,512]{1,0:T(8,128)(2,1)S(1)}, u32[]{:S(2)}, u32[]{:S(2)}) collective-permute-start(bf16[100,512]{1,0:T(8,128)(2,1)S(1)} %get-tuple-element.45), channel_id=1, source_target_pairs={{0,16},{16,32},{32,48},{48,0},{1,17},{17,33},{33,49},{49,1},{2,18}... | collective-permute-start | bytes 307208 | tf_op jit(solution)/shard_map/ppermute | solution.py:34
  166.1 8.1 %collective-permute-start.13 = (bf16[100,512]{1,0:T(8,128)(2,1)S(1)}, bf16[100,512]{1,0:T(8,128)(2,1)S(1)}, u32[]{:S(2)}, u32[]{:S(2)}) collective-permute-start(bf16[100,512]{1,0:T(8,128)(2,1)S(1)} %get-tuple-element.47), channel_id=1, source_target_pairs={{0,32},{16,48},{32,0},{48,16},{1,33},{17,49},{33,1},{49,17},{2,34}... | collective-permute-start | bytes 307208 | tf_op jit(solution)/shard_map/ppermute | solution.py:34
  170.7 7.8 %collective-permute-start.14 = (bf16[100,512]{1,0:T(8,128)(2,1)S(1)}, bf16[100,512]{1,0:T(8,128)(2,1)S(1)}, u32[]{:S(2)}, u32[]{:S(2)}) collective-permute-start(bf16[100,512]{1,0:T(8,128)(2,1)S(1)} %get-tuple-element.46), channel_id=1, source_target_pairs={{0,48},{16,0},{32,16},{48,32},{1,49},{17,1},{33,17},{49,33},{2,50}... | collective-permute-start | bytes 307208 | tf_op jit(solution)/shard_map/ppermute | solution.py:34
Sparse Core Ops, SparseCore 0:
  27.2 55.5 all-gather.2
  85.6 67.7 reduce-scatter.1

commit v5 on v4

--- a/solution.py
+++ b/solution.py
@@ -129,6 +129,7 @@
     n_z = n_zl * n_zh
     senders = n_y * n_x
     slice_rows = proj_weight.shape[0]
+    padded_rows = (slice_rows + 2 + 7) // 8 * 8
     most = embed_grad.shape[0] // senders
     blocks = width // own_width
     core, x_at = lax.axis_index("co"), lax.axis_index("x")
@@ -215,20 +216,30 @@
     xhat_own = (own_t.astype(F32) - mean) * inv
     hidden = (inv * (dnormed * gain_own - plain - xhat_own * cross)).astype(BF16).T
     sums = jnp.concatenate([jnp.sum(dnormed * xhat_own, 1), jnp.sum(dnormed, 1)])
-    grad_y, sums = lax.optimization_barrier((grad_y, sums))
     sums, embeds_recv = lax.optimization_barrier((sums, embeds_recv))
-    sums = jnp.sum(copies(sums[None], ENC), (0, 1))
-
-    grad_y = grad_y.reshape(n_x, slice_rows, out_cols)
-
-    def grad_block(step):
-        return lax.dynamic_index_in_dim(grad_y, lax.rem(x_at + step, n_x), 0, keepdims=False)
-
-    grad_weight = sum(
-        [shifted(grad_block(k), "x", k).astype(F32) for k in range(1, n_x)],
-        grad_block(0).astype(F32),
-    )
-    return embeds_recv, hidden, grad_weight, sums[:own_width], sums[own_width:]
+    sums = jnp.sum(copies(sums[None], "y"), (0, 1))
+
+    high = lax.reduce_precision(sums, 8, 7)
+    tail = jnp.stack([high, sums - high]).astype(BF16)
+    tail = jnp.pad(tail, ((0, padded_rows - slice_rows - 2), (0, out_cols - sums.size)))
+    grad_y, tail = lax.optimization_barrier((grad_y, tail))
+    grad_x = jnp.concatenate(
+        [
+            grad_y.reshape(n_x, slice_rows, out_cols),
+            jnp.broadcast_to(tail[None], (n_x, *tail.shape)),
+        ],
+        1,
+    )
+    total = jnp.sum(exchange(grad_x, "x").astype(F32), 0)
+    grad_weight = total[:slice_rows]
+    sums = total[slice_rows] + total[slice_rows + 1]
+    return (
+        embeds_recv,
+        hidden,
+        grad_weight,
+        sums[:own_width],
+        sums[own_width : 2 * own_width],
+    )
 
 
 def solution(mesh):

time: 188 us -> 184 us (0.979)
  blocking collectives: 32.8 us -> 47 us
  starting transfers between devices: 80.1 us -> 69.8 us
  waiting for transfers between devices: 27.1 us -> 19.1 us
    all_to_all x0 -> x1, blocking collectives: none -> 14.2 us  [exchange(): return lax.all_to_all(x, axes, 0, 0, tiled=True)]
    ppermute x6 -> x3, starting transfers between devices: 21.7 us -> 13.1 us  [shifted(): lax.ppermute(x, axes, [(i, (i + step) % count) for i in range(count)])]
    reduce_scatter x1, waiting for transfers between devices: 8.51 us -> 0.02 us  [body(): grad_y = lax.psum_scatter(grad_part, 'y', scatter_dimension=0, tiled=True)]
    all_to_all x3, waiting for transfers between devices: 0.01 us -> 5.5 us  [exchange(): return lax.all_to_all(x, axes, 0, 0, tiled=True)]
    ppermute x6 -> x3, waiting for transfers between devices: 9.09 us -> 4 us  [shifted(): lax.ppermute(x, axes, [(i, (i + step) % count) for i in range(count)])]
    all_to_all x3, starting transfers between devices: 24.8 us -> 21.9 us  [exchange(): return lax.all_to_all(x, axes, 0, 0, tiled=True)]
    unnamed x30 -> x32, local copies, waits for them, and re-layouts: 4.89 us -> 4.87 us
  transfers between devices with their start and end apart: 20 -> 17, of which waited for: 7 -> 6; matrix products, arithmetic and copies ran while one was open for 10% -> 9% of each run, Pallas kernels for 4% -> 4%
where the time goes in v5:
time: 184 us; the launch traced here: 182 us
  starting transfers between devices  69.8 us (38%)
  blocking collectives  47 us (26%)
  waiting for transfers between devices  19.1 us (10%)
  local copies, waits for them, and re-layouts  16 us (9%)
  between operations  14.6 us (8%)
  Pallas kernels  7.84 us (4%)
  matrix products  5.22 us (3%)
  other arithmetic  2.7 us (1%)
    all_gather x1, blocking collectives, body(): mine = lax.all_gather(own_t, ZED, axis=0)  32.8 us
    ppermute x7, starting transfers between devices, along_z(): lax.ppermute(x, ('zl', 'zh'), [(at[z], at[(z + step) % count]) for z in r...  30.8 us
    all_to_all x3, starting transfers between devices, exchange(): return lax.all_to_all(x, axes, 0, 0, tiled=True)  21.9 us
    all_to_all x1, blocking collectives, exchange(): return lax.all_to_all(x, axes, 0, 0, tiled=True)  14.2 us
    ppermute x3, starting transfers between devices, shifted(): lax.ppermute(x, axes, [(i, (i + step) % count) for i in range(count)])  13.1 us
    ppermute x7, waiting for transfers between devices, along_z(): lax.ppermute(x, ('zl', 'zh'), [(at[z], at[(z + step) % count]) for z in r...  8.3 us
    all_to_all x3, waiting for transfers between devices, exchange(): return lax.all_to_all(x, axes, 0, 0, tiled=True)  5.5 us
    unnamed x32, local copies, waits for them, and re-layouts  4.87 us
  transfers between devices with their start and end apart: 17, of which 6 were waited for; matrix products, arithmetic and copies ran while one was open for 9% of the time, Pallas kernels for 4%

profile of v5, /device:TPU:6, one launch (start us, length us, event | category | flops | bytes accessed | tf_op | source)
XLA Modules:
  0.0 182.3 jit_solution(9392372070552031264)
XLA Ops:
  7.2 2.7 %collective-permute-start = (bf16[100,512]{1,0:T(8,128)(2,1)}, bf16[100,512]{1,0:T(8,128)(2,1)S(1)}, u32[]{:S(2)}, u32[]{:S(2)}) collective-permute-start(bf16[100,512]{1,0:T(8,128)(2,1)} %param.9), channel_id=1, source_target_pairs={{0,48},{16,0},{32,16},{48,32},{1,49},{17,1},{33,17},{49,33},{2,50}... | collective-permute-start | bytes 307208 | tf_op jit(solution)/shard_map/ppermute | solution.py:34
  10.0 6.9 %collective-permute-start.2 = (bf16[100,512]{1,0:T(8,128)(2,1)}, bf16[100,512]{1,0:T(8,128)(2,1)S(1)}, u32[]{:S(2)}, u32[]{:S(2)}) collective-permute-start(bf16[100,512]{1,0:T(8,128)(2,1)} %param.9), channel_id=1, source_target_pairs={{0,16},{16,32},{32,48},{48,0},{1,17},{17,33},{33,49},{49,1},{2,18}... | collective-permute-start | bytes 307208 | tf_op jit(solution)/shard_map/ppermute | solution.py:34
  16.9 3.4 %collective-permute-start.1 = (bf16[100,512]{1,0:T(8,128)(2,1)}, bf16[100,512]{1,0:T(8,128)(2,1)S(1)}, u32[]{:S(2)}, u32[]{:S(2)}) collective-permute-start(bf16[100,512]{1,0:T(8,128)(2,1)} %param.9), channel_id=1, source_target_pairs={{0,32},{16,48},{32,0},{48,16},{1,33},{17,49},{33,1},{49,17},{2,34}... | collective-permute-start | bytes 307208 | tf_op jit(solution)/shard_map/ppermute | solution.py:34
  21.2 4.0 %collective-permute-done.1 = bf16[100,512]{1,0:T(8,128)(2,1)S(1)} collective-permute-done((bf16[100,512]{1,0:T(8,128)(2,1)}, bf16[100,512]{1,0:T(8,128)(2,1)S(1)}, u32[]{:S(2)}, u32[]{:S(2)}) %collective-permute-start.1) | collective-permute-done | bytes 102432 | tf_op jit(solution)/shard_map/ppermute | solution.py:34
  27.2 7.4 %all-to-all-start = ((bf16[32,24,512]{2,1,0:T(8,128)(2,1)}), bf16[32,24,512]{2,1,0:T(8,128)(2,1)}, u32[]{:S(2)}, u32[]{:S(2)}) async-start(bf16[32,24,512]{2,1,0:T(8,128)(2,1)} %bitcast.7), calls=%async_computation | async-start | bytes 1572864 | tf_op jit(solution)/shard_map/all_to_all | solution.py:24
  34.8 32.8 %all-gather = bf16[1600,256]{1,0:T(8,128)(2,1)S(1)} all-gather(bf16[200,256]{1,0:T(8,128)(2,1)S(1)} %bitcast.67), channel_id=2, replica_groups=mesh['y'=8,'x'=4,'zl'=4,'co'=2,'zh'=2] {'zh','zl'}, dimensions={0}, use_global_device_ids=true | all-gather | bytes 921600 | tf_op jit(solution)/shard_map/all_gather | solution.py:147
  67.6 1.9 %collective-permute-start.3 = (bf16[8,200,256]{2,1,0:T(8,128)(2,1)S(1)}, bf16[8,200,256]{2,1,0:T(8,128)(2,1)S(1)}, u32[]{:S(2)}, u32[]{:S(2)}) collective-permute-start(bf16[8,200,256]{2,1,0:T(8,128)(2,1)S(1)} %bitcast.60), channel_id=1, source_target_pairs={{0,2},{2,0},{1,3},{3,1},{4,6},{6,4},{5,7},{7,5},{8,10},{10,8},{9,1... | collective-permute-start | bytes 2457608 | tf_op jit(solution)/shard_map/ppermute | solution.py:45
  70.6 1.2 collective-permute-done.3.other
  72.3 1.7 broadcast_in_dim.17.shift
  74.0 2.5 %norm.1 = (bf16[16,200,256]{2,1,0:T(8,128)(2,1)S(1)}, f32[8,256]{1,0:T(8,128)S(1)}) custom-call(s32[2]{0:T(128)S(1)} %pad_add_fusion.at, bf16[8,200,256]{2,1,0:T(8,128)(2,1)S(1)} %bitcast.61, bf16[8,200,256]{2,1,0:T(8,128)(2,1)S(1)} %collective-permute-done.3.other, f32[16,200,128]{2,1,0:T(8,128)S(1)} %broadcast_in_dim.15.gain, ...), custom_call_target="tpu_custom_call" | custom-call | tf_op jit(solution)/shard_map/norm/pallas_call | solution.py:152
  76.5 1.2 copy-done
  77.7 2.5 %gather_fusion = bf16[256,512]{1,0:T(8,128)(2,1)S(1)} fusion(bf16[768,512]{1,0:T(8,128)(2,1)} %bitcast.8, s32[1024]{0:T(1024)S(1)} %pad_clamp_fusion), kind=kCustom, calls=%fused_computation | custom fusion | bytes 525312 | tf_op jit(solution)/shard_map/gather | solution.py:171
  80.1 4.2 %convolution_convert_fusion = bf16[3200,512]{1,0:T(8,128)(2,1)} fusion(bf16[3200,256]{1,0:T(8,128)(2,1)} %bitcast.63, bf16[256,512]{1,0:T(8,128)(2,1)S(1)} %gather_fusion), kind=kOutput, calls=%fused_computation.2 | convolution fusion | flops 840499200 | bytes 5177344 | tf_op jit(solution)/shard_map/dot_general | solution.py:173
  84.4 4.6 %part.1 = (bf16[8,208,256]{2,1,0:T(8,128)(2,1)S(1)}, bf16[8,208,256]{2,1,0:T(8,128)(2,1)}) custom-call(s32[2]{0:T(128)S(1)} %pad_add_fusion.at, bf16[16,200,512]{2,1,0:T(8,128)(2,1)} %bitcast.65, bf16[256,512]{1,0:T(8,128)(2,1)S(1)} %gather_fusion, bf16[8,200,256]{2,1,0:T(8,128)(2,1)S(1)} %bitcast.62, bf16[8,200,256]{2,1,0:T(8,128)(2,1)S(1)} %collective-permute-done.3.other, ...), custom_call_target="tpu_custom_call" | custom-call | tf_op jit(solution)/shard_map/part/pallas_call | solution.py:177
  89.9 2.0 %collective-permute-start.4 = (bf16[8,208,256]{2,1,0:T(8,128)(2,1)}, bf16[8,208,256]{2,1,0:T(8,128)(2,1)S(1)}, u32[]{:S(2)}, u32[]{:S(2)}) collective-permute-start(bf16[8,208,256]{2,1,0:T(8,128)(2,1)} %get-tuple-element.28), channel_id=1, source_target_pairs={{0,2},{2,0},{1,3},{3,1},{4,6},{6,4},{5,7},{7,5},{8,10},{10,8},{9,1... | collective-permute-start | bytes 2555912 | tf_op jit(solution)/shard_map/ppermute | solution.py:45
  92.0 1.1 convolution_convert_fusion.1
  93.0 2.7 %scatter_custom_fusion = bf16[768,512]{1,0:T(8,128)(2,1)} fusion(s32[256]{0:T(256)} %bitcast.78, bf16[256,512]{1,0:T(8,128)(2,1)S(1)} %convolution_convert_fusion.1, bf16[]{:T(256)} %constant.43.clone.1), kind=kCustom, calls=%fused_computation.6 | custom fusion | bytes 786944 | tf_op jit(solution)/shard_map/scatter | solution.py:193
  95.8 9.9 %all-to-all-start.1 = ((bf16[32,24,512]{2,1,0:T(8,128)(2,1)}), bf16[32,24,512]{2,1,0:T(8,128)(2,1)S(1)}, u32[]{:S(2)}, u32[]{:S(2)}) async-start(bf16[32,24,512]{2,1,0:T(8,128)(2,1)} %bitcast.19), calls=%async_computation.1 | async-start | bytes 1572864 | tf_op jit(solution)/shard_map/all_to_all | solution.py:24
  106.4 2.7 %collective-permute-start.5 = (bf16[208,256]{1,0:T(8,128)(2,1)S(1)}, bf16[208,256]{1,0:T(8,128)(2,1)S(1)}, u32[]{:S(2)}, u32[]{:S(2)}) collective-permute-start(bf16[208,256]{1,0:T(8,128)(2,1)S(1)} %get-tuple-element.30), channel_id=1, source_target_pairs={{0,4},{4,8},{8,12},{12,1},{1,5},{5,9},{9,13},{13,0},{2,6},{6,10},{... | collective-permute-start | bytes 319496 | tf_op jit(solution)/shard_map/ppermute | solution.py:41
  109.1 4.9 %collective-permute-start.6 = (bf16[208,256]{1,0:T(8,128)(2,1)S(1)}, bf16[208,256]{1,0:T(8,128)(2,1)S(1)}, u32[]{:S(2)}, u32[]{:S(2)}) collective-permute-start(bf16[208,256]{1,0:T(8,128)(2,1)S(1)} %get-tuple-element.31), channel_id=1, source_target_pairs={{0,8},{4,12},{8,1},{12,5},{1,9},{5,13},{9,0},{13,4},{2,10},{6,14},... | collective-permute-start | bytes 319496 | tf_op jit(solution)/shard_map/ppermute | solution.py:41
  114.8 7.3 %collective-permute-start.7 = (bf16[208,256]{1,0:T(8,128)(2,1)S(1)}, bf16[208,256]{1,0:T(8,128)(2,1)S(1)}, u32[]{:S(2)}, u32[]{:S(2)}) collective-permute-start(bf16[208,256]{1,0:T(8,128)(2,1)S(1)} %get-tuple-element.32), channel_id=1, source_target_pairs={{0,12},{4,1},{8,5},{12,9},{1,13},{5,0},{9,4},{13,8},{2,14},{6,3},{... | collective-permute-start | bytes 319496 | tf_op jit(solution)/shard_map/ppermute | solution.py:41
  122.1 2.8 %collective-permute-start.8 = (bf16[208,256]{1,0:T(8,128)(2,1)S(1)}, bf16[208,256]{1,0:T(8,128)(2,1)S(1)}, u32[]{:S(2)}, u32[]{:S(2)}) collective-permute-start(bf16[208,256]{1,0:T(8,128)(2,1)S(1)} %get-tuple-element.33), channel_id=1, source_target_pairs={{0,1},{4,5},{8,9},{12,13},{1,0},{5,4},{9,8},{13,12},{2,3},{6,7},{1... | collective-permute-start | bytes 319496 | tf_op jit(solution)/shard_map/ppermute | solution.py:41
  125.0 6.9 %collective-permute-start.9 = (bf16[208,256]{1,0:T(8,128)(2,1)S(1)}, bf16[208,256]{1,0:T(8,128)(2,1)S(1)}, u32[]{:S(2)}, u32[]{:S(2)}) collective-permute-start(bf16[208,256]{1,0:T(8,128)(2,1)S(1)} %get-tuple-element.34), channel_id=1, source_target_pairs={{0,5},{4,9},{8,13},{12,0},{1,4},{5,8},{9,12},{13,1},{2,7},{6,11},{... | collective-permute-start | bytes 319496 | tf_op jit(solution)/shard_map/ppermute | solution.py:41
  131.9 3.7 %collective-permute-start.10 = (bf16[208,256]{1,0:T(8,128)(2,1)S(1)}, bf16[208,256]{1,0:T(8,128)(2,1)S(1)}, u32[]{:S(2)}, u32[]{:S(2)}) collective-permute-start(bf16[208,256]{1,0:T(8,128)(2,1)S(1)} %get-tuple-element.35), channel_id=1, source_target_pairs={{0,9},{4,13},{8,0},{12,4},{1,8},{5,12},{9,1},{13,5},{2,11},{6,15},... | collective-permute-start | bytes 319496 | tf_op jit(solution)/shard_map/ppermute | solution.py:41
  135.6 2.5 %collective-permute-start.11 = (bf16[208,256]{1,0:T(8,128)(2,1)S(1)}, bf16[208,256]{1,0:T(8,128)(2,1)S(1)}, u32[]{:S(2)}, u32[]{:S(2)}) collective-permute-start(bf16[208,256]{1,0:T(8,128)(2,1)S(1)} %get-tuple-element.36), channel_id=1, source_target_pairs={{0,13},{4,0},{8,4},{12,8},{1,12},{5,1},{9,5},{13,9},{2,15},{6,2},{... | collective-permute-start | bytes 319496 | tf_op jit(solution)/shard_map/ppermute | solution.py:41
  138.1 4.8 %collective-permute-done.9 = bf16[208,256]{1,0:T(8,128)(2,1)S(1)} collective-permute-done((bf16[208,256]{1,0:T(8,128)(2,1)S(1)}, bf16[208,256]{1,0:T(8,128)(2,1)S(1)}, u32[]{:S(2)}, u32[]{:S(2)}) %collective-permute-start.9) | collective-permute-done | bytes 106528 | tf_op jit(solution)/shard_map/ppermute | solution.py:41
  142.9 1.9 %collective-permute-done.10 = bf16[208,256]{1,0:T(8,128)(2,1)S(1)} collective-permute-done((bf16[208,256]{1,0:T(8,128)(2,1)S(1)}, bf16[208,256]{1,0:T(8,128)(2,1)S(1)}, u32[]{:S(2)}, u32[]{:S(2)}) %collective-permute-start.10) | collective-permute-done | bytes 106528 | tf_op jit(solution)/shard_map/ppermute | solution.py:41
  144.8 1.6 collective-permute-done.11
  147.4 14.2 %all_to_all.20 = f32[8,1,400]{2,1,0:T(1,128)S(1)} all-to-all(f32[8,1,400]{2,1,0:T(1,128)S(1)} %broadcast_in_dim.19), channel_id=1, replica_groups=mesh['y'=8,'x'=4,'zl'=4,'co'=2,'zh'=2] {'y'}, dimensions={0} | all-to-all | bytes 25600 | tf_op jit(solution)/shard_map/all_to_all | solution.py:24
  161.7 1.1 reshape.85
  163.6 4.7 %all-to-all-start.3 = ((bf16[4,104,512]{2,1,0:T(8,128)(2,1)}), bf16[4,104,512]{2,1,0:T(8,128)(2,1)S(1)}, u32[]{:S(2)}, u32[]{:S(2)}) async-start(bf16[4,104,512]{2,1,0:T(8,128)(2,1)} %pad_maximum_fusion), calls=%async_computation.4 | async-start | bytes 851968 | tf_op jit(solution)/shard_map/all_to_all | solution.py:24
  168.3 5.5 %all-to-all-done.3 = bf16[4,104,512]{2,1,0:T(8,128)(2,1)S(1)} async-done(((bf16[4,104,512]{2,1,0:T(8,128)(2,1)}), bf16[4,104,512]{2,1,0:T(8,128)(2,1)S(1)}, u32[]{:S(2)}, u32[]{:S(2)}) %all-to-all-start.3) | async-done | bytes 426016 | tf_op jit(solution)/shard_map/all_to_all | solution.py:24
  (77 shorter events, 10.5 us)
Async XLA Ops:
  7.2 77.2 %all-gather.3.cloned.1.call-start = ((), (), s32[]{:S(2)}) async-start(), calls=%async_computation.5 | async-start | bytes 3686400 | tf_op jit(solution)/shard_map/all_gather | solution.py:142
  7.2 14.0 %collective-permute-start = (bf16[100,512]{1,0:T(8,128)(2,1)}, bf16[100,512]{1,0:T(8,128)(2,1)S(1)}, u32[]{:S(2)}, u32[]{:S(2)}) collective-permute-start(bf16[100,512]{1,0:T(8,128)(2,1)} %param.9), channel_id=1, source_target_pairs={{0,48},{16,0},{32,16},{48,32},{1,49},{17,1},{33,17},{49,33},{2,50}... | collective-permute-start | bytes 307208 | tf_op jit(solution)/shard_map/ppermute | solution.py:34
  10.0 15.3 %collective-permute-start.2 = (bf16[100,512]{1,0:T(8,128)(2,1)}, bf16[100,512]{1,0:T(8,128)(2,1)S(1)}, u32[]{:S(2)}, u32[]{:S(2)}) collective-permute-start(bf16[100,512]{1,0:T(8,128)(2,1)} %param.9), channel_id=1, source_target_pairs={{0,16},{16,32},{32,48},{48,0},{1,17},{17,33},{33,49},{49,1},{2,18}... | collective-permute-start | bytes 307208 | tf_op jit(solution)/shard_map/ppermute | solution.py:34
  16.9 8.3 %collective-permute-start.1 = (bf16[100,512]{1,0:T(8,128)(2,1)}, bf16[100,512]{1,0:T(8,128)(2,1)S(1)}, u32[]{:S(2)}, u32[]{:S(2)}) collective-permute-start(bf16[100,512]{1,0:T(8,128)(2,1)} %param.9), channel_id=1, source_target_pairs={{0,32},{16,48},{32,0},{48,16},{1,33},{17,49},{33,1},{49,17},{2,34}... | collective-permute-start | bytes 307208 | tf_op jit(solution)/shard_map/ppermute | solution.py:34
  26.2 8.4 %copy-start.9 = (f32[3200]{0:T(1024)S(1)}, f32[3200]{0:T(1024)}, u32[]{:S(2)}) copy-start(f32[3200]{0:T(1024)} %param.8) | copy-start | bytes 38404
  26.3 8.4 %copy-start.8 = (f32[3200]{0:T(1024)S(1)}, f32[3200]{0:T(1024)}, u32[]{:S(2)}) copy-start(f32[3200]{0:T(1024)} %param.7) | copy-start | bytes 38404
  26.3 8.5 %copy-start.5 = (bf16[256,200]{0,1:T(8,128)(2,1)S(1)}, bf16[256,200]{0,1:T(8,128)(2,1)}, u32[]{:S(2)}) copy-start(bf16[256,200]{0,1:T(8,128)(2,1)} %param.6) | copy-start | bytes 307204
  27.1 42.4 %copy-start.10 = (s32[256,1]{0,1:T(1,128)S(1)}, s32[256,1]{0,1:T(1,128)}, u32[]{:S(2)}) copy-start(s32[256,1]{0,1:T(1,128)} %param.10) | copy-start | bytes 3076
  27.2 50.5 %all-to-all-start = ((bf16[32,24,512]{2,1,0:T(8,128)(2,1)}), bf16[32,24,512]{2,1,0:T(8,128)(2,1)}, u32[]{:S(2)}, u32[]{:S(2)}) async-start(bf16[32,24,512]{2,1,0:T(8,128)(2,1)} %bitcast.7), calls=%async_computation | async-start | bytes 1572864 | tf_op jit(solution)/shard_map/all_to_all | solution.py:24
  34.5 127.2 %reduce-scatter.2.cloned.1.call-start = ((), (), s32[]{:S(2)}) async-start(), calls=%async_computation.6 | async-start | bytes 3686400 | tf_op jit(solution)/shard_map/reduce_scatter | solution.py:174
  67.6 4.2 %collective-permute-start.3 = (bf16[8,200,256]{2,1,0:T(8,128)(2,1)S(1)}, bf16[8,200,256]{2,1,0:T(8,128)(2,1)S(1)}, u32[]{:S(2)}, u32[]{:S(2)}) collective-permute-start(bf16[8,200,256]{2,1,0:T(8,128)(2,1)S(1)} %bitcast.60), channel_id=1, source_target_pairs={{0,2},{2,0},{1,3},{3,1},{4,6},{6,4},{5,7},{7,5},{8,10},{10,8},{9,1... | collective-permute-start | bytes 2457608 | tf_op jit(solution)/shard_map/ppermute | solution.py:45
  70.6 3.4 %copy-start.11 = (s32[256,1]{0,1:T(1,128)}, s32[256,1]{0,1:T(1,128)S(1)}, u32[]{:S(2)}) copy-start(s32[256,1]{0,1:T(1,128)S(1)} %compare_select_fusion) | copy-start | bytes 3076
  76.5 1.2 copy-start
  84.3 7.6 %copy-start.1 = (bf16[16,200,256]{2,1,0:T(8,128)(2,1)S(1)}, bf16[16,200,256]{2,1,0:T(8,128)(2,1)}, u32[]{:S(2)}) copy-start(bf16[16,200,256]{2,1,0:T(8,128)(2,1)} %copy-done) | copy-start | bytes 4915204
  84.4 7.6 %copy-start.4 = (bf16[3200,512]{1,0:T(8,128)(2,1)S(1)}, bf16[3200,512]{1,0:T(8,128)(2,1)}, u32[]{:S(2)}) copy-start(bf16[3200,512]{1,0:T(8,128)(2,1)} %all-gather.3.cloned.1.call-done) | copy-start | bytes 9830404
  89.0 0.9 copy-start.2
  89.9 15.7 %collective-permute-start.4 = (bf16[8,208,256]{2,1,0:T(8,128)(2,1)}, bf16[8,208,256]{2,1,0:T(8,128)(2,1)S(1)}, u32[]{:S(2)}, u32[]{:S(2)}) collective-permute-start(bf16[8,208,256]{2,1,0:T(8,128)(2,1)} %get-tuple-element.28), channel_id=1, source_target_pairs={{0,2},{2,0},{1,3},{3,1},{4,6},{6,4},{5,7},{7,5},{8,10},{10,8},{9,1... | collective-permute-start | bytes 2555912 | tf_op jit(solution)/shard_map/ppermute | solution.py:45
  93.0 12.6 %copy-start.3 = (bf16[8,208,256]{2,1,0:T(8,128)(2,1)S(1)}, bf16[8,208,256]{2,1,0:T(8,128)(2,1)}, u32[]{:S(2)}) copy-start(bf16[8,208,256]{2,1,0:T(8,128)(2,1)} %copy-done.2) | copy-start | bytes 2555908
  95.8 51.6 %all-to-all-start.1 = ((bf16[32,24,512]{2,1,0:T(8,128)(2,1)}), bf16[32,24,512]{2,1,0:T(8,128)(2,1)S(1)}, u32[]{:S(2)}, u32[]{:S(2)}) async-start(bf16[32,24,512]{2,1,0:T(8,128)(2,1)} %bitcast.19), calls=%async_computation.1 | async-start | bytes 1572864 | tf_op jit(solution)/shard_map/all_to_all | solution.py:24
  105.6 40.9 %copy-start.6 = (bf16[256,200]{0,1:T(8,128)(2,1)S(1)}, bf16[256,200]{0,1:T(8,128)(2,1)}, u32[]{:S(2)}) copy-start(bf16[256,200]{0,1:T(8,128)(2,1)} %param.6) | copy-start | bytes 307204
  106.4 25.5 %collective-permute-start.5 = (bf16[208,256]{1,0:T(8,128)(2,1)S(1)}, bf16[208,256]{1,0:T(8,128)(2,1)S(1)}, u32[]{:S(2)}, u32[]{:S(2)}) collective-permute-start(bf16[208,256]{1,0:T(8,128)(2,1)S(1)} %get-tuple-element.30), channel_id=1, source_target_pairs={{0,4},{4,8},{8,12},{12,1},{1,5},{5,9},{9,13},{13,0},{2,6},{6,10},{... | collective-permute-start | bytes 319496 | tf_op jit(solution)/shard_map/ppermute | solution.py:41
  109.1 26.5 %collective-permute-start.6 = (bf16[208,256]{1,0:T(8,128)(2,1)S(1)}, bf16[208,256]{1,0:T(8,128)(2,1)S(1)}, u32[]{:S(2)}, u32[]{:S(2)}) collective-permute-start(bf16[208,256]{1,0:T(8,128)(2,1)S(1)} %get-tuple-element.31), channel_id=1, source_target_pairs={{0,8},{4,12},{8,1},{12,5},{1,9},{5,13},{9,0},{13,4},{2,10},{6,14},... | collective-permute-start | bytes 319496 | tf_op jit(solution)/shard_map/ppermute | solution.py:41
  114.8 23.3 %collective-permute-start.7 = (bf16[208,256]{1,0:T(8,128)(2,1)S(1)}, bf16[208,256]{1,0:T(8,128)(2,1)S(1)}, u32[]{:S(2)}, u32[]{:S(2)}) collective-permute-start(bf16[208,256]{1,0:T(8,128)(2,1)S(1)} %get-tuple-element.32), channel_id=1, source_target_pairs={{0,12},{4,1},{8,5},{12,9},{1,13},{5,0},{9,4},{13,8},{2,14},{6,3},{... | collective-permute-start | bytes 319496 | tf_op jit(solution)/shard_map/ppermute | solution.py:41
  122.1 16.0 %collective-permute-start.8 = (bf16[208,256]{1,0:T(8,128)(2,1)S(1)}, bf16[208,256]{1,0:T(8,128)(2,1)S(1)}, u32[]{:S(2)}, u32[]{:S(2)}) collective-permute-start(bf16[208,256]{1,0:T(8,128)(2,1)S(1)} %get-tuple-element.33), channel_id=1, source_target_pairs={{0,1},{4,5},{8,9},{12,13},{1,0},{5,4},{9,8},{13,12},{2,3},{6,7},{1... | collective-permute-start | bytes 319496 | tf_op jit(solution)/shard_map/ppermute | solution.py:41
  125.0 17.9 %collective-permute-start.9 = (bf16[208,256]{1,0:T(8,128)(2,1)S(1)}, bf16[208,256]{1,0:T(8,128)(2,1)S(1)}, u32[]{:S(2)}, u32[]{:S(2)}) collective-permute-start(bf16[208,256]{1,0:T(8,128)(2,1)S(1)} %get-tuple-element.34), channel_id=1, source_target_pairs={{0,5},{4,9},{8,13},{12,0},{1,4},{5,8},{9,12},{13,1},{2,7},{6,11},{... | collective-permute-start | bytes 319496 | tf_op jit(solution)/shard_map/ppermute | solution.py:41
  131.9 12.9 %collective-permute-start.10 = (bf16[208,256]{1,0:T(8,128)(2,1)S(1)}, bf16[208,256]{1,0:T(8,128)(2,1)S(1)}, u32[]{:S(2)}, u32[]{:S(2)}) collective-permute-start(bf16[208,256]{1,0:T(8,128)(2,1)S(1)} %get-tuple-element.35), channel_id=1, source_target_pairs={{0,9},{4,13},{8,0},{12,4},{1,8},{5,12},{9,1},{13,5},{2,11},{6,15},... | collective-permute-start | bytes 319496 | tf_op jit(solution)/shard_map/ppermute | solution.py:41
  135.6 10.8 %collective-permute-start.11 = (bf16[208,256]{1,0:T(8,128)(2,1)S(1)}, bf16[208,256]{1,0:T(8,128)(2,1)S(1)}, u32[]{:S(2)}, u32[]{:S(2)}) collective-permute-start(bf16[208,256]{1,0:T(8,128)(2,1)S(1)} %get-tuple-element.36), channel_id=1, source_target_pairs={{0,13},{4,0},{8,4},{12,8},{1,12},{5,1},{9,5},{13,9},{2,15},{6,2},{... | collective-permute-start | bytes 319496 | tf_op jit(solution)/shard_map/ppermute | solution.py:41
  163.6 10.2 %all-to-all-start.3 = ((bf16[4,104,512]{2,1,0:T(8,128)(2,1)}), bf16[4,104,512]{2,1,0:T(8,128)(2,1)S(1)}, u32[]{:S(2)}, u32[]{:S(2)}) async-start(bf16[4,104,512]{2,1,0:T(8,128)(2,1)} %pad_maximum_fusion), calls=%async_computation.4 | async-start | bytes 851968 | tf_op jit(solution)/shard_map/all_to_all | solution.py:24
  173.9 1.5 copy-start.7
Sparse Core Ops, SparseCore 0:
  27.3 56.6 all-gather.2
  86.8 67.7 reduce-scatter.1

commit v6 on v5

--- a/solution.py
+++ b/solution.py
@@ -49,8 +49,10 @@
     return (z % n_zl) * (2 * n_zh) + core * n_zh + z // n_zl
 
 
-def wide(column, rows):
-    return jnp.concatenate([column] * (rows // column.shape[1]), 1)
+def column(table, z, owner, n_zl, n_zh):
+    first = block_of(z, 0, n_zl, n_zh)
+    second = block_of(z, 1, n_zl, n_zh)
+    return jnp.where(owner == 0, table[:, first : first + 1], table[:, second : second + 1])
 
 
 def norm_kernel(n_zl, n_zh, at, mine, other, gain, shift, normed, stats):
@@ -75,7 +77,9 @@
     for i in range(n_z):
         for ref, owner in ((mine, core), (other, 1 - core)):
             b = block_of(i, owner, n_zl, n_zh)
-            value = (ref[i].astype(F32) - mean) * inv * wide(gain[b], rows) + wide(shift[b], rows)
+            scale = column(gain, i, owner, n_zl, n_zh)
+            offset = column(shift, i, owner, n_zl, n_zh)
+            value = (ref[i].astype(F32) - mean) * inv * scale + offset
             normed[b] = value.astype(BF16)
 
 
@@ -99,7 +103,7 @@
                 weight[b], d_embed[...], (((1,), (1,)), ((), ())), preferred_element_type=F32
             ).astype(BF16)
             out[i, 0:own_width, :] = part
-            scaled = part.astype(F32) * wide(gain[b], rows)
+            scaled = part.astype(F32) * column(gain, i, owner, n_zl, n_zh)
             xhat = (source[i].astype(F32) - mean) * inv
             plain = plain + jnp.sum(scaled, 0, keepdims=True)
             cross = cross + jnp.sum(scaled * xhat, 0, keepdims=True)
@@ -132,23 +136,20 @@
     padded_rows = (slice_rows + 2 + 7) // 8 * 8
     most = embed_grad.shape[0] // senders
     blocks = width // own_width
-    core, x_at = lax.axis_index("co"), lax.axis_index("x")
+    core = lax.axis_index("co")
     at = jnp.stack([core, lax.axis_index(ZED)]).astype(jnp.int32)
 
-    weight_rel = [proj_weight] + [shifted(proj_weight, "x", k) for k in range(1, n_x)]
-    ordered = jnp.stack([weight_rel[-i % n_x] for i in range(n_x)] * 2)
-    weight_x = lax.dynamic_slice_in_dim(ordered, lax.rem(n_x - x_at, n_x), n_x, 0)
-    weight_x = weight_x.reshape(n_x * slice_rows, out_cols)
+    weight_x = copies(proj_weight, "x").reshape(n_x * slice_rows, out_cols)
     weight = lax.all_gather(weight_x, "y", axis=0, tiled=True)
 
+    embed_grad, _ = lax.optimization_barrier((embed_grad, weight_x))
     returned = exchange(embed_grad.reshape(senders, most, out_cols), ENC)
     own_t = patches.T
     own_t, _ = lax.optimization_barrier((own_t, weight_x))
     mine = lax.all_gather(own_t, ZED, axis=0)
     other = core_swap(mine)
 
-    gain_wide = jnp.broadcast_to(gain.reshape(blocks, own_width, 1), (blocks, own_width, 128))
-    shift_wide = jnp.broadcast_to(shift.reshape(blocks, own_width, 1), (blocks, own_width, 128))
+    gain_t, shift_t = gain.reshape(blocks, own_width).T, shift.reshape(blocks, own_width).T
     normed, stats = pl.pallas_call(
         functools.partial(norm_kernel, n_zl, n_zh),
         out_shape=(
@@ -159,7 +160,7 @@
         out_specs=(VMEM,) * 2,
         compiler_params=PARAMS,
         name="norm",
-    )(at, mine, other, gain_wide, shift_wide)
+    )(at, mine, other, gain_t, shift_t)
     mean, inv = stats[0], stats[1]
     normed = normed.reshape(width, rows)
 
@@ -182,7 +183,7 @@
         compiler_params=PARAMS,
         name="part",
     )(
-        at, weight.reshape(blocks, own_width, out_cols), d_embed, mine, other, gain_wide, stats
+        at, weight.reshape(blocks, own_width, out_cols), d_embed, mine, other, gain_t, stats
     )
     recv = core_swap(send)
 

time: 184 us -> 182 us (0.989)
  blocking collectives: 47 us -> 60.7 us
  starting transfers between devices: 69.8 us -> 57.1 us
  local copies, waits for them, and re-layouts: 16 us -> 12.7 us
    all_to_all x1 -> x2, blocking collectives: 14.2 us -> 27.9 us  [exchange(): return lax.all_to_all(x, axes, 0, 0, tiled=True)]
    ppermute x3 -> x0, starting transfers between devices: 13.1 us -> none  [shifted(): lax.ppermute(x, axes, [(i, (i + step) % count) for i in range(count)])]
    all_gather x1, waiting for transfers between devices: 0.02 us -> 4.21 us  [body(): weight = lax.all_gather(weight_x, 'y', axis=0, tiled=True)]
    ppermute x3 -> x0, waiting for transfers between devices: 4 us -> none  [shifted(): lax.ppermute(x, axes, [(i, (i + step) % count) for i in range(count)])]
    ppermute x7, starting transfers between devices: 30.8 us -> 33.5 us  [along_z(): lax.ppermute(x, ('zl', 'zh'), [(at[z], at[(z + step) % count]) for z in r...]
    broadcast_in_dim x4 -> x0, local copies, waits for them, and re-layouts: 2.36 us -> none  [the longest x2 1.78 us: body(): jnp.broadcast_to(shift.reshape(blocks, own_width, 1), (blocks, own_width,...]
    all_to_all x3, starting transfers between devices: 21.9 us -> 19.6 us  [exchange(): return lax.all_to_all(x, axes, 0, 0, tiled=True)]
    unnamed x32 -> x25, local copies, waits for them, and re-layouts: 4.87 us -> 2.76 us
  transfers between devices with their start and end apart: 17 -> 14, of which waited for: 6 -> 6; matrix products, arithmetic and copies ran while one was open for 9% -> 7% of each run, Pallas kernels for 4% -> 5%
where the time goes in v6:
time: 182 us; the launch traced here: 180 us
  blocking collectives  60.7 us (33%)
  starting transfers between devices  57.1 us (31%)
  waiting for transfers between devices  19.1 us (10%)
  between operations  14.5 us (8%)
  local copies, waits for them, and re-layouts  12.7 us (7%)
  Pallas kernels  9.15 us (5%)
  matrix products  3.76 us (2%)
  other arithmetic  2.71 us (1%)
    ppermute x7, starting transfers between devices, along_z(): lax.ppermute(x, ('zl', 'zh'), [(at[z], at[(z + step) % count]) for z in r...  33.5 us
    all_gather x1, blocking collectives, body(): mine = lax.all_gather(own_t, ZED, axis=0)  32.9 us
    all_to_all x2, blocking collectives, exchange(): return lax.all_to_all(x, axes, 0, 0, tiled=True)  27.9 us
    all_to_all x3, starting transfers between devices, exchange(): return lax.all_to_all(x, axes, 0, 0, tiled=True)  19.6 us
    ppermute x7, waiting for transfers between devices, along_z(): lax.ppermute(x, ('zl', 'zh'), [(at[z], at[(z + step) % count]) for z in r...  8.33 us
    all_to_all x3, waiting for transfers between devices, exchange(): return lax.all_to_all(x, axes, 0, 0, tiled=True)  5.5 us
    pallas_call x1, Pallas kernels, body(): pl.pallas_call(functools.partial(part_kernel, n_zl, n_zh), out_shape=(hal...  4.79 us
    all_gather x1, waiting for transfers between devices, body(): weight = lax.all_gather(weight_x, 'y', axis=0, tiled=True)  4.21 us
  transfers between devices with their start and end apart: 14, of which 6 were waited for; matrix products, arithmetic and copies ran while one was open for 7% of the time, Pallas kernels for 5%

profile of v6, /device:TPU:6, one launch (start us, length us, event | category | flops | bytes accessed | tf_op | source)
XLA Modules:
  0.0 179.7 jit_solution(14030326554975309844)
XLA Ops:
  7.3 0.9 broadcast_in_dim.8
  8.2 13.7 %all_to_all.25 = bf16[4,100,512]{2,1,0:T(8,128)(2,1)S(1)} all-to-all(bf16[4,100,512]{2,1,0:T(8,128)(2,1)S(1)} %broadcast_in_dim.8), channel_id=1, replica_groups=mesh['y'=8,'x'=4,'zl'=4,'co'=2,'zh'=2] {'x'}, dimensions={0} | all-to-all | bytes 819200 | tf_op jit(solution)/shard_map/all_to_all | solution.py:24
  22.7 7.2 %all-to-all-start.1 = ((bf16[32,24,512]{2,1,0:T(8,128)(2,1)}), bf16[32,24,512]{2,1,0:T(8,128)(2,1)}, u32[]{:S(2)}, u32[]{:S(2)}) async-start(bf16[32,24,512]{2,1,0:T(8,128)(2,1)} %bitcast.60), calls=%async_computation.1 | async-start | bytes 1572864 | tf_op jit(solution)/shard_map/all_to_all | solution.py:24
  30.3 32.9 %all-gather = bf16[1600,256]{1,0:T(8,128)(2,1)S(1)} all-gather(bf16[200,256]{1,0:T(8,128)(2,1)S(1)} %bitcast.61), channel_id=2, replica_groups=mesh['y'=8,'x'=4,'zl'=4,'co'=2,'zh'=2] {'zh','zl'}, dimensions={0}, use_global_device_ids=true | all-gather | bytes 921600 | tf_op jit(solution)/shard_map/all_gather | solution.py:149
  63.1 1.9 %collective-permute-start = (bf16[8,200,256]{2,1,0:T(8,128)(2,1)S(1)}, bf16[8,200,256]{2,1,0:T(8,128)(2,1)S(1)}, u32[]{:S(2)}, u32[]{:S(2)}) collective-permute-start(bf16[8,200,256]{2,1,0:T(8,128)(2,1)S(1)} %bitcast.50), channel_id=1, source_target_pairs={{0,2},{2,0},{1,3},{3,1},{4,6},{6,4},{5,7},{7,5},{8,10},{10,8},{9,1... | collective-permute-start | bytes 2457608 | tf_op jit(solution)/shard_map/ppermute | solution.py:45
  66.3 1.0 collective-permute-done.other
  67.3 3.0 %norm.1 = (bf16[16,200,256]{2,1,0:T(8,128)(2,1)S(1)}, f32[8,256]{1,0:T(8,128)S(1)}) custom-call(s32[2]{0:T(128)S(1)} %pad_add_fusion.at, bf16[8,200,256]{2,1,0:T(8,128)(2,1)S(1)} %bitcast.51, bf16[8,200,256]{2,1,0:T(8,128)(2,1)S(1)} %collective-permute-done.other, f32[200,16]{1,0:T(8,128)S(1)} %bitcast.55, f32[200,16]{1,0:T(8,128)S(1)} %bitcast.57), custom_call_target="tpu_custom_call" | custom-call | tf_op jit(solution)/shard_map/norm/pallas_call | solution.py:153
  70.4 2.4 %gather_fusion = bf16[256,512]{1,0:T(8,128)(2,1)S(1)} fusion(bf16[768,512]{1,0:T(8,128)(2,1)} %bitcast.4, s32[1024]{0:T(1024)S(1)} %pad_clamp_fusion), kind=kCustom, calls=%fused_computation | custom fusion | bytes 525312 | tf_op jit(solution)/shard_map/gather | solution.py:172
  72.8 2.7 %convolution_convert_fusion = bf16[3200,512]{1,0:T(8,128)(2,1)} fusion(bf16[3200,256]{1,0:T(8,128)(2,1)S(1)} %bitcast.53, bf16[256,512]{1,0:T(8,128)(2,1)S(1)} %gather_fusion), kind=kOutput, calls=%fused_computation.2 | convolution fusion | flops 840499200 | bytes 5177344 | tf_op jit(solution)/shard_map/dot_general | solution.py:174
  75.5 4.2 %all-gather.3.cloned.1.call-done = bf16[3200,512]{1,0:T(8,128)(2,1)} async-done(((bf16[400,512]{1,0:T(8,128)(2,1)}), bf16[3200,512]{1,0:T(8,128)(2,1)}) %all-gather.3.cloned.1.call-update) | async-done | bytes 3276816 | tf_op jit(solution)/shard_map/all_gather | solution.py:143
  79.8 0.9 copy-done.1
  80.6 4.8 %part.1 = (bf16[8,208,256]{2,1,0:T(8,128)(2,1)S(1)}, bf16[8,208,256]{2,1,0:T(8,128)(2,1)}) custom-call(s32[2]{0:T(128)S(1)} %pad_add_fusion.at, bf16[16,200,512]{2,1,0:T(8,128)(2,1)} %bitcast.58, bf16[256,512]{1,0:T(8,128)(2,1)S(1)} %gather_fusion, bf16[8,200,256]{2,1,0:T(8,128)(2,1)S(1)} %bitcast.52, bf16[8,200,256]{2,1,0:T(8,128)(2,1)S(1)} %collective-permute-done.other, ...), custom_call_target="tpu_custom_call" | custom-call | tf_op jit(solution)/shard_map/part/pallas_call | solution.py:178
  85.4 0.9 copy-done.2
  86.4 1.9 %collective-permute-start.1 = (bf16[8,208,256]{2,1,0:T(8,128)(2,1)}, bf16[8,208,256]{2,1,0:T(8,128)(2,1)}, u32[]{:S(2)}, u32[]{:S(2)}) collective-permute-start(bf16[8,208,256]{2,1,0:T(8,128)(2,1)} %get-tuple-element.30), channel_id=1, source_target_pairs={{0,2},{2,0},{1,3},{3,1},{4,6},{6,4},{5,7},{7,5},{8,10},{10,8},{9,1... | collective-permute-start | bytes 2555912 | tf_op jit(solution)/shard_map/ppermute | solution.py:45
  88.3 1.1 convolution_convert_fusion.1
  89.4 2.6 %scatter_custom_fusion = bf16[768,512]{1,0:T(8,128)(2,1)} fusion(s32[256]{0:T(256)} %bitcast.72, bf16[256,512]{1,0:T(8,128)(2,1)S(1)} %convolution_convert_fusion.1, bf16[]{:T(256)} %constant.34.clone.1), kind=kCustom, calls=%fused_computation.6 | custom fusion | bytes 786944 | tf_op jit(solution)/shard_map/scatter | solution.py:194
  92.0 7.6 %all-to-all-start.2 = ((bf16[32,24,512]{2,1,0:T(8,128)(2,1)}), bf16[32,24,512]{2,1,0:T(8,128)(2,1)S(1)}, u32[]{:S(2)}, u32[]{:S(2)}) async-start(bf16[32,24,512]{2,1,0:T(8,128)(2,1)} %bitcast.17), calls=%async_computation.2 | async-start | bytes 1572864 | tf_op jit(solution)/shard_map/all_to_all | solution.py:24
  99.6 1.4 pair.1
  101.0 4.3 %collective-permute-start.2 = (bf16[208,256]{1,0:T(8,128)(2,1)S(1)}, bf16[208,256]{1,0:T(8,128)(2,1)S(1)}, u32[]{:S(2)}, u32[]{:S(2)}) collective-permute-start(bf16[208,256]{1,0:T(8,128)(2,1)S(1)} %get-tuple-element.32), channel_id=1, source_target_pairs={{0,4},{4,8},{8,12},{12,1},{1,5},{5,9},{9,13},{13,0},{2,6},{6,10},{... | collective-permute-start | bytes 319496 | tf_op jit(solution)/shard_map/ppermute | solution.py:41
  105.3 6.1 %collective-permute-start.3 = (bf16[208,256]{1,0:T(8,128)(2,1)S(1)}, bf16[208,256]{1,0:T(8,128)(2,1)S(1)}, u32[]{:S(2)}, u32[]{:S(2)}) collective-permute-start(bf16[208,256]{1,0:T(8,128)(2,1)S(1)} %get-tuple-element.33), channel_id=1, source_target_pairs={{0,8},{4,12},{8,1},{12,5},{1,9},{5,13},{9,0},{13,4},{2,10},{6,14},... | collective-permute-start | bytes 319496 | tf_op jit(solution)/shard_map/ppermute | solution.py:41
  112.2 7.3 %collective-permute-start.4 = (bf16[208,256]{1,0:T(8,128)(2,1)S(1)}, bf16[208,256]{1,0:T(8,128)(2,1)S(1)}, u32[]{:S(2)}, u32[]{:S(2)}) collective-permute-start(bf16[208,256]{1,0:T(8,128)(2,1)S(1)} %get-tuple-element.34), channel_id=1, source_target_pairs={{0,12},{4,1},{8,5},{12,9},{1,13},{5,0},{9,4},{13,8},{2,14},{6,3},{... | collective-permute-start | bytes 319496 | tf_op jit(solution)/shard_map/ppermute | solution.py:41
  119.5 2.8 %collective-permute-start.5 = (bf16[208,256]{1,0:T(8,128)(2,1)S(1)}, bf16[208,256]{1,0:T(8,128)(2,1)S(1)}, u32[]{:S(2)}, u32[]{:S(2)}) collective-permute-start(bf16[208,256]{1,0:T(8,128)(2,1)S(1)} %get-tuple-element.35), channel_id=1, source_target_pairs={{0,1},{4,5},{8,9},{12,13},{1,0},{5,4},{9,8},{13,12},{2,3},{6,7},{1... | collective-permute-start | bytes 319496 | tf_op jit(solution)/shard_map/ppermute | solution.py:41
  122.3 6.9 %collective-permute-start.6 = (bf16[208,256]{1,0:T(8,128)(2,1)S(1)}, bf16[208,256]{1,0:T(8,128)(2,1)S(1)}, u32[]{:S(2)}, u32[]{:S(2)}) collective-permute-start(bf16[208,256]{1,0:T(8,128)(2,1)S(1)} %get-tuple-element.36), channel_id=1, source_target_pairs={{0,5},{4,9},{8,13},{12,0},{1,4},{5,8},{9,12},{13,1},{2,7},{6,11},{... | collective-permute-start | bytes 319496 | tf_op jit(solution)/shard_map/ppermute | solution.py:41
  129.3 3.7 %collective-permute-start.7 = (bf16[208,256]{1,0:T(8,128)(2,1)S(1)}, bf16[208,256]{1,0:T(8,128)(2,1)S(1)}, u32[]{:S(2)}, u32[]{:S(2)}) collective-permute-start(bf16[208,256]{1,0:T(8,128)(2,1)S(1)} %get-tuple-element.37), channel_id=1, source_target_pairs={{0,9},{4,13},{8,0},{12,4},{1,8},{5,12},{9,1},{13,5},{2,11},{6,15},... | collective-permute-start | bytes 319496 | tf_op jit(solution)/shard_map/ppermute | solution.py:41
  133.0 2.5 %collective-permute-start.8 = (bf16[208,256]{1,0:T(8,128)(2,1)S(1)}, bf16[208,256]{1,0:T(8,128)(2,1)S(1)}, u32[]{:S(2)}, u32[]{:S(2)}) collective-permute-start(bf16[208,256]{1,0:T(8,128)(2,1)S(1)} %get-tuple-element.38), channel_id=1, source_target_pairs={{0,13},{4,0},{8,4},{12,8},{1,12},{5,1},{9,5},{13,9},{2,15},{6,2},{... | collective-permute-start | bytes 319496 | tf_op jit(solution)/shard_map/ppermute | solution.py:41
  135.5 4.8 %collective-permute-done.6 = bf16[208,256]{1,0:T(8,128)(2,1)S(1)} collective-permute-done((bf16[208,256]{1,0:T(8,128)(2,1)S(1)}, bf16[208,256]{1,0:T(8,128)(2,1)S(1)}, u32[]{:S(2)}, u32[]{:S(2)}) %collective-permute-start.6) | collective-permute-done | bytes 106528 | tf_op jit(solution)/shard_map/ppermute | solution.py:41
  140.3 1.9 %collective-permute-done.7 = bf16[208,256]{1,0:T(8,128)(2,1)S(1)} collective-permute-done((bf16[208,256]{1,0:T(8,128)(2,1)S(1)}, bf16[208,256]{1,0:T(8,128)(2,1)S(1)}, u32[]{:S(2)}, u32[]{:S(2)}) %collective-permute-start.7) | collective-permute-done | bytes 106528 | tf_op jit(solution)/shard_map/ppermute | solution.py:41
  142.2 1.6 collective-permute-done.8
  144.8 14.2 %all_to_all.26 = f32[8,1,400]{2,1,0:T(1,128)S(1)} all-to-all(f32[8,1,400]{2,1,0:T(1,128)S(1)} %broadcast_in_dim.10), channel_id=1, replica_groups=mesh['y'=8,'x'=4,'zl'=4,'co'=2,'zh'=2] {'y'}, dimensions={0} | all-to-all | bytes 25600 | tf_op jit(solution)/shard_map/all_to_all | solution.py:24
  159.1 1.1 reshape.90
  160.9 4.8 %all-to-all-start.4 = ((bf16[4,104,512]{2,1,0:T(8,128)(2,1)}), bf16[4,104,512]{2,1,0:T(8,128)(2,1)S(1)}, u32[]{:S(2)}, u32[]{:S(2)}) async-start(bf16[4,104,512]{2,1,0:T(8,128)(2,1)} %pad_maximum_fusion), calls=%async_computation.5 | async-start | bytes 851968 | tf_op jit(solution)/shard_map/all_to_all | solution.py:24
  165.7 5.5 %all-to-all-done.4 = bf16[4,104,512]{2,1,0:T(8,128)(2,1)S(1)} async-done(((bf16[4,104,512]{2,1,0:T(8,128)(2,1)}), bf16[4,104,512]{2,1,0:T(8,128)(2,1)S(1)}, u32[]{:S(2)}, u32[]{:S(2)}) %all-to-all-start.4) | async-done | bytes 426016 | tf_op jit(solution)/shard_map/all_to_all | solution.py:24
  (64 shorter events, 6.6 us)
Async XLA Ops:
  7.2 22.9 %copy-start.9 = (f32[3200]{0:T(1024)S(1)}, f32[3200]{0:T(1024)}, u32[]{:S(2)}) copy-start(f32[3200]{0:T(1024)} %param.8) | copy-start | bytes 38404
  7.2 23.0 %copy-start.8 = (f32[3200]{0:T(1024)S(1)}, f32[3200]{0:T(1024)}, u32[]{:S(2)}) copy-start(f32[3200]{0:T(1024)} %param.7) | copy-start | bytes 38404
  7.2 23.1 %copy-start.5 = (bf16[256,200]{0,1:T(8,128)(2,1)S(1)}, bf16[256,200]{0,1:T(8,128)(2,1)}, u32[]{:S(2)}) copy-start(bf16[256,200]{0,1:T(8,128)(2,1)} %param.6) | copy-start | bytes 307204
  7.2 57.8 %copy-start.10 = (s32[256,1]{0,1:T(1,128)S(1)}, s32[256,1]{0,1:T(1,128)}, u32[]{:S(2)}) copy-start(s32[256,1]{0,1:T(1,128)} %param.10) | copy-start | bytes 3076
  7.2 72.5 %all-gather.3.cloned.1.call-start = ((), (), s32[]{:S(2)}) async-start(), calls=%async_computation.6 | async-start | bytes 3686400 | tf_op jit(solution)/shard_map/all_gather | solution.py:143
  22.7 47.6 %all-to-all-start.1 = ((bf16[32,24,512]{2,1,0:T(8,128)(2,1)}), bf16[32,24,512]{2,1,0:T(8,128)(2,1)}, u32[]{:S(2)}, u32[]{:S(2)}) async-start(bf16[32,24,512]{2,1,0:T(8,128)(2,1)} %bitcast.60), calls=%async_computation.1 | async-start | bytes 1572864 | tf_op jit(solution)/shard_map/all_to_all | solution.py:24
  30.0 129.1 %reduce-scatter.2.cloned.1.call-start = ((), (), s32[]{:S(2)}) async-start(), calls=%async_computation.7 | async-start | bytes 3686400 | tf_op jit(solution)/shard_map/reduce_scatter | solution.py:175
  63.1 4.2 %collective-permute-start = (bf16[8,200,256]{2,1,0:T(8,128)(2,1)S(1)}, bf16[8,200,256]{2,1,0:T(8,128)(2,1)S(1)}, u32[]{:S(2)}, u32[]{:S(2)}) collective-permute-start(bf16[8,200,256]{2,1,0:T(8,128)(2,1)S(1)} %bitcast.50), channel_id=1, source_target_pairs={{0,2},{2,0},{1,3},{3,1},{4,6},{6,4},{5,7},{7,5},{8,10},{10,8},{9,1... | collective-permute-start | bytes 2457608 | tf_op jit(solution)/shard_map/ppermute | solution.py:45
  66.0 4.4 %copy-start = (f32[16,200]{0,1:T(8,128)}, f32[16,200]{0,1:T(8,128)S(1)}, u32[]{:S(2)}) copy-start(f32[16,200]{0,1:T(8,128)S(1)} %copy.18) | copy-start | bytes 38404
  66.3 4.1 %copy-start.11 = (s32[256,1]{0,1:T(1,128)}, s32[256,1]{0,1:T(1,128)S(1)}, u32[]{:S(2)}) copy-start(s32[256,1]{0,1:T(1,128)S(1)} %compare_select_fusion) | copy-start | bytes 3076
  79.8 0.9 copy-start.1
  80.6 7.7 %copy-start.4 = (bf16[3200,512]{1,0:T(8,128)(2,1)S(1)}, bf16[3200,512]{1,0:T(8,128)(2,1)}, u32[]{:S(2)}) copy-start(bf16[3200,512]{1,0:T(8,128)(2,1)} %all-gather.3.cloned.1.call-done) | copy-start | bytes 9830404
  85.4 0.9 copy-start.2
  86.4 13.3 %collective-permute-start.1 = (bf16[8,208,256]{2,1,0:T(8,128)(2,1)}, bf16[8,208,256]{2,1,0:T(8,128)(2,1)}, u32[]{:S(2)}, u32[]{:S(2)}) collective-permute-start(bf16[8,208,256]{2,1,0:T(8,128)(2,1)} %get-tuple-element.30), channel_id=1, source_target_pairs={{0,2},{2,0},{1,3},{3,1},{4,6},{6,4},{5,7},{7,5},{8,10},{10,8},{9,1... | collective-permute-start | bytes 2555912 | tf_op jit(solution)/shard_map/ppermute | solution.py:45
  88.3 11.3 %copy-start.3 = (bf16[8,208,256]{2,1,0:T(8,128)(2,1)S(1)}, bf16[8,208,256]{2,1,0:T(8,128)(2,1)}, u32[]{:S(2)}) copy-start(bf16[8,208,256]{2,1,0:T(8,128)(2,1)} %copy-done.2) | copy-start | bytes 2555908
  89.4 54.5 %copy-start.6 = (bf16[256,200]{0,1:T(8,128)(2,1)S(1)}, bf16[256,200]{0,1:T(8,128)(2,1)}, u32[]{:S(2)}) copy-start(bf16[256,200]{0,1:T(8,128)(2,1)} %param.6) | copy-start | bytes 307204
  92.0 52.8 %all-to-all-start.2 = ((bf16[32,24,512]{2,1,0:T(8,128)(2,1)}), bf16[32,24,512]{2,1,0:T(8,128)(2,1)S(1)}, u32[]{:S(2)}, u32[]{:S(2)}) async-start(bf16[32,24,512]{2,1,0:T(8,128)(2,1)} %bitcast.17), calls=%async_computation.2 | async-start | bytes 1572864 | tf_op jit(solution)/shard_map/all_to_all | solution.py:24
  101.0 28.3 %collective-permute-start.2 = (bf16[208,256]{1,0:T(8,128)(2,1)S(1)}, bf16[208,256]{1,0:T(8,128)(2,1)S(1)}, u32[]{:S(2)}, u32[]{:S(2)}) collective-permute-start(bf16[208,256]{1,0:T(8,128)(2,1)S(1)} %get-tuple-element.32), channel_id=1, source_target_pairs={{0,4},{4,8},{8,12},{12,1},{1,5},{5,9},{9,13},{13,0},{2,6},{6,10},{... | collective-permute-start | bytes 319496 | tf_op jit(solution)/shard_map/ppermute | solution.py:41
  105.3 27.7 %collective-permute-start.3 = (bf16[208,256]{1,0:T(8,128)(2,1)S(1)}, bf16[208,256]{1,0:T(8,128)(2,1)S(1)}, u32[]{:S(2)}, u32[]{:S(2)}) collective-permute-start(bf16[208,256]{1,0:T(8,128)(2,1)S(1)} %get-tuple-element.33), channel_id=1, source_target_pairs={{0,8},{4,12},{8,1},{12,5},{1,9},{5,13},{9,0},{13,4},{2,10},{6,14},... | collective-permute-start | bytes 319496 | tf_op jit(solution)/shard_map/ppermute | solution.py:41
  112.2 23.3 %collective-permute-start.4 = (bf16[208,256]{1,0:T(8,128)(2,1)S(1)}, bf16[208,256]{1,0:T(8,128)(2,1)S(1)}, u32[]{:S(2)}, u32[]{:S(2)}) collective-permute-start(bf16[208,256]{1,0:T(8,128)(2,1)S(1)} %get-tuple-element.34), channel_id=1, source_target_pairs={{0,12},{4,1},{8,5},{12,9},{1,13},{5,0},{9,4},{13,8},{2,14},{6,3},{... | collective-permute-start | bytes 319496 | tf_op jit(solution)/shard_map/ppermute | solution.py:41
  119.5 15.9 %collective-permute-start.5 = (bf16[208,256]{1,0:T(8,128)(2,1)S(1)}, bf16[208,256]{1,0:T(8,128)(2,1)S(1)}, u32[]{:S(2)}, u32[]{:S(2)}) collective-permute-start(bf16[208,256]{1,0:T(8,128)(2,1)S(1)} %get-tuple-element.35), channel_id=1, source_target_pairs={{0,1},{4,5},{8,9},{12,13},{1,0},{5,4},{9,8},{13,12},{2,3},{6,7},{1... | collective-permute-start | bytes 319496 | tf_op jit(solution)/shard_map/ppermute | solution.py:41
  122.3 17.9 %collective-permute-start.6 = (bf16[208,256]{1,0:T(8,128)(2,1)S(1)}, bf16[208,256]{1,0:T(8,128)(2,1)S(1)}, u32[]{:S(2)}, u32[]{:S(2)}) collective-permute-start(bf16[208,256]{1,0:T(8,128)(2,1)S(1)} %get-tuple-element.36), channel_id=1, source_target_pairs={{0,5},{4,9},{8,13},{12,0},{1,4},{5,8},{9,12},{13,1},{2,7},{6,11},{... | collective-permute-start | bytes 319496 | tf_op jit(solution)/shard_map/ppermute | solution.py:41
  129.3 12.9 %collective-permute-start.7 = (bf16[208,256]{1,0:T(8,128)(2,1)S(1)}, bf16[208,256]{1,0:T(8,128)(2,1)S(1)}, u32[]{:S(2)}, u32[]{:S(2)}) collective-permute-start(bf16[208,256]{1,0:T(8,128)(2,1)S(1)} %get-tuple-element.37), channel_id=1, source_target_pairs={{0,9},{4,13},{8,0},{12,4},{1,8},{5,12},{9,1},{13,5},{2,11},{6,15},... | collective-permute-start | bytes 319496 | tf_op jit(solution)/shard_map/ppermute | solution.py:41
  133.0 10.8 %collective-permute-start.8 = (bf16[208,256]{1,0:T(8,128)(2,1)S(1)}, bf16[208,256]{1,0:T(8,128)(2,1)S(1)}, u32[]{:S(2)}, u32[]{:S(2)}) collective-permute-start(bf16[208,256]{1,0:T(8,128)(2,1)S(1)} %get-tuple-element.38), channel_id=1, source_target_pairs={{0,13},{4,0},{8,4},{12,8},{1,12},{5,1},{9,5},{13,9},{2,15},{6,2},{... | collective-permute-start | bytes 319496 | tf_op jit(solution)/shard_map/ppermute | solution.py:41
  160.9 10.3 %all-to-all-start.4 = ((bf16[4,104,512]{2,1,0:T(8,128)(2,1)}), bf16[4,104,512]{2,1,0:T(8,128)(2,1)S(1)}, u32[]{:S(2)}, u32[]{:S(2)}) async-start(bf16[4,104,512]{2,1,0:T(8,128)(2,1)} %pad_maximum_fusion), calls=%async_computation.5 | async-start | bytes 851968 | tf_op jit(solution)/shard_map/all_to_all | solution.py:24
  171.3 1.5 copy-start.7
Sparse Core Ops, SparseCore 0:
  22.9 56.8 all-gather.2
  82.6 67.8 reduce-scatter.1

commit v7 on v6

--- a/solution.py
+++ b/solution.py
@@ -27,11 +27,6 @@
 def copies(x, axes):
     count = lax.axis_size(axes)
     return exchange(jnp.broadcast_to(x[None], (count, *x.shape)), axes)
-
-
-def shifted(x, axes, step):
-    count = lax.axis_size(axes)
-    return lax.ppermute(x, axes, [(i, (i + step) % count) for i in range(count)])
 
 
 def along_z(x, step):
@@ -113,14 +108,32 @@
         send[i, own_width:, :] = tail
 
 
-def pair_kernel(at, keep, recv, *outs):
+def add_blocks(first, second):
+    own_width = first.shape[0] - EXTRA
+    a, b = first.astype(F32), second.astype(F32)
+    tail = a[own_width:] + b[own_width:]
+    return (a[:own_width] + b[:own_width]).astype(BF16), high_low(
+        tail[0:1] + tail[1:2], tail[2:3] + tail[3:4]
+    )
+
+
+def pair_kernel(at, keep, recv, own, away):
     n_z, own_width = keep.shape[0], keep.shape[1] - EXTRA
-    tail = keep[0, own_width:, :].astype(F32) + recv[0, own_width:, :].astype(F32)
-    tail = high_low(tail[0:1] + tail[1:2], tail[2:3] + tail[3:4])
-    for k, out in enumerate(outs):
-        i = lax.rem(at[1] + k, n_z)
-        pair = keep[i, 0:own_width, :].astype(F32) + recv[i, 0:own_width, :].astype(F32)
-        out[0:own_width, :] = pair.astype(BF16)
+    z = at[1]
+    neighbour = z + 1 - 2 * lax.rem(z, 2)
+    for out, start in ((own, z), (away, neighbour)):
+        for j in range(n_z // 2):
+            i = lax.rem(start + 2 * j, n_z)
+            pair, tail = add_blocks(keep[i], recv[i])
+            out[j, 0:own_width, :] = pair
+            out[j, own_width:, :] = tail
+
+
+def quad_kernel(own, recv, *outs):
+    own_width = own.shape[1] - EXTRA
+    for j, out in enumerate(outs):
+        quad, tail = add_blocks(own[j], recv[j])
+        out[0:own_width, :] = quad
         out[own_width:, :] = tail
 
 
@@ -192,20 +205,34 @@
         normed, weight_after, (((0,), (0,)), ((), ())), preferred_element_type=F32
     ).astype(BF16)
     outgoing = jnp.zeros((senders * most, out_cols), BF16).at[slot].set(embed)
+
+    pair_shape = jax.ShapeDtypeStruct((n_z // 2, own_width + EXTRA, rows), BF16)
+    pair_own, pair_away = pl.pallas_call(
+        pair_kernel,
+        out_shape=(pair_shape, pair_shape),
+        in_specs=[SMEM] + [VMEM] * 2,
+        out_specs=(VMEM,) * 2,
+        compiler_params=PARAMS,
+        name="pair",
+    )(at, keep, recv)
+    pair_recv = lax.ppermute(pair_away, "zl", [(i, i ^ 1) for i in range(n_zl)])
+
+    outgoing, _ = lax.optimization_barrier((outgoing, pair_away))
     embeds_recv = exchange(outgoing.reshape(senders, most, out_cols), ENC).reshape(
         senders * most, out_cols
     )
 
-    pairs = pl.pallas_call(
-        pair_kernel,
-        out_shape=(jax.ShapeDtypeStruct((own_width + EXTRA, rows), BF16),) * n_z,
-        in_specs=[SMEM] + [VMEM] * 2,
-        out_specs=(VMEM,) * n_z,
-        compiler_params=PARAMS,
-        name="pair",
-    )(at, keep, recv)
+    quads = pl.pallas_call(
+        quad_kernel,
+        out_shape=(jax.ShapeDtypeStruct((own_width + EXTRA, rows), BF16),) * (n_z // 2),
+        in_specs=[VMEM] * 2,
+        out_specs=(VMEM,) * (n_z // 2),
+        compiler_params=PARAMS,
+        name="quad",
+    )(pair_own, pair_recv)
     columns = sum(
-        [along_z(pairs[k], k).astype(F32) for k in range(1, n_z)], pairs[0].astype(F32)
+        [along_z(quads[j], 2 * j).astype(F32) for j in range(1, n_z // 2)],
+        quads[0].astype(F32),
     )
     dnormed = columns[:own_width]
     tail = columns[own_width:]

time: 182 us -> 177 us (0.973)
  starting transfers between devices: 57.1 us -> 46.1 us
  waiting for transfers between devices: 19.1 us -> 26.1 us
    ppermute x7 -> x3, starting transfers between devices: 33.5 us -> 18.2 us  [along_z(): lax.ppermute(x, ('zl', 'zh'), [(at[z], at[(z + step) % count]) for z in r...]
    ppermute x0 -> x1, waiting for transfers between devices: none -> 9.08 us  [body(): pair_recv = lax.ppermute(pair_away, 'zl', [(i, i ^ 1) for i in range(n_zl)])]
    ppermute x0 -> x1, starting transfers between devices: none -> 4.28 us  [body(): pair_recv = lax.ppermute(pair_away, 'zl', [(i, i ^ 1) for i in range(n_zl)])]
    ppermute x7 -> x3, waiting for transfers between devices: 8.33 us -> 6.19 us  [along_z(): lax.ppermute(x, ('zl', 'zh'), [(at[z], at[(z + step) % count]) for z in r...]
  transfers between devices with their start and end apart: 14 -> 11, of which waited for: 6 -> 6; matrix products, arithmetic and copies ran while one was open for 7% -> 7% of each run, Pallas kernels for 5% -> 5%
where the time goes in v7:
time: 177 us; the launch traced here: 176 us
  blocking collectives  60.8 us (34%)
  starting transfers between devices  46.1 us (26%)
  waiting for transfers between devices  26.1 us (15%)
  between operations  14.4 us (8%)
  local copies, waits for them, and re-layouts  12.7 us (7%)
  Pallas kernels  9.31 us (5%)
  matrix products  3.76 us (2%)
  other arithmetic  2.64 us (1%)
    all_gather x1, blocking collectives, body(): mine = lax.all_gather(own_t, ZED, axis=0)  32.9 us
    all_to_all x2, blocking collectives, exchange(): return lax.all_to_all(x, axes, 0, 0, tiled=True)  27.9 us
    all_to_all x3, starting transfers between devices, exchange(): return lax.all_to_all(x, axes, 0, 0, tiled=True)  19.6 us
    ppermute x3, starting transfers between devices, along_z(): lax.ppermute(x, ('zl', 'zh'), [(at[z], at[(z + step) % count]) for z in r...  18.2 us
    ppermute x1, waiting for transfers between devices, body(): pair_recv = lax.ppermute(pair_away, 'zl', [(i, i ^ 1) for i in range(n_zl)])  9.08 us
    ppermute x3, waiting for transfers between devices, along_z(): lax.ppermute(x, ('zl', 'zh'), [(at[z], at[(z + step) % count]) for z in r...  6.19 us
    all_to_all x3, waiting for transfers between devices, exchange(): return lax.all_to_all(x, axes, 0, 0, tiled=True)  5.5 us
    pallas_call x1, Pallas kernels, body(): pl.pallas_call(functools.partial(part_kernel, n_zl, n_zh), out_shape=(hal...  4.81 us
  transfers between devices with their start and end apart: 11, of which 6 were waited for; matrix products, arithmetic and copies ran while one was open for 7% of the time, Pallas kernels for 5%

profile of v7, /device:TPU:6, one launch (start us, length us, event | category | flops | bytes accessed | tf_op | source)
XLA Modules:
  0.0 175.7 jit_solution(94948422141075654)
XLA Ops:
  7.3 0.9 broadcast_in_dim.8
  8.2 13.7 %all_to_all.25 = bf16[4,100,512]{2,1,0:T(8,128)(2,1)S(1)} all-to-all(bf16[4,100,512]{2,1,0:T(8,128)(2,1)S(1)} %broadcast_in_dim.8), channel_id=1, replica_groups=mesh['y'=8,'x'=4,'zl'=4,'co'=2,'zh'=2] {'x'}, dimensions={0} | all-to-all | bytes 819200 | tf_op jit(solution)/shard_map/all_to_all | solution.py:24
  21.9 0.8 reshape.80
  22.7 7.2 %all-to-all-start.1 = ((bf16[32,24,512]{2,1,0:T(8,128)(2,1)}), bf16[32,24,512]{2,1,0:T(8,128)(2,1)}, u32[]{:S(2)}, u32[]{:S(2)}) async-start(bf16[32,24,512]{2,1,0:T(8,128)(2,1)} %bitcast.61), calls=%async_computation.1 | async-start | bytes 1572864 | tf_op jit(solution)/shard_map/all_to_all | solution.py:24
  30.3 32.9 %all-gather = bf16[1600,256]{1,0:T(8,128)(2,1)S(1)} all-gather(bf16[200,256]{1,0:T(8,128)(2,1)S(1)} %bitcast.62), channel_id=2, replica_groups=mesh['y'=8,'x'=4,'zl'=4,'co'=2,'zh'=2] {'zh','zl'}, dimensions={0}, use_global_device_ids=true | all-gather | bytes 921600 | tf_op jit(solution)/shard_map/all_gather | solution.py:162
  63.1 1.9 %collective-permute-start = (bf16[8,200,256]{2,1,0:T(8,128)(2,1)S(1)}, bf16[8,200,256]{2,1,0:T(8,128)(2,1)S(1)}, u32[]{:S(2)}, u32[]{:S(2)}) collective-permute-start(bf16[8,200,256]{2,1,0:T(8,128)(2,1)S(1)} %bitcast.50), channel_id=1, source_target_pairs={{0,2},{2,0},{1,3},{3,1},{4,6},{6,4},{5,7},{7,5},{8,10},{10,8},{9,1... | collective-permute-start | bytes 2457608 | tf_op jit(solution)/shard_map/ppermute | solution.py:40
  66.3 1.0 collective-permute-done.other
  67.3 3.0 %norm.1 = (bf16[16,200,256]{2,1,0:T(8,128)(2,1)S(1)}, f32[8,256]{1,0:T(8,128)S(1)}) custom-call(s32[2]{0:T(128)S(1)} %pad_add_fusion.at, bf16[8,200,256]{2,1,0:T(8,128)(2,1)S(1)} %bitcast.51, bf16[8,200,256]{2,1,0:T(8,128)(2,1)S(1)} %collective-permute-done.other, f32[200,16]{1,0:T(8,128)S(1)} %bitcast.55, f32[200,16]{1,0:T(8,128)S(1)} %bitcast.57), custom_call_target="tpu_custom_call" | custom-call | tf_op jit(solution)/shard_map/norm/pallas_call | solution.py:166
  70.4 2.4 %gather_fusion = bf16[256,512]{1,0:T(8,128)(2,1)S(1)} fusion(bf16[768,512]{1,0:T(8,128)(2,1)} %bitcast.4, s32[1024]{0:T(1024)S(1)} %pad_clamp_fusion), kind=kCustom, calls=%fused_computation | custom fusion | bytes 525312 | tf_op jit(solution)/shard_map/gather | solution.py:185
  72.8 2.7 %convolution_convert_fusion = bf16[3200,512]{1,0:T(8,128)(2,1)} fusion(bf16[3200,256]{1,0:T(8,128)(2,1)S(1)} %bitcast.53, bf16[256,512]{1,0:T(8,128)(2,1)S(1)} %gather_fusion), kind=kOutput, calls=%fused_computation.2 | convolution fusion | flops 840499200 | bytes 5177344 | tf_op jit(solution)/shard_map/dot_general | solution.py:187
  75.5 4.2 %all-gather.3.cloned.1.call-done = bf16[3200,512]{1,0:T(8,128)(2,1)} async-done(((bf16[400,512]{1,0:T(8,128)(2,1)}), bf16[3200,512]{1,0:T(8,128)(2,1)}) %all-gather.3.cloned.1.call-update) | async-done | bytes 3276816 | tf_op jit(solution)/shard_map/all_gather | solution.py:156
  79.8 0.9 copy-done.1
  80.6 4.8 %part.1 = (bf16[8,208,256]{2,1,0:T(8,128)(2,1)S(1)}, bf16[8,208,256]{2,1,0:T(8,128)(2,1)}) custom-call(s32[2]{0:T(128)S(1)} %pad_add_fusion.at, bf16[16,200,512]{2,1,0:T(8,128)(2,1)} %bitcast.58, bf16[256,512]{1,0:T(8,128)(2,1)S(1)} %gather_fusion, bf16[8,200,256]{2,1,0:T(8,128)(2,1)S(1)} %bitcast.52, bf16[8,200,256]{2,1,0:T(8,128)(2,1)S(1)} %collective-permute-done.other, ...), custom_call_target="tpu_custom_call" | custom-call | tf_op jit(solution)/shard_map/part/pallas_call | solution.py:191
  85.5 0.9 copy-done.2
  86.4 1.9 %collective-permute-start.1 = (bf16[8,208,256]{2,1,0:T(8,128)(2,1)}, bf16[8,208,256]{2,1,0:T(8,128)(2,1)}, u32[]{:S(2)}, u32[]{:S(2)}) collective-permute-start(bf16[8,208,256]{2,1,0:T(8,128)(2,1)} %get-tuple-element.29), channel_id=1, source_target_pairs={{0,2},{2,0},{1,3},{3,1},{4,6},{6,4},{5,7},{7,5},{8,10},{10,8},{9,1... | collective-permute-start | bytes 2555912 | tf_op jit(solution)/shard_map/ppermute | solution.py:40
  88.3 1.1 convolution_convert_fusion.1
  89.4 2.6 %scatter_custom_fusion = bf16[768,512]{1,0:T(8,128)(2,1)} fusion(s32[256]{0:T(256)} %bitcast.73, bf16[256,512]{1,0:T(8,128)(2,1)S(1)} %convolution_convert_fusion.1, bf16[]{:T(256)} %constant.34.clone.1), kind=kCustom, calls=%fused_computation.6 | custom fusion | bytes 786944 | tf_op jit(solution)/shard_map/scatter | solution.py:207
  92.0 1.4 pair.1
  93.4 7.6 %all-to-all-start.2 = ((bf16[32,24,512]{2,1,0:T(8,128)(2,1)}), bf16[32,24,512]{2,1,0:T(8,128)(2,1)S(1)}, u32[]{:S(2)}, u32[]{:S(2)}) async-start(bf16[32,24,512]{2,1,0:T(8,128)(2,1)} %bitcast.60), calls=%async_computation.2 | async-start | bytes 1572864 | tf_op jit(solution)/shard_map/all_to_all | solution.py:24
  101.1 4.3 %collective-permute-start.2 = (bf16[4,208,256]{2,1,0:T(8,128)(2,1)S(1)}, bf16[4,208,256]{2,1,0:T(8,128)(2,1)S(1)}, u32[]{:S(2)}, u32[]{:S(2)}) collective-permute-start(bf16[4,208,256]{2,1,0:T(8,128)(2,1)S(1)} %get-tuple-element.31), channel_id=1, source_target_pairs={{0,4},{4,0},{8,12},{12,8},{1,5},{5,1},{9,13},{13,9},{2,6},{6,2},{1... | collective-permute-start | bytes 1277960 | tf_op jit(solution)/shard_map/ppermute | solution.py:218
  106.1 9.1 %collective-permute-done.2.recv = bf16[4,208,256]{2,1,0:T(8,128)(2,1)S(1)} collective-permute-done((bf16[4,208,256]{2,1,0:T(8,128)(2,1)S(1)}, bf16[4,208,256]{2,1,0:T(8,128)(2,1)S(1)}, u32[]{:S(2)}, u32[]{:S(2)}) %collective-permute-start.2) | collective-permute-done | bytes 426016 | tf_op jit(solution)/shard_map/ppermute | solution.py:218
  115.3 6.1 %collective-permute-start.3 = (bf16[208,256]{1,0:T(8,128)(2,1)S(1)}, bf16[208,256]{1,0:T(8,128)(2,1)S(1)}, u32[]{:S(2)}, u32[]{:S(2)}) collective-permute-start(bf16[208,256]{1,0:T(8,128)(2,1)S(1)} %get-tuple-element.33), channel_id=1, source_target_pairs={{0,8},{4,12},{8,1},{12,5},{1,9},{5,13},{9,0},{13,4},{2,10},{6,14},... | collective-permute-start | bytes 319496 | tf_op jit(solution)/shard_map/ppermute | solution.py:36
  121.4 8.5 %collective-permute-start.4 = (bf16[208,256]{1,0:T(8,128)(2,1)S(1)}, bf16[208,256]{1,0:T(8,128)(2,1)S(1)}, u32[]{:S(2)}, u32[]{:S(2)}) collective-permute-start(bf16[208,256]{1,0:T(8,128)(2,1)S(1)} %get-tuple-element.34), channel_id=1, source_target_pairs={{0,1},{4,5},{8,9},{12,13},{1,0},{5,4},{9,8},{13,12},{2,3},{6,7},{1... | collective-permute-start | bytes 319496 | tf_op jit(solution)/shard_map/ppermute | solution.py:36
  129.9 3.7 %collective-permute-start.5 = (bf16[208,256]{1,0:T(8,128)(2,1)S(1)}, bf16[208,256]{1,0:T(8,128)(2,1)S(1)}, u32[]{:S(2)}, u32[]{:S(2)}) collective-permute-start(bf16[208,256]{1,0:T(8,128)(2,1)S(1)} %get-tuple-element.35), channel_id=1, source_target_pairs={{0,9},{4,13},{8,0},{12,4},{1,8},{5,12},{9,1},{13,5},{2,11},{6,15},... | collective-permute-start | bytes 319496 | tf_op jit(solution)/shard_map/ppermute | solution.py:36
  133.6 3.8 %collective-permute-done.4 = bf16[208,256]{1,0:T(8,128)(2,1)S(1)} collective-permute-done((bf16[208,256]{1,0:T(8,128)(2,1)S(1)}, bf16[208,256]{1,0:T(8,128)(2,1)S(1)}, u32[]{:S(2)}, u32[]{:S(2)}) %collective-permute-start.4) | collective-permute-done | bytes 106528 | tf_op jit(solution)/shard_map/ppermute | solution.py:36
  137.4 2.4 %collective-permute-done.5 = bf16[208,256]{1,0:T(8,128)(2,1)S(1)} collective-permute-done((bf16[208,256]{1,0:T(8,128)(2,1)S(1)}, bf16[208,256]{1,0:T(8,128)(2,1)S(1)}, u32[]{:S(2)}, u32[]{:S(2)}) %collective-permute-start.5) | collective-permute-done | bytes 106528 | tf_op jit(solution)/shard_map/ppermute | solution.py:36
  140.7 14.2 %all_to_all.26 = f32[8,1,400]{2,1,0:T(1,128)S(1)} all-to-all(f32[8,1,400]{2,1,0:T(1,128)S(1)} %broadcast_in_dim.10), channel_id=1, replica_groups=mesh['y'=8,'x'=4,'zl'=4,'co'=2,'zh'=2] {'y'}, dimensions={0} | all-to-all | bytes 25600 | tf_op jit(solution)/shard_map/all_to_all | solution.py:24
  155.1 1.1 reshape.90
  156.2 0.8 pad_maximum_fusion
  157.0 4.8 %all-to-all-start.4 = ((bf16[4,104,512]{2,1,0:T(8,128)(2,1)}), bf16[4,104,512]{2,1,0:T(8,128)(2,1)S(1)}, u32[]{:S(2)}, u32[]{:S(2)}) async-start(bf16[4,104,512]{2,1,0:T(8,128)(2,1)} %pad_maximum_fusion), calls=%async_computation.5 | async-start | bytes 851968 | tf_op jit(solution)/shard_map/all_to_all | solution.py:24
  161.8 5.5 %all-to-all-done.4 = bf16[4,104,512]{2,1,0:T(8,128)(2,1)S(1)} async-done(((bf16[4,104,512]{2,1,0:T(8,128)(2,1)}), bf16[4,104,512]{2,1,0:T(8,128)(2,1)S(1)}, u32[]{:S(2)}, u32[]{:S(2)}) %all-to-all-start.4) | async-done | bytes 426016 | tf_op jit(solution)/shard_map/all_to_all | solution.py:24
  168.0 0.9 copy.25
  (59 shorter events, 4.2 us)
Async XLA Ops:
  7.2 22.9 %copy-start.9 = (f32[3200]{0:T(1024)S(1)}, f32[3200]{0:T(1024)}, u32[]{:S(2)}) copy-start(f32[3200]{0:T(1024)} %param.8) | copy-start | bytes 38404
  7.2 23.0 %copy-start.8 = (f32[3200]{0:T(1024)S(1)}, f32[3200]{0:T(1024)}, u32[]{:S(2)}) copy-start(f32[3200]{0:T(1024)} %param.7) | copy-start | bytes 38404
  7.2 23.1 %copy-start.5 = (bf16[256,200]{0,1:T(8,128)(2,1)S(1)}, bf16[256,200]{0,1:T(8,128)(2,1)}, u32[]{:S(2)}) copy-start(bf16[256,200]{0,1:T(8,128)(2,1)} %param.6) | copy-start | bytes 307204
  7.2 57.8 %copy-start.10 = (s32[256,1]{0,1:T(1,128)S(1)}, s32[256,1]{0,1:T(1,128)}, u32[]{:S(2)}) copy-start(s32[256,1]{0,1:T(1,128)} %param.10) | copy-start | bytes 3076
  7.2 72.5 %all-gather.3.cloned.1.call-start = ((), (), s32[]{:S(2)}) async-start(), calls=%async_computation.6 | async-start | bytes 3686400 | tf_op jit(solution)/shard_map/all_gather | solution.py:156
  22.7 47.6 %all-to-all-start.1 = ((bf16[32,24,512]{2,1,0:T(8,128)(2,1)}), bf16[32,24,512]{2,1,0:T(8,128)(2,1)}, u32[]{:S(2)}, u32[]{:S(2)}) async-start(bf16[32,24,512]{2,1,0:T(8,128)(2,1)} %bitcast.61), calls=%async_computation.1 | async-start | bytes 1572864 | tf_op jit(solution)/shard_map/all_to_all | solution.py:24
  30.0 125.1 %reduce-scatter.2.cloned.1.call-start = ((), (), s32[]{:S(2)}) async-start(), calls=%async_computation.7 | async-start | bytes 3686400 | tf_op jit(solution)/shard_map/reduce_scatter | solution.py:188
  63.1 4.2 %collective-permute-start = (bf16[8,200,256]{2,1,0:T(8,128)(2,1)S(1)}, bf16[8,200,256]{2,1,0:T(8,128)(2,1)S(1)}, u32[]{:S(2)}, u32[]{:S(2)}) collective-permute-start(bf16[8,200,256]{2,1,0:T(8,128)(2,1)S(1)} %bitcast.50), channel_id=1, source_target_pairs={{0,2},{2,0},{1,3},{3,1},{4,6},{6,4},{5,7},{7,5},{8,10},{10,8},{9,1... | collective-permute-start | bytes 2457608 | tf_op jit(solution)/shard_map/ppermute | solution.py:40
  66.0 4.4 %copy-start = (f32[16,200]{0,1:T(8,128)}, f32[16,200]{0,1:T(8,128)S(1)}, u32[]{:S(2)}) copy-start(f32[16,200]{0,1:T(8,128)S(1)} %copy.18) | copy-start | bytes 38404
  66.3 4.1 %copy-start.11 = (s32[256,1]{0,1:T(1,128)}, s32[256,1]{0,1:T(1,128)S(1)}, u32[]{:S(2)}) copy-start(s32[256,1]{0,1:T(1,128)S(1)} %compare_select_fusion) | copy-start | bytes 3076
  79.8 0.9 copy-start.1
  80.6 7.7 %copy-start.4 = (bf16[3200,512]{1,0:T(8,128)(2,1)S(1)}, bf16[3200,512]{1,0:T(8,128)(2,1)}, u32[]{:S(2)}) copy-start(bf16[3200,512]{1,0:T(8,128)(2,1)} %all-gather.3.cloned.1.call-done) | copy-start | bytes 9830404
  85.5 0.9 copy-start.2
  86.4 5.6 %collective-permute-start.1 = (bf16[8,208,256]{2,1,0:T(8,128)(2,1)}, bf16[8,208,256]{2,1,0:T(8,128)(2,1)}, u32[]{:S(2)}, u32[]{:S(2)}) collective-permute-start(bf16[8,208,256]{2,1,0:T(8,128)(2,1)} %get-tuple-element.29), channel_id=1, source_target_pairs={{0,2},{2,0},{1,3},{3,1},{4,6},{6,4},{5,7},{7,5},{8,10},{10,8},{9,1... | collective-permute-start | bytes 2555912 | tf_op jit(solution)/shard_map/ppermute | solution.py:40
  88.3 3.7 %copy-start.3 = (bf16[8,208,256]{2,1,0:T(8,128)(2,1)S(1)}, bf16[8,208,256]{2,1,0:T(8,128)(2,1)}, u32[]{:S(2)}) copy-start(bf16[8,208,256]{2,1,0:T(8,128)(2,1)} %copy-done.2) | copy-start | bytes 2555908
  89.4 50.5 %copy-start.6 = (bf16[256,200]{0,1:T(8,128)(2,1)S(1)}, bf16[256,200]{0,1:T(8,128)(2,1)}, u32[]{:S(2)}) copy-start(bf16[256,200]{0,1:T(8,128)(2,1)} %param.6) | copy-start | bytes 307204
  93.4 47.3 %all-to-all-start.2 = ((bf16[32,24,512]{2,1,0:T(8,128)(2,1)}), bf16[32,24,512]{2,1,0:T(8,128)(2,1)S(1)}, u32[]{:S(2)}, u32[]{:S(2)}) async-start(bf16[32,24,512]{2,1,0:T(8,128)(2,1)} %bitcast.60), calls=%async_computation.2 | async-start | bytes 1572864 | tf_op jit(solution)/shard_map/all_to_all | solution.py:24
  101.1 14.2 %collective-permute-start.2 = (bf16[4,208,256]{2,1,0:T(8,128)(2,1)S(1)}, bf16[4,208,256]{2,1,0:T(8,128)(2,1)S(1)}, u32[]{:S(2)}, u32[]{:S(2)}) collective-permute-start(bf16[4,208,256]{2,1,0:T(8,128)(2,1)S(1)} %get-tuple-element.31), channel_id=1, source_target_pairs={{0,4},{4,0},{8,12},{12,8},{1,5},{5,1},{9,13},{13,9},{2,6},{6,2},{1... | collective-permute-start | bytes 1277960 | tf_op jit(solution)/shard_map/ppermute | solution.py:218
  115.3 18.3 %collective-permute-start.3 = (bf16[208,256]{1,0:T(8,128)(2,1)S(1)}, bf16[208,256]{1,0:T(8,128)(2,1)S(1)}, u32[]{:S(2)}, u32[]{:S(2)}) collective-permute-start(bf16[208,256]{1,0:T(8,128)(2,1)S(1)} %get-tuple-element.33), channel_id=1, source_target_pairs={{0,8},{4,12},{8,1},{12,5},{1,9},{5,13},{9,0},{13,4},{2,10},{6,14},... | collective-permute-start | bytes 319496 | tf_op jit(solution)/shard_map/ppermute | solution.py:36
  121.4 16.0 %collective-permute-start.4 = (bf16[208,256]{1,0:T(8,128)(2,1)S(1)}, bf16[208,256]{1,0:T(8,128)(2,1)S(1)}, u32[]{:S(2)}, u32[]{:S(2)}) collective-permute-start(bf16[208,256]{1,0:T(8,128)(2,1)S(1)} %get-tuple-element.34), channel_id=1, source_target_pairs={{0,1},{4,5},{8,9},{12,13},{1,0},{5,4},{9,8},{13,12},{2,3},{6,7},{1... | collective-permute-start | bytes 319496 | tf_op jit(solution)/shard_map/ppermute | solution.py:36
  129.9 9.9 %collective-permute-start.5 = (bf16[208,256]{1,0:T(8,128)(2,1)S(1)}, bf16[208,256]{1,0:T(8,128)(2,1)S(1)}, u32[]{:S(2)}, u32[]{:S(2)}) collective-permute-start(bf16[208,256]{1,0:T(8,128)(2,1)S(1)} %get-tuple-element.35), channel_id=1, source_target_pairs={{0,9},{4,13},{8,0},{12,4},{1,8},{5,12},{9,1},{13,5},{2,11},{6,15},... | collective-permute-start | bytes 319496 | tf_op jit(solution)/shard_map/ppermute | solution.py:36
  157.0 10.3 %all-to-all-start.4 = ((bf16[4,104,512]{2,1,0:T(8,128)(2,1)}), bf16[4,104,512]{2,1,0:T(8,128)(2,1)S(1)}, u32[]{:S(2)}, u32[]{:S(2)}) async-start(bf16[4,104,512]{2,1,0:T(8,128)(2,1)} %pad_maximum_fusion), calls=%async_computation.5 | async-start | bytes 851968 | tf_op jit(solution)/shard_map/all_to_all | solution.py:24
  167.3 1.5 copy-start.7
Sparse Core Ops, SparseCore 0:
  22.9 56.8 all-gather.2
  82.6 67.8 reduce-scatter.1

commit v8 on v7

--- a/solution.py
+++ b/solution.py
@@ -187,6 +187,15 @@
     grad_part = jnp.dot(normed, d_embed, preferred_element_type=F32).astype(BF16)
     grad_y = lax.psum_scatter(grad_part, "y", scatter_dimension=0, tiled=True)
 
+    embed = lax.dot_general(
+        normed, weight, (((0,), (0,)), ((), ())), preferred_element_type=F32
+    ).astype(BF16)
+    outgoing = jnp.zeros((senders * most, out_cols), BF16).at[slot].set(embed)
+    embeds_recv = exchange(outgoing.reshape(senders, most, out_cols), ENC).reshape(
+        senders * most, out_cols
+    )
+    weight, _ = lax.optimization_barrier((weight, outgoing))
+
     half_shape = jax.ShapeDtypeStruct((n_z, own_width + EXTRA, rows), BF16)
     keep, send = pl.pallas_call(
         functools.partial(part_kernel, n_zl, n_zh),
@@ -200,11 +209,6 @@
     )
     recv = core_swap(send)
 
-    weight_after, keep = lax.optimization_barrier((weight, keep))
-    embed = lax.dot_general(
-        normed, weight_after, (((0,), (0,)), ((), ())), preferred_element_type=F32
-    ).astype(BF16)
-    outgoing = jnp.zeros((senders * most, out_cols), BF16).at[slot].set(embed)
 
     pair_shape = jax.ShapeDtypeStruct((n_z // 2, own_width + EXTRA, rows), BF16)
     pair_own, pair_away = pl.pallas_call(
@@ -217,10 +221,6 @@
     )(at, keep, recv)
     pair_recv = lax.ppermute(pair_away, "zl", [(i, i ^ 1) for i in range(n_zl)])
 
-    outgoing, _ = lax.optimization_barrier((outgoing, pair_away))
-    embeds_recv = exchange(outgoing.reshape(senders, most, out_cols), ENC).reshape(
-        senders * most, out_cols
-    )
 
     quads = pl.pallas_call(
         quad_kernel,

time: 177 us -> 180 us (1.017)
  matrix products: 3.76 us -> 6.43 us
    dot_general x1, matrix products: 1.06 us -> 3.7 us  [body(): lax.dot_general(normed, weight, (((0,), (0,)), ((), ())), preferred_eleme...]
  transfers between devices with their start and end apart: 11 -> 11, of which waited for: 6 -> 6; matrix products, arithmetic and copies ran while one was open for 7% -> 8% of each run, Pallas kernels for 5% -> 5%
where the time goes in v8:
time: 180 us; the launch traced here: 178 us
  blocking collectives  60.7 us (34%)
  starting transfers between devices  46.2 us (26%)
  waiting for transfers between devices  26.2 us (15%)
  between operations  14.4 us (8%)
  local copies, waits for them, and re-layouts  13.2 us (7%)
  Pallas kernels  8.53 us (5%)
  matrix products  6.43 us (4%)
  other arithmetic  2.65 us (1%)
    all_gather x1, blocking collectives, body(): mine = lax.all_gather(own_t, ZED, axis=0)  32.7 us
    all_to_all x2, blocking collectives, exchange(): return lax.all_to_all(x, axes, 0, 0, tiled=True)  27.9 us
    all_to_all x3, starting transfers between devices, exchange(): return lax.all_to_all(x, axes, 0, 0, tiled=True)  19.7 us
    ppermute x3, starting transfers between devices, along_z(): lax.ppermute(x, ('zl', 'zh'), [(at[z], at[(z + step) % count]) for z in r...  18.2 us
    ppermute x1, waiting for transfers between devices, body(): pair_recv = lax.ppermute(pair_away, 'zl', [(i, i ^ 1) for i in range(n_zl)])  9.08 us
    ppermute x3, waiting for transfers between devices, along_z(): lax.ppermute(x, ('zl', 'zh'), [(at[z], at[(z + step) % count]) for z in r...  6.19 us
    all_to_all x3, waiting for transfers between devices, exchange(): return lax.all_to_all(x, axes, 0, 0, tiled=True)  5.5 us
    pallas_call x1, Pallas kernels, body(): pl.pallas_call(functools.partial(part_kernel, n_zl, n_zh), out_shape=(hal...  4.65 us
  transfers between devices with their start and end apart: 11, of which 6 were waited for; matrix products, arithmetic and copies ran while one was open for 8% of the time, Pallas kernels for 5%

profile of v8, /device:TPU:6, one launch (start us, length us, event | category | flops | bytes accessed | tf_op | source)
XLA Modules:
  0.0 178.2 jit_solution(1252129065723831268)
XLA Ops:
  7.3 0.9 broadcast_in_dim.8
  8.2 13.7 %all_to_all.25 = bf16[4,100,512]{2,1,0:T(8,128)(2,1)S(1)} all-to-all(bf16[4,100,512]{2,1,0:T(8,128)(2,1)S(1)} %broadcast_in_dim.8), channel_id=1, replica_groups=mesh['y'=8,'x'=4,'zl'=4,'co'=2,'zh'=2] {'x'}, dimensions={0} | all-to-all | bytes 819200 | tf_op jit(solution)/shard_map/all_to_all | solution.py:24
  21.9 0.8 reshape.80
  22.8 7.2 %all-to-all-start.1 = ((bf16[32,24,512]{2,1,0:T(8,128)(2,1)}), bf16[32,24,512]{2,1,0:T(8,128)(2,1)}, u32[]{:S(2)}, u32[]{:S(2)}) async-start(bf16[32,24,512]{2,1,0:T(8,128)(2,1)} %bitcast.59), calls=%async_computation.1 | async-start | bytes 1572864 | tf_op jit(solution)/shard_map/all_to_all | solution.py:24
  30.5 32.7 %all-gather = bf16[1600,256]{1,0:T(8,128)(2,1)S(1)} all-gather(bf16[200,256]{1,0:T(8,128)(2,1)S(1)} %bitcast.60), channel_id=2, replica_groups=mesh['y'=8,'x'=4,'zl'=4,'co'=2,'zh'=2] {'zh','zl'}, dimensions={0}, use_global_device_ids=true | all-gather | bytes 921600 | tf_op jit(solution)/shard_map/all_gather | solution.py:162
  63.2 1.9 %collective-permute-start = (bf16[8,200,256]{2,1,0:T(8,128)(2,1)S(1)}, bf16[8,200,256]{2,1,0:T(8,128)(2,1)S(1)}, u32[]{:S(2)}, u32[]{:S(2)}) collective-permute-start(bf16[8,200,256]{2,1,0:T(8,128)(2,1)S(1)} %bitcast.49), channel_id=1, source_target_pairs={{0,2},{2,0},{1,3},{3,1},{4,6},{6,4},{5,7},{7,5},{8,10},{10,8},{9,1... | collective-permute-start | bytes 2457608 | tf_op jit(solution)/shard_map/ppermute | solution.py:40
  66.2 1.2 collective-permute-done.other
  67.4 3.0 %norm.1 = (bf16[16,200,256]{2,1,0:T(8,128)(2,1)S(1)}, f32[8,256]{1,0:T(8,128)S(1)}) custom-call(s32[2]{0:T(128)S(1)} %pad_add_fusion.at, bf16[8,200,256]{2,1,0:T(8,128)(2,1)S(1)} %bitcast.50, bf16[8,200,256]{2,1,0:T(8,128)(2,1)S(1)} %collective-permute-done.other, f32[200,16]{1,0:T(8,128)S(1)} %bitcast.54, f32[200,16]{1,0:T(8,128)S(1)} %bitcast.56), custom_call_target="tpu_custom_call" | custom-call | tf_op jit(solution)/shard_map/norm/pallas_call | solution.py:166
  70.4 2.4 %gather_fusion = bf16[256,512]{1,0:T(8,128)(2,1)S(1)} fusion(bf16[768,512]{1,0:T(8,128)(2,1)} %bitcast.14, s32[1024]{0:T(1024)S(1)} %pad_clamp_fusion), kind=kCustom, calls=%fused_computation | custom fusion | bytes 525312 | tf_op jit(solution)/shard_map/gather | solution.py:185
  72.9 2.7 %convolution_convert_fusion = bf16[3200,512]{1,0:T(8,128)(2,1)} fusion(bf16[3200,256]{1,0:T(8,128)(2,1)S(1)} %bitcast.52, bf16[256,512]{1,0:T(8,128)(2,1)S(1)} %gather_fusion), kind=kOutput, calls=%fused_computation.2 | convolution fusion | flops 840499200 | bytes 5177344 | tf_op jit(solution)/shard_map/dot_general | solution.py:187
  75.7 4.1 %all-gather.3.cloned.1.call-done = bf16[3200,512]{1,0:T(8,128)(2,1)} async-done(((bf16[400,512]{1,0:T(8,128)(2,1)}), bf16[3200,512]{1,0:T(8,128)(2,1)}) %all-gather.3.cloned.1.call-update) | async-done | bytes 3276816 | tf_op jit(solution)/shard_map/all_gather | solution.py:156
  79.8 3.7 %convolution_convert_fusion.1 = bf16[256,512]{1,0:T(8,128)(2,1)} fusion(bf16[3200,256]{1,0:T(8,128)(2,1)S(1)} %bitcast.53, bf16[3200,512]{1,0:T(8,128)(2,1)} %all-gather.3.cloned.1.call-done), kind=kOutput, calls=%fused_computation.3 | convolution fusion | flops 838991872 | bytes 5177344 | tf_op jit(solution)/shard_map/dot_general | solution.py:190
  83.4 2.9 %scatter_custom_fusion = bf16[768,512]{1,0:T(8,128)(2,1)} fusion(s32[256]{0:T(256)} %bitcast.71, bf16[256,512]{1,0:T(8,128)(2,1)} %convolution_convert_fusion.1, bf16[]{:T(256)} %constant.30.clone.1), kind=kCustom, calls=%fused_computation.6 | custom fusion | bytes 786944 | tf_op jit(solution)/shard_map/scatter | solution.py:193
  86.3 0.9 copy-done.1
  87.2 4.7 %part.1 = (bf16[8,208,256]{2,1,0:T(8,128)(2,1)S(1)}, bf16[8,208,256]{2,1,0:T(8,128)(2,1)}) custom-call(s32[2]{0:T(128)S(1)} %pad_add_fusion.at, bf16[16,200,512]{2,1,0:T(8,128)(2,1)} %bitcast.57, bf16[256,512]{1,0:T(8,128)(2,1)S(1)} %gather_fusion, bf16[8,200,256]{2,1,0:T(8,128)(2,1)S(1)} %bitcast.51, bf16[8,200,256]{2,1,0:T(8,128)(2,1)S(1)} %collective-permute-done.other, ...), custom_call_target="tpu_custom_call" | custom-call | tf_op jit(solution)/shard_map/part/pallas_call | solution.py:200
  91.9 2.1 %collective-permute-start.1 = (bf16[8,208,256]{2,1,0:T(8,128)(2,1)}, bf16[8,208,256]{2,1,0:T(8,128)(2,1)S(1)}, u32[]{:S(2)}, u32[]{:S(2)}) collective-permute-start(bf16[8,208,256]{2,1,0:T(8,128)(2,1)} %get-tuple-element.28), channel_id=1, source_target_pairs={{0,2},{2,0},{1,3},{3,1},{4,6},{6,4},{5,7},{7,5},{8,10},{10,8},{9,1... | collective-permute-start | bytes 2555912 | tf_op jit(solution)/shard_map/ppermute | solution.py:40
  93.9 7.7 %all-to-all-start.2 = ((bf16[32,24,512]{2,1,0:T(8,128)(2,1)}), bf16[32,24,512]{2,1,0:T(8,128)(2,1)}, u32[]{:S(2)}, u32[]{:S(2)}) async-start(bf16[32,24,512]{2,1,0:T(8,128)(2,1)} %bitcast.58), calls=%async_computation.2 | async-start | bytes 1572864 | tf_op jit(solution)/shard_map/all_to_all | solution.py:24
  102.4 4.3 %collective-permute-start.2 = (bf16[4,208,256]{2,1,0:T(8,128)(2,1)S(1)}, bf16[4,208,256]{2,1,0:T(8,128)(2,1)S(1)}, u32[]{:S(2)}, u32[]{:S(2)}) collective-permute-start(bf16[4,208,256]{2,1,0:T(8,128)(2,1)S(1)} %get-tuple-element.30), channel_id=1, source_target_pairs={{0,4},{4,0},{8,12},{12,8},{1,5},{5,1},{9,13},{13,9},{2,6},{6,2},{1... | collective-permute-start | bytes 1277960 | tf_op jit(solution)/shard_map/ppermute | solution.py:222
  106.7 0.8 dynamic_slice.3
  107.5 9.1 %collective-permute-done.2.recv = bf16[4,208,256]{2,1,0:T(8,128)(2,1)S(1)} collective-permute-done((bf16[4,208,256]{2,1,0:T(8,128)(2,1)S(1)}, bf16[4,208,256]{2,1,0:T(8,128)(2,1)S(1)}, u32[]{:S(2)}, u32[]{:S(2)}) %collective-permute-start.2) | collective-permute-done | bytes 426016 | tf_op jit(solution)/shard_map/ppermute | solution.py:222
  116.7 6.1 %collective-permute-start.3 = (bf16[208,256]{1,0:T(8,128)(2,1)S(1)}, bf16[208,256]{1,0:T(8,128)(2,1)S(1)}, u32[]{:S(2)}, u32[]{:S(2)}) collective-permute-start(bf16[208,256]{1,0:T(8,128)(2,1)S(1)} %get-tuple-element.32), channel_id=1, source_target_pairs={{0,8},{4,12},{8,1},{12,5},{1,9},{5,13},{9,0},{13,4},{2,10},{6,14},... | collective-permute-start | bytes 319496 | tf_op jit(solution)/shard_map/ppermute | solution.py:36
  122.8 8.5 %collective-permute-start.4 = (bf16[208,256]{1,0:T(8,128)(2,1)S(1)}, bf16[208,256]{1,0:T(8,128)(2,1)S(1)}, u32[]{:S(2)}, u32[]{:S(2)}) collective-permute-start(bf16[208,256]{1,0:T(8,128)(2,1)S(1)} %get-tuple-element.33), channel_id=1, source_target_pairs={{0,1},{4,5},{8,9},{12,13},{1,0},{5,4},{9,8},{13,12},{2,3},{6,7},{1... | collective-permute-start | bytes 319496 | tf_op jit(solution)/shard_map/ppermute | solution.py:36
  131.2 3.7 %collective-permute-start.5 = (bf16[208,256]{1,0:T(8,128)(2,1)S(1)}, bf16[208,256]{1,0:T(8,128)(2,1)S(1)}, u32[]{:S(2)}, u32[]{:S(2)}) collective-permute-start(bf16[208,256]{1,0:T(8,128)(2,1)S(1)} %get-tuple-element.34), channel_id=1, source_target_pairs={{0,9},{4,13},{8,0},{12,4},{1,8},{5,12},{9,1},{13,5},{2,11},{6,15},... | collective-permute-start | bytes 319496 | tf_op jit(solution)/shard_map/ppermute | solution.py:36
  134.9 3.8 %collective-permute-done.4 = bf16[208,256]{1,0:T(8,128)(2,1)S(1)} collective-permute-done((bf16[208,256]{1,0:T(8,128)(2,1)S(1)}, bf16[208,256]{1,0:T(8,128)(2,1)S(1)}, u32[]{:S(2)}, u32[]{:S(2)}) %collective-permute-start.4) | collective-permute-done | bytes 106528 | tf_op jit(solution)/shard_map/ppermute | solution.py:36
  138.8 2.4 %collective-permute-done.5 = bf16[208,256]{1,0:T(8,128)(2,1)S(1)} collective-permute-done((bf16[208,256]{1,0:T(8,128)(2,1)S(1)}, bf16[208,256]{1,0:T(8,128)(2,1)S(1)}, u32[]{:S(2)}, u32[]{:S(2)}) %collective-permute-start.5) | collective-permute-done | bytes 106528 | tf_op jit(solution)/shard_map/ppermute | solution.py:36
  141.2 0.8 multiply_reduce_fusion
  142.1 14.2 %all_to_all.26 = f32[8,1,400]{2,1,0:T(1,128)S(1)} all-to-all(f32[8,1,400]{2,1,0:T(1,128)S(1)} %broadcast_in_dim.10), channel_id=1, replica_groups=mesh['y'=8,'x'=4,'zl'=4,'co'=2,'zh'=2] {'y'}, dimensions={0} | all-to-all | bytes 25600 | tf_op jit(solution)/shard_map/all_to_all | solution.py:24
  156.4 1.1 reshape.90
  157.5 0.8 pad_maximum_fusion
  158.3 4.8 %all-to-all-start.4 = ((bf16[4,104,512]{2,1,0:T(8,128)(2,1)}), bf16[4,104,512]{2,1,0:T(8,128)(2,1)S(1)}, u32[]{:S(2)}, u32[]{:S(2)}) async-start(bf16[4,104,512]{2,1,0:T(8,128)(2,1)} %pad_maximum_fusion), calls=%async_computation.5 | async-start | bytes 851968 | tf_op jit(solution)/shard_map/all_to_all | solution.py:24
  163.1 5.5 %all-to-all-done.4 = bf16[4,104,512]{2,1,0:T(8,128)(2,1)S(1)} async-done(((bf16[4,104,512]{2,1,0:T(8,128)(2,1)}), bf16[4,104,512]{2,1,0:T(8,128)(2,1)S(1)}, u32[]{:S(2)}, u32[]{:S(2)}) %all-to-all-start.4) | async-done | bytes 426016 | tf_op jit(solution)/shard_map/all_to_all | solution.py:24
  169.3 2.1 %copy.25 = bf16[768,512]{1,0:T(8,128)(2,1)} copy(bf16[768,512]{1,0:T(8,128)(2,1)} %bitcast.18) | data formatting | bytes 1572864
  (53 shorter events, 3.4 us)
Async XLA Ops:
  7.2 22.9 %copy-start.5 = (f32[3200]{0:T(1024)S(1)}, f32[3200]{0:T(1024)}, u32[]{:S(2)}) copy-start(f32[3200]{0:T(1024)} %param.7) | copy-start | bytes 38404
  7.2 23.1 %copy-start.6 = (f32[3200]{0:T(1024)S(1)}, f32[3200]{0:T(1024)}, u32[]{:S(2)}) copy-start(f32[3200]{0:T(1024)} %param.8) | copy-start | bytes 38404
  7.2 23.3 %copy-start.2 = (bf16[256,200]{0,1:T(8,128)(2,1)S(1)}, bf16[256,200]{0,1:T(8,128)(2,1)}, u32[]{:S(2)}) copy-start(bf16[256,200]{0,1:T(8,128)(2,1)} %param.6) | copy-start | bytes 307204
  7.2 57.9 %copy-start.7 = (s32[256,1]{0,1:T(1,128)S(1)}, s32[256,1]{0,1:T(1,128)}, u32[]{:S(2)}) copy-start(s32[256,1]{0,1:T(1,128)} %param.10) | copy-start | bytes 3076
  7.2 72.5 %all-gather.3.cloned.1.call-start = ((), (), s32[]{:S(2)}) async-start(), calls=%async_computation.6 | async-start | bytes 3686400 | tf_op jit(solution)/shard_map/all_gather | solution.py:156
  22.8 47.7 %all-to-all-start.1 = ((bf16[32,24,512]{2,1,0:T(8,128)(2,1)}), bf16[32,24,512]{2,1,0:T(8,128)(2,1)}, u32[]{:S(2)}, u32[]{:S(2)}) async-start(bf16[32,24,512]{2,1,0:T(8,128)(2,1)} %bitcast.59), calls=%async_computation.1 | async-start | bytes 1572864 | tf_op jit(solution)/shard_map/all_to_all | solution.py:24
  30.0 126.4 %reduce-scatter.2.cloned.1.call-start = ((), (), s32[]{:S(2)}) async-start(), calls=%async_computation.7 | async-start | bytes 3686400 | tf_op jit(solution)/shard_map/reduce_scatter | solution.py:188
  30.2 40.2 %copy-start = (f32[16,200]{0,1:T(8,128)}, f32[16,200]{0,1:T(8,128)S(1)}, u32[]{:S(2)}) copy-start(f32[16,200]{0,1:T(8,128)S(1)} %copy.18) | copy-start | bytes 38404
  63.2 4.2 %collective-permute-start = (bf16[8,200,256]{2,1,0:T(8,128)(2,1)S(1)}, bf16[8,200,256]{2,1,0:T(8,128)(2,1)S(1)}, u32[]{:S(2)}, u32[]{:S(2)}) collective-permute-start(bf16[8,200,256]{2,1,0:T(8,128)(2,1)S(1)} %bitcast.49), channel_id=1, source_target_pairs={{0,2},{2,0},{1,3},{3,1},{4,6},{6,4},{5,7},{7,5},{8,10},{10,8},{9,1... | collective-permute-start | bytes 2457608 | tf_op jit(solution)/shard_map/ppermute | solution.py:40
  66.2 4.3 %copy-start.8 = (s32[256,1]{0,1:T(1,128)}, s32[256,1]{0,1:T(1,128)S(1)}, u32[]{:S(2)}) copy-start(s32[256,1]{0,1:T(1,128)S(1)} %compare_select_fusion) | copy-start | bytes 3076
  86.3 0.9 copy-start.1
  91.9 49.3 %copy-start.3 = (bf16[256,200]{0,1:T(8,128)(2,1)S(1)}, bf16[256,200]{0,1:T(8,128)(2,1)}, u32[]{:S(2)}) copy-start(bf16[256,200]{0,1:T(8,128)(2,1)} %param.6) | copy-start | bytes 307204
  91.9 9.7 %collective-permute-start.1 = (bf16[8,208,256]{2,1,0:T(8,128)(2,1)}, bf16[8,208,256]{2,1,0:T(8,128)(2,1)S(1)}, u32[]{:S(2)}, u32[]{:S(2)}) collective-permute-start(bf16[8,208,256]{2,1,0:T(8,128)(2,1)} %get-tuple-element.28), channel_id=1, source_target_pairs={{0,2},{2,0},{1,3},{3,1},{4,6},{6,4},{5,7},{7,5},{8,10},{10,8},{9,1... | collective-permute-start | bytes 2555912 | tf_op jit(solution)/shard_map/ppermute | solution.py:40
  93.9 48.1 %all-to-all-start.2 = ((bf16[32,24,512]{2,1,0:T(8,128)(2,1)}), bf16[32,24,512]{2,1,0:T(8,128)(2,1)}, u32[]{:S(2)}, u32[]{:S(2)}) async-start(bf16[32,24,512]{2,1,0:T(8,128)(2,1)} %bitcast.58), calls=%async_computation.2 | async-start | bytes 1572864 | tf_op jit(solution)/shard_map/all_to_all | solution.py:24
  102.4 14.2 %collective-permute-start.2 = (bf16[4,208,256]{2,1,0:T(8,128)(2,1)S(1)}, bf16[4,208,256]{2,1,0:T(8,128)(2,1)S(1)}, u32[]{:S(2)}, u32[]{:S(2)}) collective-permute-start(bf16[4,208,256]{2,1,0:T(8,128)(2,1)S(1)} %get-tuple-element.30), channel_id=1, source_target_pairs={{0,4},{4,0},{8,12},{12,8},{1,5},{5,1},{9,13},{13,9},{2,6},{6,2},{1... | collective-permute-start | bytes 1277960 | tf_op jit(solution)/shard_map/ppermute | solution.py:222
  116.7 18.3 %collective-permute-start.3 = (bf16[208,256]{1,0:T(8,128)(2,1)S(1)}, bf16[208,256]{1,0:T(8,128)(2,1)S(1)}, u32[]{:S(2)}, u32[]{:S(2)}) collective-permute-start(bf16[208,256]{1,0:T(8,128)(2,1)S(1)} %get-tuple-element.32), channel_id=1, source_target_pairs={{0,8},{4,12},{8,1},{12,5},{1,9},{5,13},{9,0},{13,4},{2,10},{6,14},... | collective-permute-start | bytes 319496 | tf_op jit(solution)/shard_map/ppermute | solution.py:36
  122.8 16.0 %collective-permute-start.4 = (bf16[208,256]{1,0:T(8,128)(2,1)S(1)}, bf16[208,256]{1,0:T(8,128)(2,1)S(1)}, u32[]{:S(2)}, u32[]{:S(2)}) collective-permute-start(bf16[208,256]{1,0:T(8,128)(2,1)S(1)} %get-tuple-element.33), channel_id=1, source_target_pairs={{0,1},{4,5},{8,9},{12,13},{1,0},{5,4},{9,8},{13,12},{2,3},{6,7},{1... | collective-permute-start | bytes 319496 | tf_op jit(solution)/shard_map/ppermute | solution.py:36
  131.2 9.9 %collective-permute-start.5 = (bf16[208,256]{1,0:T(8,128)(2,1)S(1)}, bf16[208,256]{1,0:T(8,128)(2,1)S(1)}, u32[]{:S(2)}, u32[]{:S(2)}) collective-permute-start(bf16[208,256]{1,0:T(8,128)(2,1)S(1)} %get-tuple-element.34), channel_id=1, source_target_pairs={{0,9},{4,13},{8,0},{12,4},{1,8},{5,12},{9,1},{13,5},{2,11},{6,15},... | collective-permute-start | bytes 319496 | tf_op jit(solution)/shard_map/ppermute | solution.py:36
  158.3 10.3 %all-to-all-start.4 = ((bf16[4,104,512]{2,1,0:T(8,128)(2,1)}), bf16[4,104,512]{2,1,0:T(8,128)(2,1)S(1)}, u32[]{:S(2)}, u32[]{:S(2)}) async-start(bf16[4,104,512]{2,1,0:T(8,128)(2,1)} %pad_maximum_fusion), calls=%async_computation.5 | async-start | bytes 851968 | tf_op jit(solution)/shard_map/all_to_all | solution.py:24
  168.6 2.7 %copy-start.4 = (f32[104,512]{1,0:T(8,128)}, f32[104,512]{1,0:T(8,128)S(1)}, u32[]{:S(2)}) copy-start(f32[104,512]{1,0:T(8,128)S(1)} %convert_reduce_fusion) | copy-start | bytes 638980
Sparse Core Ops, SparseCore 0:
  22.9 56.8 all-gather.2
  82.6 67.7 reduce-scatter.1

commit v9 on v7

--- a/solution.py
+++ b/solution.py
@@ -244,16 +244,17 @@
     xhat_own = (own_t.astype(F32) - mean) * inv
     hidden = (inv * (dnormed * gain_own - plain - xhat_own * cross)).astype(BF16).T
     sums = jnp.concatenate([jnp.sum(dnormed * xhat_own, 1), jnp.sum(dnormed, 1)])
+    grad_y, _ = lax.optimization_barrier((grad_y, sums))
     sums, embeds_recv = lax.optimization_barrier((sums, embeds_recv))
     sums = jnp.sum(copies(sums[None], "y"), (0, 1))
 
     high = lax.reduce_precision(sums, 8, 7)
     tail = jnp.stack([high, sums - high]).astype(BF16)
     tail = jnp.pad(tail, ((0, padded_rows - slice_rows - 2), (0, out_cols - sums.size)))
-    grad_y, tail = lax.optimization_barrier((grad_y, tail))
+    grad_y, tail = lax.optimization_barrier((grad_y.reshape(n_x, slice_rows, out_cols), tail))
     grad_x = jnp.concatenate(
         [
-            grad_y.reshape(n_x, slice_rows, out_cols),
+            grad_y,
             jnp.broadcast_to(tail[None], (n_x, *tail.shape)),
         ],
         1,

time: 177 us -> 177 us (level)
  blocking collectives: 60.8 us -> 46.6 us
  starting transfers between devices: 46.1 us -> 52.7 us
  waiting for transfers between devices: 26.1 us -> 32.7 us
    all_to_all x2 -> x1, blocking collectives: 27.9 us -> 13.7 us  [exchange(): return lax.all_to_all(x, axes, 0, 0, tiled=True)]
    all_to_all x3 -> x4, starting transfers between devices: 19.6 us -> 26.3 us  [exchange(): return lax.all_to_all(x, axes, 0, 0, tiled=True)]
    all_to_all x3 -> x4, waiting for transfers between devices: 5.5 us -> 9.78 us  [exchange(): return lax.all_to_all(x, axes, 0, 0, tiled=True)]
    reduce_scatter x1, waiting for transfers between devices: 0.02 us -> 2.41 us  [body(): grad_y = lax.psum_scatter(grad_part, 'y', scatter_dimension=0, tiled=True)]
  transfers between devices with their start and end apart: 11 -> 12, of which waited for: 6 -> 8; matrix products, arithmetic and copies ran while one was open for 7% -> 8% of each run, Pallas kernels for 5% -> 5%
where the time goes in v9:
time: 177 us; the launch traced here: 175 us
  starting transfers between devices  52.7 us (30%)
  blocking collectives  46.6 us (26%)
  waiting for transfers between devices  32.7 us (18%)
  between operations  14.4 us (8%)
  local copies, waits for them, and re-layouts  13.3 us (8%)
  Pallas kernels  9.3 us (5%)
  matrix products  3.76 us (2%)
  other arithmetic  2.64 us (1%)
    all_gather x1, blocking collectives, body(): mine = lax.all_gather(own_t, ZED, axis=0)  32.9 us
    all_to_all x4, starting transfers between devices, exchange(): return lax.all_to_all(x, axes, 0, 0, tiled=True)  26.3 us
    ppermute x3, starting transfers between devices, along_z(): lax.ppermute(x, ('zl', 'zh'), [(at[z], at[(z + step) % count]) for z in r...  18.2 us
    all_to_all x1, blocking collectives, exchange(): return lax.all_to_all(x, axes, 0, 0, tiled=True)  13.7 us
    all_to_all x4, waiting for transfers between devices, exchange(): return lax.all_to_all(x, axes, 0, 0, tiled=True)  9.78 us
    ppermute x1, waiting for transfers between devices, body(): pair_recv = lax.ppermute(pair_away, 'zl', [(i, i ^ 1) for i in range(n_zl)])  9.08 us
    ppermute x3, waiting for transfers between devices, along_z(): lax.ppermute(x, ('zl', 'zh'), [(at[z], at[(z + step) % count]) for z in r...  6.19 us
    pallas_call x1, Pallas kernels, body(): pl.pallas_call(functools.partial(part_kernel, n_zl, n_zh), out_shape=(hal...  4.8 us
  transfers between devices with their start and end apart: 12, of which 8 were waited for; matrix products, arithmetic and copies ran while one was open for 8% of the time, Pallas kernels for 5%

profile of v9, /device:TPU:6, one launch (start us, length us, event | category | flops | bytes accessed | tf_op | source)
XLA Modules:
  0.0 175.4 jit_solution(9215959667233188628)
XLA Ops:
  7.3 0.9 broadcast_in_dim.8
  8.2 13.7 %all_to_all.25 = bf16[4,100,512]{2,1,0:T(8,128)(2,1)S(1)} all-to-all(bf16[4,100,512]{2,1,0:T(8,128)(2,1)S(1)} %broadcast_in_dim.8), channel_id=1, replica_groups=mesh['y'=8,'x'=4,'zl'=4,'co'=2,'zh'=2] {'x'}, dimensions={0} | all-to-all | bytes 819200 | tf_op jit(solution)/shard_map/all_to_all | solution.py:24
  22.7 7.2 %all-to-all-start.1 = ((bf16[32,24,512]{2,1,0:T(8,128)(2,1)}), bf16[32,24,512]{2,1,0:T(8,128)(2,1)}, u32[]{:S(2)}, u32[]{:S(2)}) async-start(bf16[32,24,512]{2,1,0:T(8,128)(2,1)} %bitcast.61), calls=%async_computation.1 | async-start | bytes 1572864 | tf_op jit(solution)/shard_map/all_to_all | solution.py:24
  30.3 32.9 %all-gather = bf16[1600,256]{1,0:T(8,128)(2,1)S(1)} all-gather(bf16[200,256]{1,0:T(8,128)(2,1)S(1)} %bitcast.62), channel_id=2, replica_groups=mesh['y'=8,'x'=4,'zl'=4,'co'=2,'zh'=2] {'zh','zl'}, dimensions={0}, use_global_device_ids=true | all-gather | bytes 921600 | tf_op jit(solution)/shard_map/all_gather | solution.py:162
  63.1 1.9 %collective-permute-start = (bf16[8,200,256]{2,1,0:T(8,128)(2,1)S(1)}, bf16[8,200,256]{2,1,0:T(8,128)(2,1)S(1)}, u32[]{:S(2)}, u32[]{:S(2)}) collective-permute-start(bf16[8,200,256]{2,1,0:T(8,128)(2,1)S(1)} %bitcast.50), channel_id=1, source_target_pairs={{0,2},{2,0},{1,3},{3,1},{4,6},{6,4},{5,7},{7,5},{8,10},{10,8},{9,1... | collective-permute-start | bytes 2457608 | tf_op jit(solution)/shard_map/ppermute | solution.py:40
  66.3 1.0 collective-permute-done.other
  67.3 3.0 %norm.1 = (bf16[16,200,256]{2,1,0:T(8,128)(2,1)S(1)}, f32[8,256]{1,0:T(8,128)S(1)}) custom-call(s32[2]{0:T(128)S(1)} %pad_add_fusion.at, bf16[8,200,256]{2,1,0:T(8,128)(2,1)S(1)} %bitcast.51, bf16[8,200,256]{2,1,0:T(8,128)(2,1)S(1)} %collective-permute-done.other, f32[200,16]{1,0:T(8,128)S(1)} %bitcast.55, f32[200,16]{1,0:T(8,128)S(1)} %bitcast.57), custom_call_target="tpu_custom_call" | custom-call | tf_op jit(solution)/shard_map/norm/pallas_call | solution.py:166
  70.4 2.4 %gather_fusion = bf16[256,512]{1,0:T(8,128)(2,1)S(1)} fusion(bf16[768,512]{1,0:T(8,128)(2,1)} %bitcast.4, s32[1024]{0:T(1024)S(1)} %pad_clamp_fusion), kind=kCustom, calls=%fused_computation | custom fusion | bytes 525312 | tf_op jit(solution)/shard_map/gather | solution.py:185
  72.8 2.7 %convolution_convert_fusion = bf16[3200,512]{1,0:T(8,128)(2,1)} fusion(bf16[3200,256]{1,0:T(8,128)(2,1)S(1)} %bitcast.53, bf16[256,512]{1,0:T(8,128)(2,1)S(1)} %gather_fusion), kind=kOutput, calls=%fused_computation.2 | convolution fusion | flops 840499200 | bytes 5177344 | tf_op jit(solution)/shard_map/dot_general | solution.py:187
  75.5 4.2 %all-gather.3.cloned.1.call-done = bf16[3200,512]{1,0:T(8,128)(2,1)} async-done(((bf16[400,512]{1,0:T(8,128)(2,1)}), bf16[3200,512]{1,0:T(8,128)(2,1)}) %all-gather.3.cloned.1.call-update) | async-done | bytes 3276816 | tf_op jit(solution)/shard_map/all_gather | solution.py:156
  79.7 0.9 copy-done.1
  80.6 4.8 %part.1 = (bf16[8,208,256]{2,1,0:T(8,128)(2,1)S(1)}, bf16[8,208,256]{2,1,0:T(8,128)(2,1)}) custom-call(s32[2]{0:T(128)S(1)} %pad_add_fusion.at, bf16[16,200,512]{2,1,0:T(8,128)(2,1)} %bitcast.58, bf16[256,512]{1,0:T(8,128)(2,1)S(1)} %gather_fusion, bf16[8,200,256]{2,1,0:T(8,128)(2,1)S(1)} %bitcast.52, bf16[8,200,256]{2,1,0:T(8,128)(2,1)S(1)} %collective-permute-done.other, ...), custom_call_target="tpu_custom_call" | custom-call | tf_op jit(solution)/shard_map/part/pallas_call | solution.py:191
  85.4 0.9 copy-done.2
  86.4 1.9 %collective-permute-start.1 = (bf16[8,208,256]{2,1,0:T(8,128)(2,1)}, bf16[8,208,256]{2,1,0:T(8,128)(2,1)}, u32[]{:S(2)}, u32[]{:S(2)}) collective-permute-start(bf16[8,208,256]{2,1,0:T(8,128)(2,1)} %get-tuple-element.30), channel_id=1, source_target_pairs={{0,2},{2,0},{1,3},{3,1},{4,6},{6,4},{5,7},{7,5},{8,10},{10,8},{9,1... | collective-permute-start | bytes 2555912 | tf_op jit(solution)/shard_map/ppermute | solution.py:40
  88.3 1.1 convolution_convert_fusion.1
  89.4 2.6 %scatter_custom_fusion = bf16[768,512]{1,0:T(8,128)(2,1)} fusion(s32[256]{0:T(256)} %bitcast.73, bf16[256,512]{1,0:T(8,128)(2,1)S(1)} %convolution_convert_fusion.1, bf16[]{:T(256)} %constant.34.clone.1), kind=kCustom, calls=%fused_computation.6 | custom fusion | bytes 786944 | tf_op jit(solution)/shard_map/scatter | solution.py:207
  92.0 1.4 pair.1
  93.4 7.6 %all-to-all-start.2 = ((bf16[32,24,512]{2,1,0:T(8,128)(2,1)}), bf16[32,24,512]{2,1,0:T(8,128)(2,1)S(1)}, u32[]{:S(2)}, u32[]{:S(2)}) async-start(bf16[32,24,512]{2,1,0:T(8,128)(2,1)} %bitcast.60), calls=%async_computation.2 | async-start | bytes 1572864 | tf_op jit(solution)/shard_map/all_to_all | solution.py:24
  101.0 4.3 %collective-permute-start.2 = (bf16[4,208,256]{2,1,0:T(8,128)(2,1)S(1)}, bf16[4,208,256]{2,1,0:T(8,128)(2,1)S(1)}, u32[]{:S(2)}, u32[]{:S(2)}) collective-permute-start(bf16[4,208,256]{2,1,0:T(8,128)(2,1)S(1)} %get-tuple-element.32), channel_id=1, source_target_pairs={{0,4},{4,0},{8,12},{12,8},{1,5},{5,1},{9,13},{13,9},{2,6},{6,2},{1... | collective-permute-start | bytes 1277960 | tf_op jit(solution)/shard_map/ppermute | solution.py:218
  106.1 9.1 %collective-permute-done.2.recv = bf16[4,208,256]{2,1,0:T(8,128)(2,1)S(1)} collective-permute-done((bf16[4,208,256]{2,1,0:T(8,128)(2,1)S(1)}, bf16[4,208,256]{2,1,0:T(8,128)(2,1)S(1)}, u32[]{:S(2)}, u32[]{:S(2)}) %collective-permute-start.2) | collective-permute-done | bytes 426016 | tf_op jit(solution)/shard_map/ppermute | solution.py:218
  115.3 6.1 %collective-permute-start.3 = (bf16[208,256]{1,0:T(8,128)(2,1)S(1)}, bf16[208,256]{1,0:T(8,128)(2,1)S(1)}, u32[]{:S(2)}, u32[]{:S(2)}) collective-permute-start(bf16[208,256]{1,0:T(8,128)(2,1)S(1)} %get-tuple-element.34), channel_id=1, source_target_pairs={{0,8},{4,12},{8,1},{12,5},{1,9},{5,13},{9,0},{13,4},{2,10},{6,14},... | collective-permute-start | bytes 319496 | tf_op jit(solution)/shard_map/ppermute | solution.py:36
  121.4 8.5 %collective-permute-start.4 = (bf16[208,256]{1,0:T(8,128)(2,1)S(1)}, bf16[208,256]{1,0:T(8,128)(2,1)S(1)}, u32[]{:S(2)}, u32[]{:S(2)}) collective-permute-start(bf16[208,256]{1,0:T(8,128)(2,1)S(1)} %get-tuple-element.35), channel_id=1, source_target_pairs={{0,1},{4,5},{8,9},{12,13},{1,0},{5,4},{9,8},{13,12},{2,3},{6,7},{1... | collective-permute-start | bytes 319496 | tf_op jit(solution)/shard_map/ppermute | solution.py:36
  129.9 3.7 %collective-permute-start.5 = (bf16[208,256]{1,0:T(8,128)(2,1)S(1)}, bf16[208,256]{1,0:T(8,128)(2,1)S(1)}, u32[]{:S(2)}, u32[]{:S(2)}) collective-permute-start(bf16[208,256]{1,0:T(8,128)(2,1)S(1)} %get-tuple-element.36), channel_id=1, source_target_pairs={{0,9},{4,13},{8,0},{12,4},{1,8},{5,12},{9,1},{13,5},{2,11},{6,15},... | collective-permute-start | bytes 319496 | tf_op jit(solution)/shard_map/ppermute | solution.py:36
  133.6 3.8 %collective-permute-done.4 = bf16[208,256]{1,0:T(8,128)(2,1)S(1)} collective-permute-done((bf16[208,256]{1,0:T(8,128)(2,1)S(1)}, bf16[208,256]{1,0:T(8,128)(2,1)S(1)}, u32[]{:S(2)}, u32[]{:S(2)}) %collective-permute-start.4) | collective-permute-done | bytes 106528 | tf_op jit(solution)/shard_map/ppermute | solution.py:36
  137.4 2.4 %collective-permute-done.5 = bf16[208,256]{1,0:T(8,128)(2,1)S(1)} collective-permute-done((bf16[208,256]{1,0:T(8,128)(2,1)S(1)}, bf16[208,256]{1,0:T(8,128)(2,1)S(1)}, u32[]{:S(2)}, u32[]{:S(2)}) %collective-permute-start.5) | collective-permute-done | bytes 106528 | tf_op jit(solution)/shard_map/ppermute | solution.py:36
  141.3 6.7 %all-to-all-start.3 = ((f32[8,1,400]{2,1,0:T(1,128)}), f32[8,1,400]{2,1,0:T(1,128)S(1)}, u32[]{:S(2)}, u32[]{:S(2)}) async-start(f32[8,1,400]{2,1,0:T(1,128)} %broadcast_in_dim.10), calls=%async_computation.4 | async-start | bytes 32768 | tf_op jit(solution)/shard_map/all_to_all | solution.py:24
  148.0 2.4 %reduce-scatter.2.cloned.1.call-done = bf16[400,512]{1,0:T(8,128)(2,1)} async-done(((bf16[3200,512]{1,0:T(8,128)(2,1)}), bf16[400,512]{1,0:T(8,128)(2,1)}) %reduce-scatter.2.cloned.1.call-update) | async-done | bytes 409616 | tf_op jit(solution)/shard_map/reduce_scatter | solution.py:188
  150.4 1.1 reshape.90
  151.5 4.3 %all-to-all-done.3 = f32[8,1,400]{2,1,0:T(1,128)S(1)} async-done(((f32[8,1,400]{2,1,0:T(1,128)}), f32[8,1,400]{2,1,0:T(1,128)S(1)}, u32[]{:S(2)}, u32[]{:S(2)}) %all-to-all-start.3) | async-done | bytes 12832 | tf_op jit(solution)/shard_map/all_to_all | solution.py:24
  156.6 4.8 %all-to-all-start.4 = ((bf16[4,104,512]{2,1,0:T(8,128)(2,1)}), bf16[4,104,512]{2,1,0:T(8,128)(2,1)S(1)}, u32[]{:S(2)}, u32[]{:S(2)}) async-start(bf16[4,104,512]{2,1,0:T(8,128)(2,1)} %pad_maximum_fusion), calls=%async_computation.5 | async-start | bytes 851968 | tf_op jit(solution)/shard_map/all_to_all | solution.py:24
  161.4 5.5 %all-to-all-done.4 = bf16[4,104,512]{2,1,0:T(8,128)(2,1)S(1)} async-done(((bf16[4,104,512]{2,1,0:T(8,128)(2,1)}), bf16[4,104,512]{2,1,0:T(8,128)(2,1)S(1)}, u32[]{:S(2)}, u32[]{:S(2)}) %all-to-all-start.4) | async-done | bytes 426016 | tf_op jit(solution)/shard_map/all_to_all | solution.py:24
  167.7 0.9 copy.25
  (60 shorter events, 6.4 us)
Async XLA Ops:
  7.2 22.9 %copy-start.9 = (f32[3200]{0:T(1024)S(1)}, f32[3200]{0:T(1024)}, u32[]{:S(2)}) copy-start(f32[3200]{0:T(1024)} %param.8) | copy-start | bytes 38404
  7.2 23.0 %copy-start.8 = (f32[3200]{0:T(1024)S(1)}, f32[3200]{0:T(1024)}, u32[]{:S(2)}) copy-start(f32[3200]{0:T(1024)} %param.7) | copy-start | bytes 38404
  7.2 23.1 %copy-start.5 = (bf16[256,200]{0,1:T(8,128)(2,1)S(1)}, bf16[256,200]{0,1:T(8,128)(2,1)}, u32[]{:S(2)}) copy-start(bf16[256,200]{0,1:T(8,128)(2,1)} %param.6) | copy-start | bytes 307204
  7.2 57.8 %copy-start.10 = (s32[256,1]{0,1:T(1,128)S(1)}, s32[256,1]{0,1:T(1,128)}, u32[]{:S(2)}) copy-start(s32[256,1]{0,1:T(1,128)} %param.10) | copy-start | bytes 3076
  7.2 72.5 %all-gather.3.cloned.1.call-start = ((), (), s32[]{:S(2)}) async-start(), calls=%async_computation.6 | async-start | bytes 3686400 | tf_op jit(solution)/shard_map/all_gather | solution.py:156
  22.7 47.6 %all-to-all-start.1 = ((bf16[32,24,512]{2,1,0:T(8,128)(2,1)}), bf16[32,24,512]{2,1,0:T(8,128)(2,1)}, u32[]{:S(2)}, u32[]{:S(2)}) async-start(bf16[32,24,512]{2,1,0:T(8,128)(2,1)} %bitcast.61), calls=%async_computation.1 | async-start | bytes 1572864 | tf_op jit(solution)/shard_map/all_to_all | solution.py:24
  30.0 120.4 %reduce-scatter.2.cloned.1.call-start = ((), (), s32[]{:S(2)}) async-start(), calls=%async_computation.7 | async-start | bytes 3686400 | tf_op jit(solution)/shard_map/reduce_scatter | solution.py:188
  63.1 4.2 %collective-permute-start = (bf16[8,200,256]{2,1,0:T(8,128)(2,1)S(1)}, bf16[8,200,256]{2,1,0:T(8,128)(2,1)S(1)}, u32[]{:S(2)}, u32[]{:S(2)}) collective-permute-start(bf16[8,200,256]{2,1,0:T(8,128)(2,1)S(1)} %bitcast.50), channel_id=1, source_target_pairs={{0,2},{2,0},{1,3},{3,1},{4,6},{6,4},{5,7},{7,5},{8,10},{10,8},{9,1... | collective-permute-start | bytes 2457608 | tf_op jit(solution)/shard_map/ppermute | solution.py:40
  66.0 4.4 %copy-start = (f32[16,200]{0,1:T(8,128)}, f32[16,200]{0,1:T(8,128)S(1)}, u32[]{:S(2)}) copy-start(f32[16,200]{0,1:T(8,128)S(1)} %copy.18) | copy-start | bytes 38404
  66.3 4.1 %copy-start.11 = (s32[256,1]{0,1:T(1,128)}, s32[256,1]{0,1:T(1,128)S(1)}, u32[]{:S(2)}) copy-start(s32[256,1]{0,1:T(1,128)S(1)} %compare_select_fusion) | copy-start | bytes 3076
  79.7 0.9 copy-start.1
  80.6 7.7 %copy-start.4 = (bf16[3200,512]{1,0:T(8,128)(2,1)S(1)}, bf16[3200,512]{1,0:T(8,128)(2,1)}, u32[]{:S(2)}) copy-start(bf16[3200,512]{1,0:T(8,128)(2,1)} %all-gather.3.cloned.1.call-done) | copy-start | bytes 9830404
  85.4 0.9 copy-start.2
  86.4 5.6 %collective-permute-start.1 = (bf16[8,208,256]{2,1,0:T(8,128)(2,1)}, bf16[8,208,256]{2,1,0:T(8,128)(2,1)}, u32[]{:S(2)}, u32[]{:S(2)}) collective-permute-start(bf16[8,208,256]{2,1,0:T(8,128)(2,1)} %get-tuple-element.30), channel_id=1, source_target_pairs={{0,2},{2,0},{1,3},{3,1},{4,6},{6,4},{5,7},{7,5},{8,10},{10,8},{9,1... | collective-permute-start | bytes 2555912 | tf_op jit(solution)/shard_map/ppermute | solution.py:40
  88.3 3.7 %copy-start.3 = (bf16[8,208,256]{2,1,0:T(8,128)(2,1)S(1)}, bf16[8,208,256]{2,1,0:T(8,128)(2,1)}, u32[]{:S(2)}) copy-start(bf16[8,208,256]{2,1,0:T(8,128)(2,1)} %copy-done.2) | copy-start | bytes 2555908
  89.4 50.5 %copy-start.6 = (bf16[256,200]{0,1:T(8,128)(2,1)S(1)}, bf16[256,200]{0,1:T(8,128)(2,1)}, u32[]{:S(2)}) copy-start(bf16[256,200]{0,1:T(8,128)(2,1)} %param.6) | copy-start | bytes 307204
  93.4 47.3 %all-to-all-start.2 = ((bf16[32,24,512]{2,1,0:T(8,128)(2,1)}), bf16[32,24,512]{2,1,0:T(8,128)(2,1)S(1)}, u32[]{:S(2)}, u32[]{:S(2)}) async-start(bf16[32,24,512]{2,1,0:T(8,128)(2,1)} %bitcast.60), calls=%async_computation.2 | async-start | bytes 1572864 | tf_op jit(solution)/shard_map/all_to_all | solution.py:24
  101.0 14.2 %collective-permute-start.2 = (bf16[4,208,256]{2,1,0:T(8,128)(2,1)S(1)}, bf16[4,208,256]{2,1,0:T(8,128)(2,1)S(1)}, u32[]{:S(2)}, u32[]{:S(2)}) collective-permute-start(bf16[4,208,256]{2,1,0:T(8,128)(2,1)S(1)} %get-tuple-element.32), channel_id=1, source_target_pairs={{0,4},{4,0},{8,12},{12,8},{1,5},{5,1},{9,13},{13,9},{2,6},{6,2},{1... | collective-permute-start | bytes 1277960 | tf_op jit(solution)/shard_map/ppermute | solution.py:218
  115.3 18.3 %collective-permute-start.3 = (bf16[208,256]{1,0:T(8,128)(2,1)S(1)}, bf16[208,256]{1,0:T(8,128)(2,1)S(1)}, u32[]{:S(2)}, u32[]{:S(2)}) collective-permute-start(bf16[208,256]{1,0:T(8,128)(2,1)S(1)} %get-tuple-element.34), channel_id=1, source_target_pairs={{0,8},{4,12},{8,1},{12,5},{1,9},{5,13},{9,0},{13,4},{2,10},{6,14},... | collective-permute-start | bytes 319496 | tf_op jit(solution)/shard_map/ppermute | solution.py:36
  121.4 16.0 %collective-permute-start.4 = (bf16[208,256]{1,0:T(8,128)(2,1)S(1)}, bf16[208,256]{1,0:T(8,128)(2,1)S(1)}, u32[]{:S(2)}, u32[]{:S(2)}) collective-permute-start(bf16[208,256]{1,0:T(8,128)(2,1)S(1)} %get-tuple-element.35), channel_id=1, source_target_pairs={{0,1},{4,5},{8,9},{12,13},{1,0},{5,4},{9,8},{13,12},{2,3},{6,7},{1... | collective-permute-start | bytes 319496 | tf_op jit(solution)/shard_map/ppermute | solution.py:36
  129.9 9.9 %collective-permute-start.5 = (bf16[208,256]{1,0:T(8,128)(2,1)S(1)}, bf16[208,256]{1,0:T(8,128)(2,1)S(1)}, u32[]{:S(2)}, u32[]{:S(2)}) collective-permute-start(bf16[208,256]{1,0:T(8,128)(2,1)S(1)} %get-tuple-element.36), channel_id=1, source_target_pairs={{0,9},{4,13},{8,0},{12,4},{1,8},{5,12},{9,1},{13,5},{2,11},{6,15},... | collective-permute-start | bytes 319496 | tf_op jit(solution)/shard_map/ppermute | solution.py:36
  141.3 14.4 %all-to-all-start.3 = ((f32[8,1,400]{2,1,0:T(1,128)}), f32[8,1,400]{2,1,0:T(1,128)S(1)}, u32[]{:S(2)}, u32[]{:S(2)}) async-start(f32[8,1,400]{2,1,0:T(1,128)} %broadcast_in_dim.10), calls=%async_computation.4 | async-start | bytes 32768 | tf_op jit(solution)/shard_map/all_to_all | solution.py:24
  156.6 10.3 %all-to-all-start.4 = ((bf16[4,104,512]{2,1,0:T(8,128)(2,1)}), bf16[4,104,512]{2,1,0:T(8,128)(2,1)S(1)}, u32[]{:S(2)}, u32[]{:S(2)}) async-start(bf16[4,104,512]{2,1,0:T(8,128)(2,1)} %pad_maximum_fusion), calls=%async_computation.5 | async-start | bytes 851968 | tf_op jit(solution)/shard_map/all_to_all | solution.py:24
  167.0 1.5 copy-start.7
Sparse Core Ops, SparseCore 0:
  22.9 56.8 all-gather.2
  82.6 67.7 reduce-scatter.1
